TPU v7x, 128 devices: a whole 4x4x4 slice. The times are simulated.
128 devices in a mesh: row: 16 (over z_lo, y, core), col: 8 (over x, z_hi).
Axes of the slice: x: 4, y: 4, z: 4 (z_hi: 2, z_lo: 2; z = z_hi * 2 + z_lo), core: 2. Of those that a mesh axis runs over, the one named last changes fastest.
Arguments:
- features: bfloat16 [32768, 128], P(('col', 'row')), may hold values from -6 to 6
- weight: bfloat16 [128, 256], replicated, may hold values from -0.5 to 0.5
- adj_values: bfloat16 [12288, 256, 256], P(('row', 'col')), may hold values from -0.0390625 to 0.0390625
- slot_rows: int32 [12288], P(('row', 'col')), may hold values from 0 to 7, as said below
- slot_cols: int32 [12288], P(('row', 'col')), may hold values from 0 to 15
- slot_live: int32 [128], P(('row', 'col')), may hold values from 13 to 96, as said below
- cotangent: bfloat16 [32768, 256], P(('row', 'col')), may hold values from -6 to 6
Outputs:
- output: bfloat16 [32768, 256], P(('row', 'col'))
- grad_features: bfloat16 [32768, 128], P(('col', 'row'))
- grad_weight: float32 [128, 256], replicated
Inputs may be any that keep to these rules, and one draw needn't show every extreme that they name: Within one device's slots the pairs (slot_rows, slot_cols) are distinct. `slot_live`: some device has all 96 slots live.
All inputs are finite; a program needn't handle non-finite values.
Results may differ from a plain program's by a relative error of at most 0.006.
Values may be sent and summed in bfloat16 or wider, within the bound.
A program may use at most 128 MiB of HBM per device.

v0:
```python
import math

import jax
import jax.numpy as jnp
from jax import lax
from jax.sharding import PartitionSpec as P


def silu_slope(value):
    sig = jax.nn.sigmoid(value)
    return sig * (1.0 + value * (1.0 - sig))


def block_product(adj_values, index_in, index_out, keep, source, count_out, transposed):
    slots, size = (adj_values.shape[0], adj_values.shape[1])
    width = source.shape[2]
    group = math.gcd(slots, 32)
    groups = slots // group

    def step(total, item):
        values, taken, placed, weights = item
        picked = source[taken]
        if transposed:
            product = jnp.einsum("sab,saf->sbf", values, picked, preferred_element_type=jnp.float32)
        else:
            product = jnp.einsum("sab,sbf->saf", values, picked, preferred_element_type=jnp.float32)
        return (total.at[placed].add(product * weights[:, None, None]), None)

    items = (
        adj_values.reshape(groups, group, size, size),
        index_in.reshape(groups, group),
        index_out.reshape(groups, group),
        keep.reshape(groups, group),
    )
    total, _ = lax.scan(step, jnp.zeros((count_out, size, width), jnp.float32), items)
    return total.reshape(count_out * size, width)


def body(features, weight, adj_values, slot_rows, slot_cols, slot_live, cotangent):
    size = adj_values.shape[1]
    slots = adj_values.shape[0]
    width = weight.shape[1]
    own_rows = features.shape[0]
    per_device = own_rows // size
    tile_rows = per_device * lax.axis_size("col")
    tile_cols = per_device * lax.axis_size("row")
    nodes = own_rows * lax.axis_size("row") * lax.axis_size("col")
    keep = (jnp.arange(slots, dtype=jnp.int32) < slot_live[0]).astype(jnp.float32)
    projected = jnp.dot(features, weight, preferred_element_type=jnp.float32).astype(jnp.bfloat16)
    column_rows = lax.all_gather(projected, "row", axis=0, tiled=True)
    column_blocks = column_rows.reshape(tile_cols, size, width)
    partial_value = block_product(
        adj_values, slot_cols, slot_rows, keep, column_blocks, tile_rows, False
    )
    summed = lax.psum_scatter(partial_value, "col", scatter_dimension=0, tiled=True)
    output = jax.nn.silu(summed).astype(jnp.bfloat16)
    grad_summed = (cotangent.astype(jnp.float32) * silu_slope(summed)).astype(jnp.bfloat16)
    grad_range = lax.all_gather(grad_summed, "col", axis=0, tiled=True)
    grad_blocks = grad_range.reshape(tile_rows, size, width)
    back = block_product(adj_values, slot_rows, slot_cols, keep, grad_blocks, tile_cols, True)
    grad_projected = lax.psum_scatter(back, "row", scatter_dimension=0, tiled=True).astype(
        jnp.bfloat16
    )
    grad_features = jnp.dot(grad_projected, weight.T, preferred_element_type=jnp.float32).astype(
        jnp.bfloat16
    )
    local_term = lax.dot_general(
        features, grad_projected, (((0,), (0,)), ((), ())), preferred_element_type=jnp.float32
    )
    grad_weight = lax.psum(local_term, ("row", "col")) / math.sqrt(nodes)
    return (output, grad_features, grad_weight)


def solution(mesh):
    placed = (
        P(("col", "row"), None),
        P(),
        P(("row", "col"), None, None),
        P(("row", "col")),
        P(("row", "col")),
        P(("row", "col")),
        P(("row", "col"), None),
    )
    return jax.shard_map(
        body,
        mesh=mesh,
        in_specs=placed,
        out_specs=(P(("row", "col"), None), P(("col", "row"), None), P()),
        check_vma=False,
    )
```

profile of v0, /device:TPU:1, one launch (start us, length us, event | category | flops | bytes accessed | tf_op | source)
XLA Modules:
  0.0 557.1 jit_solution(4911130216952027264)
XLA Ops:
  8.0 1.7 convolution_convert_fusion
  11.9 35.7 %all-gather.3.cloned.1.call-done = bf16[4096,256]{1,0:T(8,128)(2,1)} async-done(((bf16[256,256]{1,0:T(8,128)(2,1)}), bf16[4096,256]{1,0:T(8,128)(2,1)}) %all-gather.3.cloned.1.call-update) | async-done | bytes 2097168 | tf_op jit(solution)/shard_map/all_gather | solution.py:50
  47.8 72.5 %while.20 = (s32[]{:T(128)}, f32[8,256,256]{2,1,0:T(8,128)S(1)}, s32[3,32]{1,0:T(4,128)S(1)}, bf16[3,32,256,256]{3,2,1,0:T(8,128)(2,1)}, s32[3,32]{1,0:T(4,128)S...) while((s32[]{:T(128)}, f32[8,256,256]{2,1,0:T(8,128)S(1)}, s32[3,32]{1,0:T(4,128)S(1)}, ...), condition=%wide.region_2.3_spmd, body=%wide.region_0.2_spmd.sunk | while | flops 1077937408 | bytes 50337628 | solution.py:35
  47.8 4.4 gather_fusion
  52.2 7.9 %broadcast_multiply_fusion.5 = f32[32,256,256]{2,1,0:T(8,128)} fusion(f32[32]{0:T(128)S(1)} %fusion.42, bf16[32,256,256]{2,1,0:T(8,128)(2,1)} %gather_fusion, bf16[3,32,256,256]{3,2,1,0:T(8,128)(2,1)} %get-tuple-element.236, s32[]{:T(128)} %get-tuple-element.225), kind=kOutput, calls=%fused_computation.6.clone.1 | convolution fusion | flops 1075838976 | bytes 16777856 | tf_op jit(solution)/shard_map/while/body/eval_jaxpr/sab,sbf->saf/dot_general | solution.py:26
  60.2 11.8 %scatter_fusion = f32[8,256,256]{2,1,0:T(8,128)S(1)} fusion(f32[8,256,256]{2,1,0:T(8,128)S(1)} %get-tuple-element.226, s32[32]{0:T(128)S(1)} %get-tuple-element.206, f32[32,256,256]{2,1,0:T(8,128)} %broadcast_multiply_fusion.5), kind=kCustom, calls=%fused_computation.2.clone.1 | custom fusion | flops 2097152 | bytes 25165952 | tf_op jit(solution)/shard_map/while/body/eval_jaxpr/scatter-add | solution.py:27
  72.0 4.4 gather_fusion
  76.4 7.9 %broadcast_multiply_fusion.5 = f32[32,256,256]{2,1,0:T(8,128)} fusion(f32[32]{0:T(128)S(1)} %fusion.42, bf16[32,256,256]{2,1,0:T(8,128)(2,1)} %gather_fusion, bf16[3,32,256,256]{3,2,1,0:T(8,128)(2,1)} %get-tuple-element.236, s32[]{:T(128)} %get-tuple-element.225), kind=kOutput, calls=%fused_computation.6.clone.1 | convolution fusion | flops 1075838976 | bytes 16777856 | tf_op jit(solution)/shard_map/while/body/eval_jaxpr/sab,sbf->saf/dot_general | solution.py:26
  84.3 11.8 %scatter_fusion = f32[8,256,256]{2,1,0:T(8,128)S(1)} fusion(f32[8,256,256]{2,1,0:T(8,128)S(1)} %get-tuple-element.226, s32[32]{0:T(128)S(1)} %get-tuple-element.206, f32[32,256,256]{2,1,0:T(8,128)} %broadcast_multiply_fusion.5), kind=kCustom, calls=%fused_computation.2.clone.1 | custom fusion | flops 2097152 | bytes 25165952 | tf_op jit(solution)/shard_map/while/body/eval_jaxpr/scatter-add | solution.py:27
  96.2 4.4 gather_fusion
  100.5 7.9 %broadcast_multiply_fusion.5 = f32[32,256,256]{2,1,0:T(8,128)} fusion(f32[32]{0:T(128)S(1)} %fusion.42, bf16[32,256,256]{2,1,0:T(8,128)(2,1)} %gather_fusion, bf16[3,32,256,256]{3,2,1,0:T(8,128)(2,1)} %get-tuple-element.236, s32[]{:T(128)} %get-tuple-element.225), kind=kOutput, calls=%fused_computation.6.clone.1 | convolution fusion | flops 1075838976 | bytes 16777856 | tf_op jit(solution)/shard_map/while/body/eval_jaxpr/sab,sbf->saf/dot_general | solution.py:26
  108.5 11.7 %scatter_fusion = f32[8,256,256]{2,1,0:T(8,128)S(1)} fusion(f32[8,256,256]{2,1,0:T(8,128)S(1)} %get-tuple-element.226, s32[32]{0:T(128)S(1)} %get-tuple-element.206, f32[32,256,256]{2,1,0:T(8,128)} %broadcast_multiply_fusion.5), kind=kCustom, calls=%fused_computation.2.clone.1 | custom fusion | flops 2097152 | bytes 25165952 | tf_op jit(solution)/shard_map/while/body/eval_jaxpr/scatter-add | solution.py:27
  120.2 1.3 copy-done.1
  121.6 75.0 %reduce-scatter.3.cloned.1.call-done = f32[256,256]{1,0:T(8,128)} async-done(((f32[2048,256]{1,0:T(8,128)}), f32[256,256]{1,0:T(8,128)}) %reduce-scatter.3.cloned.1.call-update) | async-done | bytes 262160 | tf_op jit(solution)/shard_map/reduce_scatter | solution.py:55
  196.7 1.8 multiply_convert_fusion
  198.5 16.6 %copy.10 = bf16[96,256,256]{1,2,0:T(8,128)(2,1)} copy(bf16[96,256,256]{2,1,0:T(8,128)(2,1)} %bitcast.87) | data formatting | bytes 25165824 | tf_op args[2]
  215.2 30.1 %all-gather.5.cloned.1.call-done = bf16[2048,256]{1,0:T(8,128)(2,1)} async-done(((bf16[256,256]{1,0:T(8,128)(2,1)}), bf16[2048,256]{1,0:T(8,128)(2,1)}) %all-gather.5.cloned.1.call-update) | async-done | bytes 1048592 | tf_op jit(solution)/shard_map/all_gather | solution.py:58
  245.3 2.4 broadcast_in_dim.8
  247.7 87.7 %while.21 = (s32[]{:T(128)}, f32[16,256,256]{2,1,0:T(8,128)}, s32[3,32]{1,0:T(4,128)S(1)}, bf16[3,32,256,256]{2,3,1,0:T(8,128)(2,1)}, s32[3,32]{1,0:T(4,128)S(1)...) while((s32[]{:T(128)}, f32[16,256,256]{2,1,0:T(8,128)}, s32[3,32]{1,0:T(4,128)S(1)}, ...), condition=%wide.region_6.7_spmd, body=%wide.region_4.6_spmd.sunk | while | flops 1077937408 | bytes 50337628 | solution.py:35
  247.7 2.8 gather_fusion.1
  250.5 7.9 %broadcast_multiply_fusion.6 = f32[32,256,256]{2,1,0:T(8,128)} fusion(f32[32]{0:T(128)S(1)} %fusion.46, bf16[32,256,256]{2,1,0:T(8,128)(2,1)} %gather_fusion.1, bf16[3,32,256,256]{2,3,1,0:T(8,128)(2,1)} %get-tuple-element.260, s32[]{:T(128)} %get-tuple-element.249), kind=kOutput, calls=%fused_computation.22.clone.1 | convolution fusion | flops 1075838976 | bytes 16777856 | tf_op jit(solution)/shard_map/while/body/eval_jaxpr/sab,saf->sbf/dot_general | solution.py:24
  258.4 18.5 %scatter_fusion.1 = f32[16,256,256]{2,1,0:T(8,128)} fusion(f32[16,256,256]{2,1,0:T(8,128)} %get-tuple-element.250, s32[32]{0:T(128)S(1)} %get-tuple-element.215, f32[32,256,256]{2,1,0:T(8,128)} %broadcast_multiply_fusion.6), kind=kCustom, calls=%fused_computation.3.clone.1 | custom fusion | flops 2097152 | bytes 25165952 | tf_op jit(solution)/shard_map/while/body/eval_jaxpr/scatter-add | solution.py:27
  277.0 2.8 gather_fusion.1
  279.8 7.9 %broadcast_multiply_fusion.6 = f32[32,256,256]{2,1,0:T(8,128)} fusion(f32[32]{0:T(128)S(1)} %fusion.46, bf16[32,256,256]{2,1,0:T(8,128)(2,1)} %gather_fusion.1, bf16[3,32,256,256]{2,3,1,0:T(8,128)(2,1)} %get-tuple-element.260, s32[]{:T(128)} %get-tuple-element.249), kind=kOutput, calls=%fused_computation.22.clone.1 | convolution fusion | flops 1075838976 | bytes 16777856 | tf_op jit(solution)/shard_map/while/body/eval_jaxpr/sab,saf->sbf/dot_general | solution.py:24
  287.7 18.5 %scatter_fusion.1 = f32[16,256,256]{2,1,0:T(8,128)} fusion(f32[16,256,256]{2,1,0:T(8,128)} %get-tuple-element.250, s32[32]{0:T(128)S(1)} %get-tuple-element.215, f32[32,256,256]{2,1,0:T(8,128)} %broadcast_multiply_fusion.6), kind=kCustom, calls=%fused_computation.3.clone.1 | custom fusion | flops 2097152 | bytes 25165952 | tf_op jit(solution)/shard_map/while/body/eval_jaxpr/scatter-add | solution.py:27
  306.2 2.8 gather_fusion.1
  309.0 7.9 %broadcast_multiply_fusion.6 = f32[32,256,256]{2,1,0:T(8,128)} fusion(f32[32]{0:T(128)S(1)} %fusion.46, bf16[32,256,256]{2,1,0:T(8,128)(2,1)} %gather_fusion.1, bf16[3,32,256,256]{2,3,1,0:T(8,128)(2,1)} %get-tuple-element.260, s32[]{:T(128)} %get-tuple-element.249), kind=kOutput, calls=%fused_computation.22.clone.1 | convolution fusion | flops 1075838976 | bytes 16777856 | tf_op jit(solution)/shard_map/while/body/eval_jaxpr/sab,saf->sbf/dot_general | solution.py:24
  316.9 18.5 %scatter_fusion.1 = f32[16,256,256]{2,1,0:T(8,128)} fusion(f32[16,256,256]{2,1,0:T(8,128)} %get-tuple-element.250, s32[32]{0:T(128)S(1)} %get-tuple-element.215, f32[32,256,256]{2,1,0:T(8,128)} %broadcast_multiply_fusion.6), kind=kCustom, calls=%fused_computation.3.clone.1 | custom fusion | flops 2097152 | bytes 25165952 | tf_op jit(solution)/shard_map/while/body/eval_jaxpr/scatter-add | solution.py:27
  335.5 63.8 %reduce-scatter.5.cloned.1.call-done = f32[256,256]{1,0:T(8,128)} async-done(((f32[4096,256]{1,0:T(8,128)}), f32[256,256]{1,0:T(8,128)}) %reduce-scatter.5.cloned.1.call-update) | async-done | bytes 262160 | tf_op jit(solution)/shard_map/reduce_scatter | solution.py:61
  399.3 1.8 convolution_bitcast_fusion
  401.2 1.8 convolution_convert_fusion.1
  403.0 146.0 %all-reduce.2.cloned.1.call-done = f32[128,256]{0,1:T(8,128)} async-done(((f32[128,256]{0,1:T(8,128)}), f32[128,256]{0,1:T(8,128)}) %all-reduce.2.cloned.1.call-update) | async-done | bytes 131088 | tf_op jit(solution)/shard_map/psum | solution.py:70
  (43 shorter events, 4.5 us)
Async XLA Ops:
  7.2 0.8 copy-start
  7.2 40.4 %all-gather.3.cloned.1.call-start = ((), (), s32[]{:S(2)}) async-start(), calls=%async_computation.2 | async-start | bytes 2228224 | tf_op jit(solution)/shard_map/all_gather | solution.py:50
  9.7 187.0 %reduce-scatter.3.cloned.1.call-start = ((), (), s32[]{:S(2)}) async-start(), calls=%async_computation.3 | async-start | bytes 2359296 | tf_op jit(solution)/shard_map/reduce_scatter | solution.py:55
  47.8 148.9 %copy-start.4 = (bf16[256,256]{1,0:T(8,128)(2,1)S(1)}, bf16[256,256]{1,0:T(8,128)(2,1)}, u32[]{:S(2)}) copy-start(bf16[256,256]{1,0:T(8,128)(2,1)} %param.17) | copy-start | bytes 393220
  120.2 1.3 copy-start.1
  121.6 123.7 %all-gather.5.cloned.1.call-start = ((), (), s32[]{:S(2)}) async-start(), calls=%async_computation.4 | async-start | bytes 1179648 | tf_op jit(solution)/shard_map/all_gather | solution.py:58
  198.5 200.8 %reduce-scatter.5.cloned.1.call-start = ((), (), s32[]{:S(2)}) async-start(), calls=%async_computation.5 | async-start | bytes 4456448 | tf_op jit(solution)/shard_map/reduce_scatter | solution.py:61
  245.3 2.4 copy-start.2
  335.4 65.7 %copy-start.3 = (bf16[128,256]{1,0:T(8,128)(2,1)S(1)}, bf16[128,256]{1,0:T(8,128)(2,1)}, u32[]{:S(2)}) copy-start(bf16[128,256]{1,0:T(8,128)(2,1)} %param.12) | copy-start | bytes 196612
  335.5 213.5 %all-reduce.2.cloned.1.call-start = ((), (), s32[]{:S(2)}) async-start(), calls=%async_computation.6 | async-start | bytes 262144 | tf_op jit(solution)/shard_map/psum | solution.py:70
Sparse Core Ops, SparseCore 0:
  10.3 37.2 all-gather.2
  121.7 74.9 reduce-scatter.2
  199.6 45.6 all-gather.4
  335.6 63.6 reduce-scatter.4
  404.5 144.3 all-reduce.1
where the time goes:
time: 558 us; the launch traced here: 557 us
  waiting for transfers between devices  351 us (63%)
  other arithmetic  93.6 us (17%)
  matrix products  52.9 us (9%)
  local copies, waits for them, and re-layouts  45.1 us (8%)
  between operations  14.5 us (3%)
    psum x1, waiting for transfers between devices, body(): grad_weight = lax.psum(local_term, ('row', 'col')) / math.sqrt(nodes)  146 us
    scatter-add x6, other arithmetic, step(): return (total.at[placed].add(product * weights[:, None, None]), None)  90.8 us
    reduce_scatter x1, waiting for transfers between devices, body(): lax.psum_scatter(partial_value, 'col', scatter_dimension=0, tiled=True)  75 us
    reduce_scatter x1, waiting for transfers between devices, body(): lax.psum_scatter(back, 'row', scatter_dimension=0, tiled=True)  63.8 us
    all_gather x1, waiting for transfers between devices, body(): column_rows = lax.all_gather(projected, 'row', axis=0, tiled=True)  35.7 us
    all_gather x1, waiting for transfers between devices, body(): grad_range = lax.all_gather(grad_summed, 'col', axis=0, tiled=True)  30.1 us
    dot_general x3, matrix products, step(): jnp.einsum('sab,sbf->saf', values, picked, preferred_element_type=jnp.flo...  23.8 us
    dot_general x3, matrix products, step(): jnp.einsum('sab,saf->sbf', values, picked, preferred_element_type=jnp.flo...  23.8 us
  transfers between devices with their start and end apart: 5, of which 5 were waited for; matrix products, arithmetic and copies ran while one was open for 4% of the time, Pallas kernels for 0%

commit v1 on v0

v1 whole, which is shorter than its diff:
```python
import functools
import math

import jax
import jax.numpy as jnp
from jax import lax
from jax.experimental import pallas as pl
from jax.experimental.pallas import tpu as pltpu
from jax.sharding import PartitionSpec as P

GROUP = 8


def silu_slope(value):
    sig = jax.nn.sigmoid(value)
    return sig * (1.0 + value * (1.0 - sig))


def _block_kernel(transposed, n_in, n_out, rows_ref, cols_ref, live_ref, a_ref, src_ref, out_ref):
    g = pl.program_id(0)
    live = live_ref[0]

    @pl.when(g == 0)
    def _():
        out_ref[...] = jnp.zeros_like(out_ref)

    for k in range(GROUP):
        s = g * GROUP + k

        @pl.when(s < live)
        def _():
            if transposed:
                taken = jnp.clip(rows_ref[s], 0, n_in - 1)
                placed = jnp.clip(cols_ref[s], 0, n_out - 1)
                product = lax.dot_general(
                    a_ref[k], src_ref[taken], (((0,), (0,)), ((), ())),
                    preferred_element_type=jnp.float32,
                )
            else:
                taken = jnp.clip(cols_ref[s], 0, n_in - 1)
                placed = jnp.clip(rows_ref[s], 0, n_out - 1)
                product = jnp.dot(a_ref[k], src_ref[taken], preferred_element_type=jnp.float32)
            out_ref[placed] += product


def block_product(adj_values, slot_rows, slot_cols, slot_live, source, count_out, transposed):
    slots, size, _ = adj_values.shape
    n_in, _, width = source.shape
    steps = slots // GROUP

    def a_map(g, rows, cols, live):
        last = jnp.maximum((live[0] - 1) // GROUP, 0)
        return (jnp.minimum(g, last), 0, 0)

    kernel = functools.partial(_block_kernel, transposed, n_in, count_out)
    return pl.pallas_call(
        kernel,
        grid_spec=pltpu.PrefetchScalarGridSpec(
            num_scalar_prefetch=3,
            grid=(steps,),
            in_specs=[
                pl.BlockSpec((GROUP, size, size), a_map),
                pl.BlockSpec((n_in, size, width), lambda g, r, c, l: (0, 0, 0)),
            ],
            out_specs=pl.BlockSpec((count_out, size, width), lambda g, r, c, l: (0, 0, 0)),
        ),
        out_shape=jax.ShapeDtypeStruct((count_out, size, width), jnp.float32),
        compiler_params=pltpu.CompilerParams(dimension_semantics=("arbitrary",)),
        cost_estimate=pl.CostEstimate(
            flops=2 * slots * size * size * width,
            bytes_accessed=slots * size * size * 2 + n_in * size * width * 2 + count_out * size * width * 4,
            transcendentals=0,
        ),
    )(slot_rows, slot_cols, slot_live, adj_values, source)


def split_dot(left, right, dims):
    high = left.astype(jnp.bfloat16)
    low = (left - high.astype(jnp.float32)).astype(jnp.bfloat16)
    first = lax.dot_general(high, right, dims, preferred_element_type=jnp.float32)
    second = lax.dot_general(low, right, dims, preferred_element_type=jnp.float32)
    return first + second


def body(features, weight, adj_values, slot_rows, slot_cols, slot_live, cotangent):
    size = adj_values.shape[1]
    width = weight.shape[1]
    fin = weight.shape[0]
    own_rows = features.shape[0]
    per_device = own_rows // size
    n_row = lax.axis_size("row")
    n_col = lax.axis_size("col")
    tile_rows = per_device * n_col
    tile_cols = per_device * n_row
    nodes = own_rows * n_row * n_col

    feature_cols = lax.all_gather(features, "row", axis=0, tiled=True)
    projected = jnp.dot(feature_cols, weight, preferred_element_type=jnp.float32).astype(jnp.bfloat16)
    column_blocks = projected.reshape(tile_cols, size, width)
    partial_value = block_product(
        adj_values, slot_rows, slot_cols, slot_live, column_blocks, tile_rows, False
    )
    received = lax.all_to_all(partial_value, "col", 0, 0, tiled=True)
    summed = received.sum(axis=0)
    output = jax.nn.silu(summed).astype(jnp.bfloat16)
    grad_summed = (cotangent.astype(jnp.float32) * silu_slope(summed)).astype(jnp.bfloat16)
    grad_range = lax.all_gather(grad_summed, "col", axis=0, tiled=True)
    grad_blocks = grad_range.reshape(tile_rows, size, width)
    back = block_product(
        adj_values, slot_rows, slot_cols, slot_live, grad_blocks, tile_cols, True
    ).reshape(tile_cols * size, width)
    feature_part = split_dot(back, weight, (((1,), (1,)), ((), ())))
    weight_part = split_dot(back, feature_cols, (((0,), (0,)), ((), ()))).T
    pieces = weight_part.reshape(tile_cols, fin * width // (tile_cols * fin), fin)
    payload = jnp.concatenate([feature_part.reshape(tile_cols, size, fin), pieces], axis=1)
    gathered = lax.all_to_all(payload, "row", 0, 0, tiled=True).sum(axis=0)
    grad_features = gathered[:size].astype(jnp.bfloat16)
    weight_piece = lax.psum(gathered[size:], "col")
    grad_weight = lax.all_gather(weight_piece, "row", axis=0, tiled=True).reshape(fin, width)
    grad_weight = grad_weight / math.sqrt(nodes)
    return (output, grad_features, grad_weight)


def solution(mesh):
    placed = (
        P(("col", "row"), None),
        P(),
        P(("row", "col"), None, None),
        P(("row", "col")),
        P(("row", "col")),
        P(("row", "col")),
        P(("row", "col"), None),
    )
    return jax.shard_map(
        body,
        mesh=mesh,
        in_specs=placed,
        out_specs=(P(("row", "col"), None), P(("col", "row"), None), P()),
        check_vma=False,
    )
```

time: 558 us -> 266 us (0.48)
  waiting for transfers between devices: 351 us -> 82.4 us
  blocking collectives: 0 us -> 117 us
  other arithmetic: 93.6 us -> 3.89 us
  matrix products: 52.9 us -> 9.1 us
  local copies, waits for them, and re-layouts: 45.1 us -> 2.21 us
  Pallas kernels: 0 us -> 35.4 us
    psum x1 -> x0, waiting for transfers between devices: 146 us -> none  [body(): grad_weight = lax.psum(local_term, ('row', 'col')) / math.sqrt(nodes)]
    reduce_scatter x2 -> x0, waiting for transfers between devices: 139 us -> none  [the longest x1 75 us: body(): lax.psum_scatter(partial_value, 'col', scatter_dimension=0, tiled=True)]
    scatter-add x6 -> x0, other arithmetic: 90.8 us -> none  [step(): return (total.at[placed].add(product * weights[:, None, None]), None)]
    all_to_all x0 -> x2, blocking collectives: none -> 76.1 us  [the longest x1 39.3 us: body(): gathered = lax.all_to_all(payload, 'row', 0, 0, tiled=True).sum(axis=0)]
    dot_general x9 -> x5, matrix products: 52.9 us -> 9.1 us  [the longest x1 3.25 us: body(): jnp.dot(feature_cols, weight, preferred_element_type=jnp.float32)]
    pallas_call x0 -> x2, Pallas kernels: none -> 35.4 us  [block_product(): pl.pallas_call(kernel, grid_spec=pltpu.PrefetchScalarGridSpec(num_scalar_...]
    gather x6 -> x0, local copies, waits for them, and re-layouts: 21.5 us -> none  [step(): picked = source[taken]]
    all_gather x0 -> x1, blocking collectives: none -> 21 us  [body(): lax.all_gather(weight_piece, 'row', axis=0, tiled=True).reshape(fin, width)]
  transfers between devices with their start and end apart: 5 -> 2, of which waited for: 5 -> 2; matrix products, arithmetic and copies ran while one was open for 4% -> 0% of each run, Pallas kernels for 0% -> 0%
where the time goes in v1:
time: 266 us; the launch traced here: 265 us
  blocking collectives  117 us (44%)
  waiting for transfers between devices  82.4 us (31%)
  Pallas kernels  35.4 us (13%)
  between operations  14.8 us (6%)
  matrix products  9.1 us (3%)
  other arithmetic  3.89 us (1%)
    all_gather x1, waiting for transfers between devices, body(): grad_range = lax.all_gather(grad_summed, 'col', axis=0, tiled=True)  44.7 us
    all_to_all x1, blocking collectives, body(): gathered = lax.all_to_all(payload, 'row', 0, 0, tiled=True).sum(axis=0)  39.3 us
    all_gather x1, waiting for transfers between devices, body(): feature_cols = lax.all_gather(features, 'row', axis=0, tiled=True)  37 us
    all_to_all x1, blocking collectives, body(): received = lax.all_to_all(partial_value, 'col', 0, 0, tiled=True)  36.8 us
    pallas_call x2, Pallas kernels, block_product(): pl.pallas_call(kernel, grid_spec=pltpu.PrefetchScalarGridSpec(num_scalar_...  35.4 us
    all_gather x1, blocking collectives, body(): lax.all_gather(weight_piece, 'row', axis=0, tiled=True).reshape(fin, width)  21 us
    psum x1, blocking collectives, body(): weight_piece = lax.psum(gathered[size:], 'col')  20.2 us
  transfers between devices with their start and end apart: 2, of which 2 were waited for; matrix products, arithmetic and copies ran while one was open for 0% of the time, Pallas kernels for 0%

profile of v1, /device:TPU:1, one launch (start us, length us, event | category | flops | bytes accessed | tf_op | source)
XLA Modules:
  0.0 265.2 jit_solution(10108578425064976066)
XLA Ops:
  7.2 0.0 copy-start
  7.2 0.0 all-gather.3.cloned.1.call-start
  7.2 0.7 all-gather.3.cloned.1.call-update
  7.9 0.0 all-gather.5.cloned.1.call-start
  8.6 37.0 %all-gather.3.cloned.1.call-done = bf16[4096,128]{1,0:T(8,128)(2,1)} async-done(((bf16[256,128]{1,0:T(8,128)(2,1)}), bf16[4096,128]{1,0:T(8,128)(2,1)}) %all-gather.3.cloned.1.call-update) | async-done | bytes 1048592 | tf_op jit(solution)/shard_map/all_gather | solution.py:97
  45.6 0.0 copy-done
  45.6 3.2 %convolution_convert_fusion = bf16[4096,256]{1,0:T(8,128)(2,1)} fusion(bf16[4096,128]{1,0:T(8,128)(2,1)} %all-gather.3.cloned.1.call-done, bf16[128,256]{1,0:T(8,128)(2,1)S(1)} %copy-done), kind=kOutput, calls=%fused_computation | convolution fusion | flops 269484032 | bytes 3211264 | tf_op jit(solution)/shard_map/dot_general | solution.py:98
  48.9 16.6 %shard_map.94 = f32[8,256,256]{2,1,0:T(8,128)} custom-call(s32[96]{0:T(128)} %rows_ref.3, s32[96]{0:T(128)} %cols_ref.3, s32[1]{0:T(128)S(6)} %copy.11.live_ref, bf16[96,256,256]{2,1,0:T(8,128)(2,1)} %a_ref.3, bf16[16,256,256]{2,1,0:T(8,128)(2,1)} %bitcast.22), custom_call_target="tpu_custom_call" | custom-call | flops 3221225472 | bytes 16777216 | tf_op jit(solution)/shard_map/pallas_call | solution.py:56
  65.4 36.8 %all_to_all.10 = f32[8,256,256]{2,1,0:T(8,128)S(1)} all-to-all(f32[8,256,256]{2,1,0:T(8,128)} %shard_map.94), channel_id=1, replica_groups=mesh['row'=16,'col'=8] {'col'}, dimensions={0} | all-to-all | bytes 4194304 | tf_op jit(solution)/shard_map/all_to_all | solution.py:103
  102.2 0.0 copy-start.2
  102.3 0.1 reduce_sum.18
  102.4 0.8 copy-done.2
  103.2 0.8 multiply_convert_fusion
  104.0 0.0 all-gather.5.cloned.1.call-update
  104.0 44.7 %all-gather.5.cloned.1.call-done = bf16[2048,256]{1,0:T(8,128)(2,1)} async-done(((bf16[256,256]{1,0:T(8,128)(2,1)}), bf16[2048,256]{1,0:T(8,128)(2,1)}) %all-gather.5.cloned.1.call-update) | async-done | bytes 1048592 | tf_op jit(solution)/shard_map/all_gather | solution.py:107
  148.7 18.8 %shard_map.95 = f32[16,256,256]{2,1,0:T(8,128)} custom-call(s32[96]{0:T(128)} %rows_ref.3, s32[96]{0:T(128)} %cols_ref.3, s32[1]{0:T(128)S(6)} %copy.11.live_ref, bf16[96,256,256]{2,1,0:T(8,128)(2,1)} %a_ref.3, bf16[8,256,256]{2,1,0:T(8,128)(2,1)} %bitcast.23), custom_call_target="tpu_custom_call" | custom-call | flops 3221225472 | bytes 17825792 | tf_op jit(solution)/shard_map/pallas_call | solution.py:56
  167.5 2.7 %fusion = (bf16[4096,256]{1,0:T(8,128)(2,1)S(1)}, bf16[4096,256]{1,0:T(8,128)(2,1)S(1)}) fusion(f32[16,256,256]{2,1,0:T(8,128)} %shard_map.95), kind=kLoop, calls=%fused_computation.4 | loop fusion | flops 4194304 | bytes 8388608 | tf_op jit(solution)/shard_map/convert_element_type | solution.py:79
  170.2 0.0 copy-start.1
  170.2 2.0 fusion.2
  172.3 0.0 copy-done.1
  172.3 0.8 fusion.3
  173.0 0.8 fusion.1
  173.8 0.1 copy.10
  173.9 2.3 convolution_add_fusion
  176.2 0.2 pad_maximum_fusion
  176.4 39.3 %all_to_all.11 = f32[16,272,128]{2,1,0:T(8,128)S(1)} all-to-all(f32[16,272,128]{2,1,0:T(8,128)S(1)} %pad_maximum_fusion), channel_id=1, replica_groups=mesh['row'=16,'col'=8] {'row'}, dimensions={0} | all-to-all | bytes 4456448 | tf_op jit(solution)/shard_map/all_to_all | solution.py:116
  215.7 0.1 reduce_sum.19
  215.8 0.6 slice.12
  216.4 20.2 %psum.7 = f32[16,128]{1,0:T(8,128)S(1)} all-reduce(f32[16,128]{1,0:T(8,128)S(1)} %slice.10), channel_id=1, replica_groups=mesh['row'=16,'col'=8] {'col'}, use_global_device_ids=true, to_apply=%region_2.3 | all-reduce | flops 2048 | bytes 16384 | tf_op jit(solution)/shard_map/psum | solution.py:118
  236.7 21.0 %all_gather.11 = f32[256,128]{1,0:T(8,128)S(1)} all-gather(f32[16,128]{1,0:T(8,128)S(1)} %psum.7), channel_id=1, replica_groups=mesh['row'=16,'col'=8] {'row'}, dimensions={0}, use_global_device_ids=true | all-gather | bytes 139264 | tf_op jit(solution)/shard_map/all_gather | solution.py:119
  257.7 0.7 div.16
  (3 shorter events, 0.0 us)
Async XLA Ops:
  7.2 38.5 %copy-start = (bf16[128,256]{1,0:T(8,128)(2,1)S(1)}, bf16[128,256]{1,0:T(8,128)(2,1)}, u32[]{:S(2)}) copy-start(bf16[128,256]{1,0:T(8,128)(2,1)} %param.8) | copy-start | bytes 196612
  7.2 38.4 %all-gather.3.cloned.1.call-start = ((), (), s32[]{:S(2)}) async-start(), calls=%async_computation.2 | async-start | bytes 1114112 | tf_op jit(solution)/shard_map/all_gather | solution.py:97
  7.9 140.8 %all-gather.5.cloned.1.call-start = ((), (), s32[]{:S(2)}) async-start(), calls=%async_computation.3 | async-start | bytes 1179648 | tf_op jit(solution)/shard_map/all_gather | solution.py:107
  102.2 0.9 copy-start.2
  170.2 2.1 copy-start.1
Sparse Core Ops, SparseCore 0:
  9.7 35.8 all-gather.2
  104.1 44.5 all-gather.4

commit v2 on v1

--- a/solution.py
+++ b/solution.py
@@ -24,11 +24,10 @@
     def _():
         out_ref[...] = jnp.zeros_like(out_ref)
 
-    for k in range(GROUP):
-        s = g * GROUP + k
-
-        @pl.when(s < live)
-        def _():
+    @pl.when(g * GROUP < live)
+    def _():
+        for k in range(GROUP):
+            s = g * GROUP + k
             if transposed:
                 taken = jnp.clip(rows_ref[s], 0, n_in - 1)
                 placed = jnp.clip(cols_ref[s], 0, n_out - 1)
@@ -40,7 +39,8 @@
                 taken = jnp.clip(cols_ref[s], 0, n_in - 1)
                 placed = jnp.clip(rows_ref[s], 0, n_out - 1)
                 product = jnp.dot(a_ref[k], src_ref[taken], preferred_element_type=jnp.float32)
-            out_ref[placed] += product
+            keep = jnp.where(s < live, 1.0, 0.0).astype(jnp.float32)
+            out_ref[placed] += product * keep
 
 
 def block_product(adj_values, slot_rows, slot_cols, slot_live, source, count_out, transposed):
@@ -74,6 +74,11 @@
     )(slot_rows, slot_cols, slot_live, adj_values, source)
 
 
+def gather_axis(block, axis, count):
+    spread = jnp.broadcast_to(block[None], (count,) + block.shape)
+    return lax.all_to_all(spread, axis, 0, 0, tiled=True)
+
+
 def split_dot(left, right, dims):
     high = left.astype(jnp.bfloat16)
     low = (left - high.astype(jnp.float32)).astype(jnp.bfloat16)
@@ -94,7 +99,7 @@
     tile_cols = per_device * n_row
     nodes = own_rows * n_row * n_col
 
-    feature_cols = lax.all_gather(features, "row", axis=0, tiled=True)
+    feature_cols = gather_axis(features, "row", n_row).reshape(own_rows * n_row, fin)
     projected = jnp.dot(feature_cols, weight, preferred_element_type=jnp.float32).astype(jnp.bfloat16)
     column_blocks = projected.reshape(tile_cols, size, width)
     partial_value = block_product(
@@ -104,7 +109,7 @@
     summed = received.sum(axis=0)
     output = jax.nn.silu(summed).astype(jnp.bfloat16)
     grad_summed = (cotangent.astype(jnp.float32) * silu_slope(summed)).astype(jnp.bfloat16)
-    grad_range = lax.all_gather(grad_summed, "col", axis=0, tiled=True)
+    grad_range = gather_axis(grad_summed, "col", n_col)
     grad_blocks = grad_range.reshape(tile_rows, size, width)
     back = block_product(
         adj_values, slot_rows, slot_cols, slot_live, grad_blocks, tile_cols, True

time: 266 us -> 189 us (0.71)
  waiting for transfers between devices: 82.4 us -> 15.1 us
  Pallas kernels: 35.4 us -> 21.7 us
  between operations: 14.8 us -> 1.37 us
  blocking collectives: 117 us -> 127 us
  starting transfers between devices: 0.08 us -> 7.33 us
  matrix products: 9.1 us -> 5.01 us
    all_gather x2 -> x0, waiting for transfers between devices: 81.7 us -> none  [the longest x1 44.7 us: body(): grad_range = lax.all_gather(grad_summed, 'col', axis=0, tiled=True)]
    all_to_all x0 -> x1, blocking collectives: none -> 17.1 us  [gather_axis(): return lax.all_to_all(spread, axis, 0, 0, tiled=True)]
    all_to_all x0 -> x1, waiting for transfers between devices: none -> 15.1 us  [gather_axis(): return lax.all_to_all(spread, axis, 0, 0, tiled=True)]
    pallas_call x2, Pallas kernels: 35.4 us -> 21.7 us  [block_product(): pl.pallas_call(kernel, grid_spec=pltpu.PrefetchScalarGridSpec(num_scalar_...]
    all_to_all x0 -> x1, starting transfers between devices: none -> 7.33 us  [gather_axis(): return lax.all_to_all(spread, axis, 0, 0, tiled=True)]
    all_to_all x1, blocking collectives: 39.3 us -> 36.3 us  [body(): gathered = lax.all_to_all(payload, 'row', 0, 0, tiled=True).sum(axis=0)]
  transfers between devices with their start and end apart: 2 -> 1, of which waited for: 2 -> 1; matrix products, arithmetic and copies ran while one was open for 0% -> 0% of each run, Pallas kernels for 0% -> 0%
where the time goes in v2:
time: 189 us
  blocking collectives  127 us (67%)
  Pallas kernels  21.7 us (11%)
  waiting for transfers between devices  15.1 us (8%)
  starting transfers between devices  7.33 us (4%)
  other arithmetic  6.24 us (3%)
  matrix products  5.01 us (3%)
  local copies, waits for them, and re-layouts  4.47 us (2%)
    all_to_all x1, blocking collectives, body(): gathered = lax.all_to_all(payload, 'row', 0, 0, tiled=True).sum(axis=0)  36.3 us
    all_to_all x1, blocking collectives, body(): received = lax.all_to_all(partial_value, 'col', 0, 0, tiled=True)  34.4 us
    pallas_call x2, Pallas kernels, block_product(): pl.pallas_call(kernel, grid_spec=pltpu.PrefetchScalarGridSpec(num_scalar_...  21.7 us
    all_gather x1, blocking collectives, body(): lax.all_gather(weight_piece, 'row', axis=0, tiled=True).reshape(fin, width)  20.9 us
    psum x1, blocking collectives, body(): weight_piece = lax.psum(gathered[size:], 'col')  18.8 us
    all_to_all x1, blocking collectives, gather_axis(): return lax.all_to_all(spread, axis, 0, 0, tiled=True)  17.1 us
    all_to_all x1, waiting for transfers between devices, gather_axis(): return lax.all_to_all(spread, axis, 0, 0, tiled=True)  15.1 us
    all_to_all x1, starting transfers between devices, gather_axis(): return lax.all_to_all(spread, axis, 0, 0, tiled=True)  7.33 us
  transfers between devices with their start and end apart: 1, of which 1 were waited for; matrix products, arithmetic and copies ran while one was open for 0% of the time, Pallas kernels for 0%

profile of v2, /device:TPU:1, one launch (start us, length us, event | category | flops | bytes accessed | tf_op | source)
XLA Modules:
  0.0 188.6 jit_solution(727767777830429429)
XLA Ops:
  0.6 0.0 copy-start
  0.6 2.1 %broadcast_in_dim.4 = bf16[16,256,128]{2,1,0:T(8,128)(2,1)} broadcast(bf16[256,128]{1,0:T(8,128)(2,1)} %param.7), dimensions={1,2} | broadcast | bytes 1114112 | tf_op jit(solution)/shard_map/broadcast_in_dim | solution.py:78
  2.7 7.3 %all-to-all-start = ((bf16[16,256,128]{2,1,0:T(8,128)(2,1)}), bf16[16,256,128]{2,1,0:T(8,128)(2,1)S(1)}, u32[]{:S(2)}, u32[]{:S(2)}) async-start(bf16[16,256,128]{2,1,0:T(8,128)(2,1)} %broadcast_in_dim.4), calls=%async_computation | async-start | bytes 2097152 | tf_op jit(solution)/shard_map/all_to_all | solution.py:79
  10.7 15.1 %all-to-all-done = bf16[16,256,128]{2,1,0:T(8,128)(2,1)S(1)} async-done(((bf16[16,256,128]{2,1,0:T(8,128)(2,1)}), bf16[16,256,128]{2,1,0:T(8,128)(2,1)S(1)}, u32[]{:S(2)}, u32[]{:S(2)}) %all-to-all-start) | async-done | bytes 1048608 | tf_op jit(solution)/shard_map/all_to_all | solution.py:79
  25.8 0.0 copy-done
  25.8 2.0 %convolution_convert_fusion = bf16[4096,256]{1,0:T(8,128)(2,1)} fusion(bf16[4096,128]{1,0:T(8,128)(2,1)S(1)} %bitcast.27, bf16[128,256]{1,0:T(8,128)(2,1)S(1)} %copy-done), kind=kOutput, calls=%fused_computation | convolution fusion | flops 269484032 | bytes 3211264 | tf_op jit(solution)/shard_map/dot_general | solution.py:103
  27.8 10.6 %shard_map.94 = f32[8,256,256]{2,1,0:T(8,128)} custom-call(s32[96]{0:T(128)} %rows_ref.3, s32[96]{0:T(128)} %cols_ref.3, s32[1]{0:T(128)S(6)} %copy.17.live_ref, bf16[96,256,256]{2,1,0:T(8,128)(2,1)} %a_ref.3, bf16[16,256,256]{2,1,0:T(8,128)(2,1)} %bitcast.29), custom_call_target="tpu_custom_call" | custom-call | flops 3221225472 | bytes 16777216 | tf_op jit(solution)/shard_map/pallas_call | solution.py:56
  38.4 34.4 %all_to_all.20 = f32[8,256,256]{2,1,0:T(8,128)S(1)} all-to-all(f32[8,256,256]{2,1,0:T(8,128)} %shard_map.94), channel_id=1, replica_groups=mesh['row'=16,'col'=8] {'col'}, dimensions={0} | all-to-all | bytes 4194304 | tf_op jit(solution)/shard_map/all_to_all | solution.py:108
  72.9 0.1 reduce_sum.18
  73.0 1.7 multiply_convert_fusion
  74.7 0.1 broadcast_in_dim.5
  74.8 17.1 %all_to_all.21.src_ref = bf16[8,256,256]{2,1,0:T(8,128)(2,1)} all-to-all(bf16[8,256,256]{2,1,0:T(8,128)(2,1)S(1)} %broadcast_in_dim.5), channel_id=1, replica_groups=mesh['row'=16,'col'=8] {'col'}, dimensions={0} | all-to-all | bytes 2097152 | tf_op jit(solution)/shard_map/all_to_all | solution.py:79
  91.8 11.1 %shard_map.95 = f32[16,256,256]{2,1,0:T(8,128)} custom-call(s32[96]{0:T(128)} %rows_ref.3, s32[96]{0:T(128)} %cols_ref.3, s32[1]{0:T(128)S(6)} %copy.17.live_ref, bf16[96,256,256]{2,1,0:T(8,128)(2,1)} %a_ref.3, bf16[8,256,256]{2,1,0:T(8,128)(2,1)} %all_to_all.21.src_ref), custom_call_target="tpu_custom_call" | custom-call | flops 3221225472 | bytes 17825792 | tf_op jit(solution)/shard_map/pallas_call | solution.py:56
  102.9 0.0 copy-start.1
  102.9 4.1 %fusion = (bf16[4096,256]{1,0:T(8,128)(2,1)}, bf16[4096,256]{1,0:T(8,128)(2,1)S(1)}) fusion(f32[16,256,256]{2,1,0:T(8,128)} %shard_map.95), kind=kLoop, calls=%fused_computation.4 | loop fusion | flops 4194304 | bytes 8388608 | tf_op jit(solution)/shard_map/convert_element_type | solution.py:84
  107.1 0.0 copy-done.1
  107.1 0.8 fusion.2
  107.8 0.8 fusion.4
  108.6 0.1 copy.14
  108.8 0.0 copy-start.2
  108.8 0.7 fusion.7
  109.5 0.9 copy-done.2
  110.4 0.7 convolution_add_fusion
  111.1 0.2 pad_maximum_fusion
  111.2 36.3 %all_to_all.22 = f32[16,272,128]{2,1,0:T(8,128)S(1)} all-to-all(f32[16,272,128]{2,1,0:T(8,128)S(1)} %pad_maximum_fusion), channel_id=1, replica_groups=mesh['row'=16,'col'=8] {'row'}, dimensions={0} | all-to-all | bytes 4456448 | tf_op jit(solution)/shard_map/all_to_all | solution.py:121
  147.5 0.1 reduce_sum.19
  147.6 0.6 slice.12
  148.2 18.8 %psum.7 = f32[16,128]{1,0:T(8,128)S(1)} all-reduce(f32[16,128]{1,0:T(8,128)S(1)} %slice.10), channel_id=1, replica_groups=mesh['row'=16,'col'=8] {'col'}, use_global_device_ids=true, to_apply=%region_2.3 | all-reduce | flops 2048 | bytes 16384 | tf_op jit(solution)/shard_map/psum | solution.py:123
  167.0 20.9 %all_gather.3 = f32[256,128]{1,0:T(8,128)S(1)} all-gather(f32[16,128]{1,0:T(8,128)S(1)} %psum.7), channel_id=1, replica_groups=mesh['row'=16,'col'=8] {'row'}, dimensions={0}, use_global_device_ids=true | all-gather | bytes 139264 | tf_op jit(solution)/shard_map/all_gather | solution.py:124
  187.9 0.7 div.16
  (3 shorter events, 0.0 us)
Async XLA Ops:
  0.6 25.2 %copy-start = (bf16[128,256]{1,0:T(8,128)(2,1)S(1)}, bf16[128,256]{1,0:T(8,128)(2,1)}, u32[]{:S(2)}) copy-start(bf16[128,256]{1,0:T(8,128)(2,1)} %param.8) | copy-start | bytes 196612
  2.7 23.1 %all-to-all-start = ((bf16[16,256,128]{2,1,0:T(8,128)(2,1)}), bf16[16,256,128]{2,1,0:T(8,128)(2,1)S(1)}, u32[]{:S(2)}, u32[]{:S(2)}) async-start(bf16[16,256,128]{2,1,0:T(8,128)(2,1)} %broadcast_in_dim.4), calls=%async_computation | async-start | bytes 2097152 | tf_op jit(solution)/shard_map/all_to_all | solution.py:79
  102.9 4.1 %copy-start.1 = (f32[16,256,256]{2,1,0:T(8,128)S(1)}, f32[16,256,256]{2,1,0:T(8,128)}, u32[]{:S(2)}) copy-start(f32[16,256,256]{2,1,0:T(8,128)} %shard_map.95) | copy-start | bytes 12582916
  108.8 1.6 copy-start.2

commit v3 on v2

--- a/solution.py
+++ b/solution.py
@@ -105,8 +105,8 @@
     partial_value = block_product(
         adj_values, slot_rows, slot_cols, slot_live, column_blocks, tile_rows, False
     )
-    received = lax.all_to_all(partial_value, "col", 0, 0, tiled=True)
-    summed = received.sum(axis=0)
+    received = lax.all_to_all(partial_value.astype(jnp.bfloat16), "col", 0, 0, tiled=True)
+    summed = received.astype(jnp.float32).sum(axis=0)
     output = jax.nn.silu(summed).astype(jnp.bfloat16)
     grad_summed = (cotangent.astype(jnp.float32) * silu_slope(summed)).astype(jnp.bfloat16)
     grad_range = gather_axis(grad_summed, "col", n_col)
@@ -118,10 +118,11 @@
     weight_part = split_dot(back, feature_cols, (((0,), (0,)), ((), ()))).T
     pieces = weight_part.reshape(tile_cols, fin * width // (tile_cols * fin), fin)
     payload = jnp.concatenate([feature_part.reshape(tile_cols, size, fin), pieces], axis=1)
-    gathered = lax.all_to_all(payload, "row", 0, 0, tiled=True).sum(axis=0)
+    exchanged = lax.all_to_all(payload.astype(jnp.bfloat16), "row", 0, 0, tiled=True)
+    gathered = exchanged.astype(jnp.float32).sum(axis=0)
     grad_features = gathered[:size].astype(jnp.bfloat16)
-    weight_piece = lax.psum(gathered[size:], "col")
-    grad_weight = lax.all_gather(weight_piece, "row", axis=0, tiled=True).reshape(fin, width)
+    weight_piece = gather_axis(gathered[size:], "col", n_col).sum(axis=0)
+    grad_weight = gather_axis(weight_piece, "row", n_row).reshape(fin, width)
     grad_weight = grad_weight / math.sqrt(nodes)
     return (output, grad_features, grad_weight)
 

time: 189 us -> 151 us (0.80)
  blocking collectives: 127 us -> 84 us
  Pallas kernels: 21.7 us -> 14.7 us
  waiting for transfers between devices: 15.1 us -> 20.6 us
  starting transfers between devices: 7.33 us -> 12.5 us
    all_gather x1 -> x0, blocking collectives: 20.9 us -> none  [body(): lax.all_gather(weight_piece, 'row', axis=0, tiled=True).reshape(fin, width)]
    psum x1 -> x0, blocking collectives: 18.8 us -> none  [body(): weight_piece = lax.psum(gathered[size:], 'col')]
    all_to_all x2, blocking collectives: 70.7 us -> 57.4 us  [the longest x1 30.8 us: body(): lax.all_to_all(payload.astype(jnp.bfloat16), 'row', 0, 0, tiled=True)]
    all_to_all x1 -> x2, blocking collectives: 17.1 us -> 26.6 us  [gather_axis(): return lax.all_to_all(spread, axis, 0, 0, tiled=True)]
    pallas_call x2, Pallas kernels: 21.7 us -> 14.7 us  [block_product(): pl.pallas_call(kernel, grid_spec=pltpu.PrefetchScalarGridSpec(num_scalar_...]
    all_to_all x1 -> x2, waiting for transfers between devices: 15.1 us -> 20.6 us  [gather_axis(): return lax.all_to_all(spread, axis, 0, 0, tiled=True)]
    all_to_all x1 -> x2, starting transfers between devices: 7.33 us -> 12.5 us  [gather_axis(): return lax.all_to_all(spread, axis, 0, 0, tiled=True)]
  transfers between devices with their start and end apart: 1 -> 2, of which waited for: 1 -> 2; matrix products, arithmetic and copies ran while one was open for 0% -> 0% of each run, Pallas kernels for 0% -> 0%
where the time goes in v3:
time: 151 us; the launch traced here: 150 us
  blocking collectives  84 us (56%)
  waiting for transfers between devices  20.6 us (14%)
  Pallas kernels  14.7 us (10%)
  starting transfers between devices  12.5 us (8%)
  other arithmetic  7 us (5%)
  local copies, waits for them, and re-layouts  5.17 us (3%)
  matrix products  4.97 us (3%)
    all_to_all x1, blocking collectives, body(): lax.all_to_all(payload.astype(jnp.bfloat16), 'row', 0, 0, tiled=True)  30.8 us
    all_to_all x2, blocking collectives, gather_axis(): return lax.all_to_all(spread, axis, 0, 0, tiled=True)  26.6 us
    all_to_all x1, blocking collectives, body(): lax.all_to_all(partial_value.astype(jnp.bfloat16), 'col', 0, 0, tiled=True)  26.6 us
    all_to_all x2, waiting for transfers between devices, gather_axis(): return lax.all_to_all(spread, axis, 0, 0, tiled=True)  20.6 us
    pallas_call x2, Pallas kernels, block_product(): pl.pallas_call(kernel, grid_spec=pltpu.PrefetchScalarGridSpec(num_scalar_...  14.7 us
    all_to_all x2, starting transfers between devices, gather_axis(): return lax.all_to_all(spread, axis, 0, 0, tiled=True)  12.5 us
    convert_element_type x1, other arithmetic, split_dot(): low = (left - high.astype(jnp.float32)).astype(jnp.bfloat16)  4.13 us
  transfers between devices with their start and end apart: 2, of which 2 were waited for; matrix products, arithmetic and copies ran while one was open for 0% of the time, Pallas kernels for 0%

profile of v3, /device:TPU:1, one launch (start us, length us, event | category | flops | bytes accessed | tf_op | source)
XLA Modules:
  0.0 150.3 jit_solution(544615193757475431)
XLA Ops:
  0.6 0.0 copy-start
  0.6 2.1 %broadcast_in_dim.8 = bf16[16,256,128]{2,1,0:T(8,128)(2,1)} broadcast(bf16[256,128]{1,0:T(8,128)(2,1)} %param.7), dimensions={1,2} | broadcast | bytes 1114112 | tf_op jit(solution)/shard_map/broadcast_in_dim | solution.py:78
  2.7 7.3 %all-to-all-start = ((bf16[16,256,128]{2,1,0:T(8,128)(2,1)}), bf16[16,256,128]{2,1,0:T(8,128)(2,1)S(1)}, u32[]{:S(2)}, u32[]{:S(2)}) async-start(bf16[16,256,128]{2,1,0:T(8,128)(2,1)} %broadcast_in_dim.8), calls=%async_computation | async-start | bytes 2097152 | tf_op jit(solution)/shard_map/all_to_all | solution.py:79
  10.7 15.1 %all-to-all-done = bf16[16,256,128]{2,1,0:T(8,128)(2,1)S(1)} async-done(((bf16[16,256,128]{2,1,0:T(8,128)(2,1)}), bf16[16,256,128]{2,1,0:T(8,128)(2,1)S(1)}, u32[]{:S(2)}, u32[]{:S(2)}) %all-to-all-start) | async-done | bytes 1048608 | tf_op jit(solution)/shard_map/all_to_all | solution.py:79
  25.8 0.0 copy-done
  25.8 2.0 %convolution_convert_fusion = bf16[4096,256]{1,0:T(8,128)(2,1)} fusion(bf16[4096,128]{1,0:T(8,128)(2,1)S(1)} %bitcast.29, bf16[128,256]{1,0:T(8,128)(2,1)S(1)} %copy-done), kind=kOutput, calls=%fused_computation | convolution fusion | flops 269484032 | bytes 3211264 | tf_op jit(solution)/shard_map/dot_general | solution.py:103
  27.8 7.2 %shard_map.94 = f32[8,256,256]{2,1,0:T(8,128)} custom-call(s32[96]{0:T(128)} %rows_ref.3, s32[96]{0:T(128)} %cols_ref.3, s32[1]{0:T(128)S(6)} %copy.20.live_ref, bf16[96,256,256]{2,1,0:T(8,128)(2,1)} %a_ref.3, bf16[16,256,256]{2,1,0:T(8,128)(2,1)} %bitcast.30), custom_call_target="tpu_custom_call" | custom-call | flops 3221225472 | bytes 16777216 | tf_op jit(solution)/shard_map/pallas_call | solution.py:56
  35.0 1.7 %convert_element_type.46 = bf16[8,256,256]{2,1,0:T(8,128)(2,1)S(1)} convert(f32[8,256,256]{2,1,0:T(8,128)} %shard_map.94) | non-fusion elementwise | flops 524288 | bytes 3145728 | tf_op jit(solution)/shard_map/convert_element_type | solution.py:108
  36.7 0.0 copy-start.3
  36.7 26.6 %all_to_all.30 = bf16[8,256,256]{2,1,0:T(8,128)(2,1)S(1)} all-to-all(bf16[8,256,256]{2,1,0:T(8,128)(2,1)S(1)} %convert_element_type.46), channel_id=1, replica_groups=mesh['row'=16,'col'=8] {'col'}, dimensions={0} | all-to-all | bytes 2097152 | tf_op jit(solution)/shard_map/all_to_all | solution.py:108
  63.3 0.1 convert_reduce_fusion.1
  63.4 0.8 multiply_convert_fusion
  64.2 0.1 broadcast_in_dim.9
  64.3 17.1 %all_to_all.31.src_ref = bf16[8,256,256]{2,1,0:T(8,128)(2,1)} all-to-all(bf16[8,256,256]{2,1,0:T(8,128)(2,1)S(1)} %broadcast_in_dim.9), channel_id=1, replica_groups=mesh['row'=16,'col'=8] {'col'}, dimensions={0} | all-to-all | bytes 2097152 | tf_op jit(solution)/shard_map/all_to_all | solution.py:79
  81.3 7.6 %shard_map.95 = f32[16,256,256]{2,1,0:T(8,128)} custom-call(s32[96]{0:T(128)} %rows_ref.3, s32[96]{0:T(128)} %cols_ref.3, s32[1]{0:T(128)S(6)} %copy.20.live_ref, bf16[96,256,256]{2,1,0:T(8,128)(2,1)} %a_ref.3, bf16[8,256,256]{2,1,0:T(8,128)(2,1)} %all_to_all.31.src_ref), custom_call_target="tpu_custom_call" | custom-call | flops 3221225472 | bytes 17825792 | tf_op jit(solution)/shard_map/pallas_call | solution.py:56
  88.9 4.1 %fusion.1 = (bf16[4096,256]{1,0:T(8,128)(2,1)}, bf16[4096,256]{1,0:T(8,128)(2,1)S(1)}) fusion(f32[16,256,256]{2,1,0:T(8,128)} %shard_map.95), kind=kLoop, calls=%fused_computation.5 | loop fusion | flops 4194304 | bytes 8388608 | tf_op jit(solution)/shard_map/convert_element_type | solution.py:84
  93.0 0.8 fusion.3
  93.8 0.8 fusion.6
  94.6 0.1 copy.17
  94.8 0.0 copy-start.2
  94.8 0.7 fusion.9
  95.5 0.9 copy-done.2
  96.4 0.7 fusion
  97.1 0.1 pad_maximum_fusion
  97.1 30.8 %all_to_all.32 = bf16[16,272,128]{2,1,0:T(8,128)(2,1)S(1)} all-to-all(bf16[16,272,128]{2,1,0:T(8,128)(2,1)S(1)} %pad_maximum_fusion), channel_id=1, replica_groups=mesh['row'=16,'col'=8] {'row'}, dimensions={0} | all-to-all | bytes 2228224 | tf_op jit(solution)/shard_map/all_to_all | solution.py:121
  127.9 0.2 convert_reduce_fusion
  128.1 9.6 %all_to_all.33 = f32[8,16,128]{2,1,0:T(8,128)S(1)} all-to-all(f32[8,16,128]{2,1,0:T(8,128)S(1)} %broadcast_in_dim.10), channel_id=1, replica_groups=mesh['row'=16,'col'=8] {'col'}, dimensions={0} | all-to-all | bytes 131072 | tf_op jit(solution)/shard_map/all_to_all | solution.py:79
  137.7 0.7 broadcast_in_dim.11
  138.3 5.1 %all-to-all-start.5 = ((f32[16,16,128]{2,1,0:T(8,128)}), f32[16,16,128]{2,1,0:T(8,128)S(1)}, u32[]{:S(2)}, u32[]{:S(2)}) async-start(f32[16,16,128]{2,1,0:T(8,128)} %broadcast_in_dim.11), calls=%async_computation.5 | async-start | bytes 262144 | tf_op jit(solution)/shard_map/all_to_all | solution.py:79
  143.5 0.6 slice.12
  144.1 5.5 %all-to-all-done.5 = f32[16,16,128]{2,1,0:T(8,128)S(1)} async-done(((f32[16,16,128]{2,1,0:T(8,128)}), f32[16,16,128]{2,1,0:T(8,128)S(1)}, u32[]{:S(2)}, u32[]{:S(2)}) %all-to-all-start.5) | async-done | bytes 131104 | tf_op jit(solution)/shard_map/all_to_all | solution.py:79
  149.6 0.7 div.16
  (8 shorter events, 0.1 us)
Async XLA Ops:
  0.6 25.2 %copy-start = (bf16[128,256]{1,0:T(8,128)(2,1)S(1)}, bf16[128,256]{1,0:T(8,128)(2,1)}, u32[]{:S(2)}) copy-start(bf16[128,256]{1,0:T(8,128)(2,1)} %param.8) | copy-start | bytes 196612
  2.7 23.1 %all-to-all-start = ((bf16[16,256,128]{2,1,0:T(8,128)(2,1)}), bf16[16,256,128]{2,1,0:T(8,128)(2,1)S(1)}, u32[]{:S(2)}, u32[]{:S(2)}) async-start(bf16[16,256,128]{2,1,0:T(8,128)(2,1)} %broadcast_in_dim.8), calls=%async_computation | async-start | bytes 2097152 | tf_op jit(solution)/shard_map/all_to_all | solution.py:79
  36.7 26.7 %copy-start.3 = (bf16[256,256]{1,0:T(8,128)(2,1)S(1)}, bf16[256,256]{1,0:T(8,128)(2,1)}, u32[]{:S(2)}) copy-start(bf16[256,256]{1,0:T(8,128)(2,1)} %param.13) | copy-start | bytes 393220
  88.9 4.1 %copy-start.1 = (f32[16,256,256]{2,1,0:T(8,128)S(1)}, f32[16,256,256]{2,1,0:T(8,128)}, u32[]{:S(2)}) copy-start(f32[16,256,256]{2,1,0:T(8,128)} %shard_map.95) | copy-start | bytes 12582916
  94.8 1.6 %copy-start.2 = (bf16[4096,256]{1,0:T(8,128)(2,1)S(1)}, bf16[4096,256]{1,0:T(8,128)(2,1)}, u32[]{:S(2)}) copy-start(bf16[4096,256]{1,0:T(8,128)(2,1)} %get-tuple-element.3) | copy-start | bytes 6291460
  138.3 11.3 %all-to-all-start.5 = ((f32[16,16,128]{2,1,0:T(8,128)}), f32[16,16,128]{2,1,0:T(8,128)S(1)}, u32[]{:S(2)}, u32[]{:S(2)}) async-start(f32[16,16,128]{2,1,0:T(8,128)} %broadcast_in_dim.11), calls=%async_computation.5 | async-start | bytes 262144 | tf_op jit(solution)/shard_map/all_to_all | solution.py:79

commit v4 on v3

--- a/solution.py
+++ b/solution.py
@@ -74,6 +74,18 @@
     )(slot_rows, slot_cols, slot_live, adj_values, source)
 
 
+def dense_tile(adj_values, slot_rows, slot_cols, slot_live, n_r, n_c):
+    slots, size, _ = adj_values.shape
+    ids = jnp.arange(slots, dtype=jnp.int32)
+    live = ids < slot_live[0]
+    flat = jnp.clip(slot_rows, 0, n_r - 1) * n_c + jnp.clip(slot_cols, 0, n_c - 1)
+    pos = jnp.full((n_r * n_c,), slots, jnp.int32).at[flat].set(jnp.where(live, ids, slots))
+    blocks = jnp.where(
+        (pos < slots)[:, None, None], adj_values[jnp.minimum(pos, slots - 1)], jnp.zeros((), adj_values.dtype)
+    )
+    return blocks.reshape(n_r, n_c, size, size).transpose(0, 2, 1, 3).reshape(n_r * size, n_c * size)
+
+
 def gather_axis(block, axis, count):
     spread = jnp.broadcast_to(block[None], (count,) + block.shape)
     return lax.all_to_all(spread, axis, 0, 0, tiled=True)
@@ -101,19 +113,17 @@
 
     feature_cols = gather_axis(features, "row", n_row).reshape(own_rows * n_row, fin)
     projected = jnp.dot(feature_cols, weight, preferred_element_type=jnp.float32).astype(jnp.bfloat16)
-    column_blocks = projected.reshape(tile_cols, size, width)
-    partial_value = block_product(
-        adj_values, slot_rows, slot_cols, slot_live, column_blocks, tile_rows, False
-    )
+    matrix = dense_tile(adj_values, slot_rows, slot_cols, slot_live, tile_rows, tile_cols)
+    partial_value = jnp.dot(matrix, projected, preferred_element_type=jnp.float32).reshape(tile_rows, size, width)
     received = lax.all_to_all(partial_value.astype(jnp.bfloat16), "col", 0, 0, tiled=True)
     summed = received.astype(jnp.float32).sum(axis=0)
     output = jax.nn.silu(summed).astype(jnp.bfloat16)
     grad_summed = (cotangent.astype(jnp.float32) * silu_slope(summed)).astype(jnp.bfloat16)
     grad_range = gather_axis(grad_summed, "col", n_col)
-    grad_blocks = grad_range.reshape(tile_rows, size, width)
-    back = block_product(
-        adj_values, slot_rows, slot_cols, slot_live, grad_blocks, tile_cols, True
-    ).reshape(tile_cols * size, width)
+    back = lax.dot_general(
+        matrix, grad_range.reshape(tile_rows * size, width), (((0,), (0,)), ((), ())),
+        preferred_element_type=jnp.float32,
+    )
     feature_part = split_dot(back, weight, (((1,), (1,)), ((), ())))
     weight_part = split_dot(back, feature_cols, (((0,), (0,)), ((), ()))).T
     pieces = weight_part.reshape(tile_cols, fin * width // (tile_cols * fin), fin)

time: 151 us -> 200 us (1.32)
  local copies, waits for them, and re-layouts: 5.17 us -> 55.8 us
  other arithmetic: 7 us -> 35.1 us
  blocking collectives: 84 us -> 59.2 us
  matrix products: 4.97 us -> 25.4 us
  waiting for transfers between devices: 20.6 us -> 5.5 us
  Pallas kernels: 14.7 us -> 0 us
  starting transfers between devices: 12.5 us -> 16.3 us
    dot_general x0 -> x1, local copies, waits for them, and re-layouts: none -> 25.6 us  [body(): jnp.dot(matrix, projected, preferred_element_type=jnp.float32)]
    transpose x0 -> x1, other arithmetic: none -> 18.6 us  [dense_tile(): blocks.reshape(n_r, n_c, size, size).transpose(0, 2, 1, 3)]
    dot_general x1 -> x2, matrix products: 2.03 us -> 19 us  [the longest x1 10.3 us: body(): jnp.dot(matrix, projected, preferred_element_type=jnp.float32)]
    select_n x0 -> x3, other arithmetic: none -> 15.4 us  [the longest x1 14.7 us: dense_tile(): jnp.where((pos < slots)[:, None, None], adj_values[jnp.minimum(pos, slots...]
    all_to_all x2 -> x3, waiting for transfers between devices: 20.6 us -> 5.5 us  [gather_axis(): return lax.all_to_all(spread, axis, 0, 0, tiled=True)]
    pallas_call x2 -> x0, Pallas kernels: 14.7 us -> none  [block_product(): pl.pallas_call(kernel, grid_spec=pltpu.PrefetchScalarGridSpec(num_scalar_...]
    all_to_all x2 -> x1, blocking collectives: 26.6 us -> 13.7 us  [gather_axis(): return lax.all_to_all(spread, axis, 0, 0, tiled=True)]
    gather x0 -> x1, local copies, waits for them, and re-layouts: none -> 12.9 us  [dense_tile(): adj_values[jnp.minimum(pos, slots - 1)]]
  transfers between devices with their start and end apart: 2 -> 3, of which waited for: 2 -> 1; matrix products, arithmetic and copies ran while one was open for 0% -> 43% of each run, Pallas kernels for 0% -> 0%
where the time goes in v4:
time: 200 us; the launch traced here: 199 us
  blocking collectives  59.2 us (30%)
  local copies, waits for them, and re-layouts  55.8 us (28%)
  other arithmetic  35.1 us (18%)
  matrix products  25.4 us (13%)
  starting transfers between devices  16.3 us (8%)
  waiting for transfers between devices  5.5 us (3%)
    dot_general x1, local copies, waits for them, and re-layouts, body(): jnp.dot(matrix, projected, preferred_element_type=jnp.float32)  25.6 us
    all_to_all x1, blocking collectives, body(): lax.all_to_all(payload.astype(jnp.bfloat16), 'row', 0, 0, tiled=True)  23.6 us
    all_to_all x1, blocking collectives, body(): lax.all_to_all(partial_value.astype(jnp.bfloat16), 'col', 0, 0, tiled=True)  22 us
    transpose x1, other arithmetic, dense_tile(): blocks.reshape(n_r, n_c, size, size).transpose(0, 2, 1, 3)  18.6 us
    all_to_all x3, starting transfers between devices, gather_axis(): return lax.all_to_all(spread, axis, 0, 0, tiled=True)  16.3 us
    select_n x1, other arithmetic, dense_tile(): jnp.where((pos < slots)[:, None, None], adj_values[jnp.minimum(pos, slots...  14.7 us
    all_to_all x1, blocking collectives, gather_axis(): return lax.all_to_all(spread, axis, 0, 0, tiled=True)  13.7 us
    gather x1, local copies, waits for them, and re-layouts, dense_tile(): adj_values[jnp.minimum(pos, slots - 1)]  12.9 us
  transfers between devices with their start and end apart: 3, of which 1 were waited for; matrix products, arithmetic and copies ran while one was open for 43% of the time, Pallas kernels for 0%

profile of v4, /device:TPU:1, one launch (start us, length us, event | category | flops | bytes accessed | tf_op | source)
XLA Modules:
  0.0 198.8 jit_solution(14902238584358223290)
XLA Ops:
  0.6 2.0 %broadcast_in_dim.55 = bf16[16,256,128]{2,1,0:T(8,128)(2,1)} broadcast(bf16[256,128]{1,0:T(8,128)(2,1)} %param.7), dimensions={1,2} | broadcast | bytes 1114112 | tf_op jit(solution)/shard_map/broadcast_in_dim | solution.py:90
  2.7 7.3 %all-to-all-start = ((bf16[16,256,128]{2,1,0:T(8,128)(2,1)}), bf16[16,256,128]{2,1,0:T(8,128)(2,1)S(1)}, u32[]{:S(2)}, u32[]{:S(2)}) async-start(bf16[16,256,128]{2,1,0:T(8,128)(2,1)} %broadcast_in_dim.55), calls=%async_computation | async-start | bytes 2097152 | tf_op jit(solution)/shard_map/all_to_all | solution.py:91
  10.7 0.7 compare_select_fusion.1
  11.4 0.9 scatter_custom_fusion
  12.3 0.1 broadcast_in_dim.51
  12.4 12.9 %gather_fusion = bf16[128,256,256]{2,1,0:T(8,128)(2,1)} fusion(bf16[96,256,256]{2,1,0:T(8,128)(2,1)} %param.9, s32[1024]{0:T(1024)S(1)} %pad_clamp_fusion), kind=kCustom, calls=%fused_computation | custom fusion | bytes 33554944 | tf_op jit(solution)/shard_map/gather | solution.py:84
  25.2 18.6 %fusion.20 = bf16[8,256,16,256]{3,2,1,0:T(8,128)(2,1)} fusion(bf16[8,16,256,256]{3,2,1,0:T(8,128)(2,1)} %bitcast.28, pred[8,16]{1,0:T(8,128)(4,1)S(1)} %broadcast_in_dim.51), kind=kLoop, calls=%fused_computation.32 | loop fusion | flops 8388608 | bytes 33554560 | tf_op jit(solution)/shard_map/transpose | solution.py:86
  43.8 25.6 %dot_general.23 = bf16[8,256,4096]{2,1,0:T(8,128)(2,1)} reshape(bf16[8,256,16,256]{3,2,1,0:T(8,128)(2,1)} %fusion.20) | data formatting | bytes 33554432 | tf_op jit(solution)/shard_map/dot_general | solution.py:117
  69.4 10.3 %convolution_convert_fusion.1 = bf16[8,256,256]{2,1,0:T(8,128)(2,1)S(1)} fusion(bf16[8,256,4096]{2,1,0:T(8,128)(2,1)} %dot_general.23, bf16[4096,128]{1,0:T(8,128)(2,1)S(1)} %bitcast.32, bf16[128,256]{1,0:T(8,128)(2,1)S(1)} %copy-done), kind=kOutput, calls=%fused_computation.10 | convolution fusion | flops 4564975616 | bytes 18939904 | tf_op jit(solution)/shard_map/dot_general | solution.py:117
  79.7 22.0 %all_to_all.30 = bf16[8,256,256]{2,1,0:T(8,128)(2,1)S(1)} all-to-all(bf16[8,256,256]{2,1,0:T(8,128)(2,1)S(1)} %convolution_convert_fusion.1), channel_id=1, replica_groups=mesh['row'=16,'col'=8] {'col'}, dimensions={0} | all-to-all | bytes 2097152 | tf_op jit(solution)/shard_map/all_to_all | solution.py:118
  101.7 0.1 convert_reduce_fusion.1
  101.8 0.8 multiply_convert_fusion
  102.6 1.1 broadcast_in_dim.56
  103.7 3.9 %all-to-all-start.2 = ((bf16[8,256,256]{2,1,0:T(8,128)(2,1)}), bf16[8,256,256]{2,1,0:T(8,128)(2,1)S(1)}, u32[]{:S(2)}, u32[]{:S(2)}) async-start(bf16[8,256,256]{2,1,0:T(8,128)(2,1)} %broadcast_in_dim.56), calls=%async_computation.2 | async-start | bytes 2097152 | tf_op jit(solution)/shard_map/all_to_all | solution.py:91
  107.5 14.7 %copy_select_fusion = bf16[8,16,256,256]{3,1,2,0:T(8,128)(2,1)S(1)} fusion(bf16[8,16,256,256]{3,2,1,0:T(8,128)(2,1)} %bitcast.29, pred[8,16]{1,0:T(8,128)(4,1)S(1)} %broadcast_in_dim.51), kind=kLoop, calls=%fused_computation.2 | loop fusion | flops 8388608 | bytes 33554560 | tf_op jit(solution)/shard_map/jit(_where)/select_n | solution.py:83
  122.3 10.7 %copy.15 = bf16[256,8,16,256]{3,1,2,0:T(8,128)(2,1)} copy(bf16[256,8,16,256]{3,2,1,0:T(8,128)(2,1)S(1)} %bitcast.30) | data formatting | bytes 33554432
  132.9 8.7 %fusion.10 = f32[4096,256]{1,0:T(8,128)S(1)} fusion(bf16[2048,4096]{1,0:T(8,128)(2,1)} %bitcast.31, bf16[2048,256]{1,0:T(8,128)(2,1)S(1)} %bitcast.36), kind=kOutput, calls=%fused_computation.31 | convolution fusion | flops 4294967296 | bytes 22020096 | tf_op jit(solution)/shard_map/dot_general | solution.py:123
  141.6 0.8 fusion.6
  142.4 0.7 fusion.8
  143.1 0.4 copy-done.1
  143.6 0.8 fusion.3
  144.3 0.1 copy.14
  144.5 4.2 %fusion.1 = bf16[4096,128]{1,0:T(8,128)(2,1)S(1)} fusion(f32[4096,128]{1,0:T(8,128)S(1)} %fusion.8, bf16[128,256]{1,0:T(8,128)(2,1)S(1)} %copy-done, f32[4096,256]{1,0:T(8,128)} %copy-done.1), kind=kOutput, calls=%fused_computation.6 | convolution fusion | flops 273678336 | bytes 7405568 | tf_op jit(solution)/shard_map/dot_general | solution.py:98
  148.7 0.1 pad_maximum_fusion
  148.8 23.6 %all_to_all.31 = bf16[16,272,128]{2,1,0:T(8,128)(2,1)S(1)} all-to-all(bf16[16,272,128]{2,1,0:T(8,128)(2,1)S(1)} %pad_maximum_fusion), channel_id=1, replica_groups=mesh['row'=16,'col'=8] {'row'}, dimensions={0} | all-to-all | bytes 2228224 | tf_op jit(solution)/shard_map/all_to_all | solution.py:131
  172.3 0.2 convert_reduce_fusion
  172.5 13.7 %all_to_all.32 = f32[8,16,128]{2,1,0:T(8,128)S(1)} all-to-all(f32[8,16,128]{2,1,0:T(8,128)S(1)} %broadcast_in_dim.57), channel_id=1, replica_groups=mesh['row'=16,'col'=8] {'col'}, dimensions={0} | all-to-all | bytes 131072 | tf_op jit(solution)/shard_map/all_to_all | solution.py:91
  186.2 0.7 broadcast_in_dim.58
  186.9 5.1 %all-to-all-start.5 = ((f32[16,16,128]{2,1,0:T(8,128)}), f32[16,16,128]{2,1,0:T(8,128)S(1)}, u32[]{:S(2)}, u32[]{:S(2)}) async-start(f32[16,16,128]{2,1,0:T(8,128)} %broadcast_in_dim.58), calls=%async_computation.5 | async-start | bytes 262144 | tf_op jit(solution)/shard_map/all_to_all | solution.py:91
  192.0 0.6 slice.14
  192.6 5.5 %all-to-all-done.5 = f32[16,16,128]{2,1,0:T(8,128)S(1)} async-done(((f32[16,16,128]{2,1,0:T(8,128)}), f32[16,16,128]{2,1,0:T(8,128)S(1)}, u32[]{:S(2)}, u32[]{:S(2)}) %all-to-all-start.5) | async-done | bytes 131104 | tf_op jit(solution)/shard_map/all_to_all | solution.py:91
  198.1 0.7 div.16
  (15 shorter events, 0.1 us)
Async XLA Ops:
  0.6 68.7 %copy-start = (bf16[128,256]{1,0:T(8,128)(2,1)S(1)}, bf16[128,256]{1,0:T(8,128)(2,1)}, u32[]{:S(2)}) copy-start(bf16[128,256]{1,0:T(8,128)(2,1)} %param.8) | copy-start | bytes 196612
  2.7 66.7 %all-to-all-start = ((bf16[16,256,128]{2,1,0:T(8,128)(2,1)}), bf16[16,256,128]{2,1,0:T(8,128)(2,1)S(1)}, u32[]{:S(2)}, u32[]{:S(2)}) async-start(bf16[16,256,128]{2,1,0:T(8,128)(2,1)} %broadcast_in_dim.55), calls=%async_computation | async-start | bytes 2097152 | tf_op jit(solution)/shard_map/all_to_all | solution.py:91
  69.4 32.4 %copy-start.2 = (bf16[256,256]{1,0:T(8,128)(2,1)S(1)}, bf16[256,256]{1,0:T(8,128)(2,1)}, u32[]{:S(2)}) copy-start(bf16[256,256]{1,0:T(8,128)(2,1)} %param.13) | copy-start | bytes 393220
  103.7 29.3 %all-to-all-start.2 = ((bf16[8,256,256]{2,1,0:T(8,128)(2,1)}), bf16[8,256,256]{2,1,0:T(8,128)(2,1)S(1)}, u32[]{:S(2)}, u32[]{:S(2)}) async-start(bf16[8,256,256]{2,1,0:T(8,128)(2,1)} %broadcast_in_dim.56), calls=%async_computation.2 | async-start | bytes 2097152 | tf_op jit(solution)/shard_map/all_to_all | solution.py:91
  141.6 1.9 copy-start.1
  186.9 11.3 %all-to-all-start.5 = ((f32[16,16,128]{2,1,0:T(8,128)}), f32[16,16,128]{2,1,0:T(8,128)S(1)}, u32[]{:S(2)}, u32[]{:S(2)}) async-start(f32[16,16,128]{2,1,0:T(8,128)} %broadcast_in_dim.58), calls=%async_computation.5 | async-start | bytes 262144 | tf_op jit(solution)/shard_map/all_to_all | solution.py:91

commit v5 on v3

--- a/solution.py
+++ b/solution.py
@@ -9,6 +9,7 @@
 from jax.sharding import PartitionSpec as P
 
 GROUP = 8
+PARTS = 2
 
 
 def silu_slope(value):
@@ -43,9 +44,10 @@
             out_ref[placed] += product * keep
 
 
-def block_product(adj_values, slot_rows, slot_cols, slot_live, source, count_out, transposed):
+def block_product(adj_values, slot_rows, slot_cols, slot_live, source, count_out, transposed, part=0, parts=1):
     slots, size, _ = adj_values.shape
-    n_in, _, width = source.shape
+    n_in, _, full = source.shape
+    width = full // parts
     steps = slots // GROUP
 
     def a_map(g, rows, cols, live):
@@ -60,7 +62,7 @@
             grid=(steps,),
             in_specs=[
                 pl.BlockSpec((GROUP, size, size), a_map),
-                pl.BlockSpec((n_in, size, width), lambda g, r, c, l: (0, 0, 0)),
+                pl.BlockSpec((n_in, size, width), lambda g, r, c, l: (0, 0, part)),
             ],
             out_specs=pl.BlockSpec((count_out, size, width), lambda g, r, c, l: (0, 0, 0)),
         ),
@@ -102,18 +104,20 @@
     feature_cols = gather_axis(features, "row", n_row).reshape(own_rows * n_row, fin)
     projected = jnp.dot(feature_cols, weight, preferred_element_type=jnp.float32).astype(jnp.bfloat16)
     column_blocks = projected.reshape(tile_cols, size, width)
-    partial_value = block_product(
-        adj_values, slot_rows, slot_cols, slot_live, column_blocks, tile_rows, False
-    )
-    received = lax.all_to_all(partial_value.astype(jnp.bfloat16), "col", 0, 0, tiled=True)
-    summed = received.astype(jnp.float32).sum(axis=0)
-    output = jax.nn.silu(summed).astype(jnp.bfloat16)
-    grad_summed = (cotangent.astype(jnp.float32) * silu_slope(summed)).astype(jnp.bfloat16)
-    grad_range = gather_axis(grad_summed, "col", n_col)
-    grad_blocks = grad_range.reshape(tile_rows, size, width)
-    back = block_product(
-        adj_values, slot_rows, slot_cols, slot_live, grad_blocks, tile_cols, True
-    ).reshape(tile_cols * size, width)
+    outputs, backs = [], []
+    for part in range(PARTS):
+        partial_value = block_product(
+            adj_values, slot_rows, slot_cols, slot_live, column_blocks, tile_rows, False, part, PARTS
+        )
+        received = lax.all_to_all(partial_value.astype(jnp.bfloat16), "col", 0, 0, tiled=True)
+        summed = received.astype(jnp.float32).sum(axis=0)
+        outputs.append(jax.nn.silu(summed).astype(jnp.bfloat16))
+        cot = cotangent[:, part * (width // PARTS):(part + 1) * (width // PARTS)]
+        grad_summed = (cot.astype(jnp.float32) * silu_slope(summed)).astype(jnp.bfloat16)
+        grad_range = gather_axis(grad_summed, "col", n_col)
+        backs.append(block_product(adj_values, slot_rows, slot_cols, slot_live, grad_range, tile_cols, True))
+    output = jnp.concatenate(outputs, axis=1)
+    back = jnp.concatenate(backs, axis=2).reshape(tile_cols * size, width)
     feature_part = split_dot(back, weight, (((1,), (1,)), ((), ())))
     weight_part = split_dot(back, feature_cols, (((0,), (0,)), ((), ()))).T
     pieces = weight_part.reshape(tile_cols, fin * width // (tile_cols * fin), fin)

time: 151 us -> 185 us (1.23)
  starting transfers between devices: 12.5 us -> 39.9 us
  blocking collectives: 84 us -> 58.1 us
  Pallas kernels: 14.7 us -> 32.6 us
  waiting for transfers between devices: 20.6 us -> 29.1 us
  other arithmetic: 7 us -> 12 us
    all_to_all x1 -> x0, blocking collectives: 26.6 us -> none  [body(): lax.all_to_all(partial_value.astype(jnp.bfloat16), 'col', 0, 0, tiled=True)]
    all_to_all x0 -> x2, starting transfers between devices: none -> 23.3 us  [body(): lax.all_to_all(partial_value.astype(jnp.bfloat16), 'col', 0, 0, tiled=True)]
    pallas_call x2 -> x4, Pallas kernels: 14.7 us -> 32.6 us  [block_product(): pl.pallas_call(kernel, grid_spec=pltpu.PrefetchScalarGridSpec(num_scalar_...]
    all_to_all x0 -> x2, waiting for transfers between devices: none -> 8.46 us  [body(): lax.all_to_all(partial_value.astype(jnp.bfloat16), 'col', 0, 0, tiled=True)]
    concatenate x0 -> x2, other arithmetic: none -> 4.62 us  [the longest x1 3.95 us: body(): back = jnp.concatenate(backs, axis=2).reshape(tile_cols * size, width)]
    all_to_all x2 -> x3, starting transfers between devices: 12.5 us -> 16.6 us  [gather_axis(): return lax.all_to_all(spread, axis, 0, 0, tiled=True)]
    all_to_all x1, blocking collectives: 30.8 us -> 33.9 us  [body(): lax.all_to_all(payload.astype(jnp.bfloat16), 'row', 0, 0, tiled=True)]
    convert_element_type x1 -> x2, other arithmetic: 1.7 us -> 4.23 us  [body(): partial_value.astype(jnp.bfloat16)]
  transfers between devices with their start and end apart: 2 -> 5, of which waited for: 2 -> 4; matrix products, arithmetic and copies ran while one was open for 0% -> 2% of each run, Pallas kernels for 0% -> 9%
where the time goes in v5:
time: 185 us; the launch traced here: 183 us
  blocking collectives  58.1 us (31%)
  starting transfers between devices  39.9 us (22%)
  Pallas kernels  32.6 us (18%)
  waiting for transfers between devices  29.1 us (16%)
  other arithmetic  12 us (6%)
  local copies, waits for them, and re-layouts  5.12 us (3%)
  matrix products  4.94 us (3%)
    all_to_all x1, blocking collectives, body(): lax.all_to_all(payload.astype(jnp.bfloat16), 'row', 0, 0, tiled=True)  33.9 us
    pallas_call x4, Pallas kernels, block_product(): pl.pallas_call(kernel, grid_spec=pltpu.PrefetchScalarGridSpec(num_scalar_...  32.6 us
    all_to_all x2, blocking collectives, gather_axis(): return lax.all_to_all(spread, axis, 0, 0, tiled=True)  24.2 us
    all_to_all x2, starting transfers between devices, body(): lax.all_to_all(partial_value.astype(jnp.bfloat16), 'col', 0, 0, tiled=True)  23.3 us
    all_to_all x3, waiting for transfers between devices, gather_axis(): return lax.all_to_all(spread, axis, 0, 0, tiled=True)  20.6 us
    all_to_all x3, starting transfers between devices, gather_axis(): return lax.all_to_all(spread, axis, 0, 0, tiled=True)  16.6 us
    all_to_all x2, waiting for transfers between devices, body(): lax.all_to_all(partial_value.astype(jnp.bfloat16), 'col', 0, 0, tiled=True)  8.46 us
    convert_element_type x2, other arithmetic, body(): partial_value.astype(jnp.bfloat16)  4.23 us
  transfers between devices with their start and end apart: 5, of which 4 were waited for; matrix products, arithmetic and copies ran while one was open for 2% of the time, Pallas kernels for 9%

profile of v5, /device:TPU:1, one launch (start us, length us, event | category | flops | bytes accessed | tf_op | source)
XLA Modules:
  0.0 183.2 jit_solution(7742595925229129659)
XLA Ops:
  0.6 2.0 %broadcast_in_dim.10 = bf16[16,256,128]{2,1,0:T(8,128)(2,1)} broadcast(bf16[256,128]{1,0:T(8,128)(2,1)} %param.7), dimensions={1,2} | broadcast | bytes 1114112 | tf_op jit(solution)/shard_map/broadcast_in_dim | solution.py:80
  2.7 7.3 %all-to-all-start = ((bf16[16,256,128]{2,1,0:T(8,128)(2,1)}), bf16[16,256,128]{2,1,0:T(8,128)(2,1)S(1)}, u32[]{:S(2)}, u32[]{:S(2)}) async-start(bf16[16,256,128]{2,1,0:T(8,128)(2,1)} %broadcast_in_dim.10), calls=%async_computation | async-start | bytes 2097152 | tf_op jit(solution)/shard_map/all_to_all | solution.py:81
  10.7 15.1 %all-to-all-done = bf16[16,256,128]{2,1,0:T(8,128)(2,1)S(1)} async-done(((bf16[16,256,128]{2,1,0:T(8,128)(2,1)}), bf16[16,256,128]{2,1,0:T(8,128)(2,1)S(1)}, u32[]{:S(2)}, u32[]{:S(2)}) %all-to-all-start) | async-done | bytes 1048608 | tf_op jit(solution)/shard_map/all_to_all | solution.py:81
  25.8 2.0 %convolution_convert_fusion = bf16[4096,256]{1,0:T(8,128)(2,1)} fusion(bf16[4096,128]{1,0:T(8,128)(2,1)S(1)} %bitcast.31, bf16[128,256]{1,0:T(8,128)(2,1)S(1)} %copy-done), kind=kOutput, calls=%fused_computation | convolution fusion | flops 269484032 | bytes 3211264 | tf_op jit(solution)/shard_map/dot_general | solution.py:105
  27.8 8.0 %shard_map.95 = f32[8,256,128]{2,1,0:T(8,128)} custom-call(s32[96]{0:T(128)} %rows_ref.7, s32[96]{0:T(128)} %cols_ref.7, s32[1]{0:T(128)S(6)} %copy.20.live_ref, bf16[96,256,256]{2,1,0:T(8,128)(2,1)} %a_ref.7, bf16[16,256,256]{2,1,0:T(8,128)(2,1)} %bitcast.29), custom_call_target="tpu_custom_call" | custom-call | flops 1610612736 | bytes 14680064 | tf_op jit(solution)/shard_map/pallas_call | solution.py:58
  35.7 2.1 %convert_element_type.64 = bf16[8,256,128]{2,1,0:T(8,128)(2,1)} convert(f32[8,256,128]{2,1,0:T(8,128)} %shard_map.95) | non-fusion elementwise | flops 262144 | bytes 1572864 | tf_op jit(solution)/shard_map/convert_element_type | solution.py:112
  37.8 11.8 %all-to-all-start.2 = ((bf16[8,256,128]{2,1,0:T(8,128)(2,1)}), bf16[8,256,128]{2,1,0:T(8,128)(2,1)S(1)}, u32[]{:S(2)}, u32[]{:S(2)}) async-start(bf16[8,256,128]{2,1,0:T(8,128)(2,1)} %convert_element_type.64), calls=%async_computation.2 | async-start | bytes 1048576 | tf_op jit(solution)/shard_map/all_to_all | solution.py:112
  49.7 8.0 %shard_map.94 = f32[8,256,128]{2,1,0:T(8,128)} custom-call(s32[96]{0:T(128)} %rows_ref.7, s32[96]{0:T(128)} %cols_ref.7, s32[1]{0:T(128)S(6)} %copy.20.live_ref, bf16[96,256,256]{2,1,0:T(8,128)(2,1)} %a_ref.7, bf16[16,256,256]{2,1,0:T(8,128)(2,1)} %bitcast.30), custom_call_target="tpu_custom_call" | custom-call | flops 1610612736 | bytes 14680064 | tf_op jit(solution)/shard_map/pallas_call | solution.py:58
  57.6 2.1 %convert_element_type.61 = bf16[8,256,128]{2,1,0:T(8,128)(2,1)} convert(f32[8,256,128]{2,1,0:T(8,128)} %shard_map.94) | non-fusion elementwise | flops 262144 | bytes 1572864 | tf_op jit(solution)/shard_map/convert_element_type | solution.py:112
  59.8 11.4 %all-to-all-start.1 = ((bf16[8,256,128]{2,1,0:T(8,128)(2,1)}), bf16[8,256,128]{2,1,0:T(8,128)(2,1)S(1)}, u32[]{:S(2)}, u32[]{:S(2)}) async-start(bf16[8,256,128]{2,1,0:T(8,128)(2,1)} %convert_element_type.61), calls=%async_computation.1 | async-start | bytes 1048576 | tf_op jit(solution)/shard_map/all_to_all | solution.py:112
  71.3 8.5 %all-to-all-done.1 = bf16[8,256,128]{2,1,0:T(8,128)(2,1)S(1)} async-done(((bf16[8,256,128]{2,1,0:T(8,128)(2,1)}), bf16[8,256,128]{2,1,0:T(8,128)(2,1)S(1)}, u32[]{:S(2)}, u32[]{:S(2)}) %all-to-all-start.1) | async-done | bytes 524320 | tf_op jit(solution)/shard_map/all_to_all | solution.py:112
  80.0 11.8 %all_to_all.40.src_ref = bf16[8,256,128]{2,1,0:T(8,128)(2,1)} all-to-all(bf16[8,256,128]{2,1,0:T(8,128)(2,1)S(1)} %broadcast_in_dim.12), channel_id=1, replica_groups=mesh['row'=16,'col'=8] {'col'}, dimensions={0} | all-to-all | bytes 1048576 | tf_op jit(solution)/shard_map/all_to_all | solution.py:81
  91.8 0.9 broadcast_in_dim.11
  92.7 4.2 %all-to-all-start.3 = ((bf16[8,256,128]{2,1,0:T(8,128)(2,1)}), bf16[8,256,128]{2,1,0:T(8,128)(2,1)}, u32[]{:S(2)}, u32[]{:S(2)}) async-start(bf16[8,256,128]{2,1,0:T(8,128)(2,1)} %broadcast_in_dim.11), calls=%async_computation.3 | async-start | bytes 1048576 | tf_op jit(solution)/shard_map/all_to_all | solution.py:81
  96.8 8.3 %shard_map.97 = f32[16,256,128]{2,1,0:T(8,128)} custom-call(s32[96]{0:T(128)} %rows_ref.7, s32[96]{0:T(128)} %cols_ref.7, s32[1]{0:T(128)S(6)} %copy.20.live_ref, bf16[96,256,256]{2,1,0:T(8,128)(2,1)} %a_ref.7, bf16[8,256,128]{2,1,0:T(8,128)(2,1)} %all_to_all.40.src_ref), custom_call_target="tpu_custom_call" | custom-call | flops 1610612736 | bytes 15204352 | tf_op jit(solution)/shard_map/pallas_call | solution.py:58
  105.2 0.7 all-to-all-done.3.src_ref
  105.9 8.3 %shard_map.96 = f32[16,256,128]{2,1,0:T(8,128)} custom-call(s32[96]{0:T(128)} %rows_ref.7, s32[96]{0:T(128)} %cols_ref.7, s32[1]{0:T(128)S(6)} %copy.20.live_ref, bf16[96,256,256]{2,1,0:T(8,128)(2,1)} %a_ref.7, bf16[8,256,128]{2,1,0:T(8,128)(2,1)} %all-to-all-done.3.src_ref), custom_call_target="tpu_custom_call" | custom-call | flops 1610612736 | bytes 15204352 | tf_op jit(solution)/shard_map/pallas_call | solution.py:58
  114.2 3.9 %pad_maximum_fusion = f32[16,256,256]{2,1,0:T(8,128)} fusion(f32[16,256,128]{2,1,0:T(8,128)S(1)} %copy-done.1, f32[16,256,128]{2,1,0:T(8,128)} %shard_map.96), kind=kLoop, calls=%fused_computation.3 | loop fusion | flops 1048576 | bytes 8388608 | tf_op jit(solution)/shard_map/concatenate | solution.py:120
  118.2 0.8 fusion.3
  118.9 0.8 fusion.6
  119.8 2.7 %fusion.1 = (bf16[4096,256]{1,0:T(8,128)(2,1)S(1)}, bf16[4096,256]{1,0:T(8,128)(2,1)S(1)}) fusion(f32[16,256,256]{2,1,0:T(8,128)} %pad_maximum_fusion), kind=kLoop, calls=%fused_computation.6 | loop fusion | flops 4194304 | bytes 8388608 | tf_op jit(solution)/shard_map/convert_element_type | solution.py:86
  122.5 0.7 fusion.9
  123.2 0.7 fusion
  124.0 33.9 %all_to_all.41 = bf16[16,272,128]{2,1,0:T(8,128)(2,1)S(1)} all-to-all(bf16[16,272,128]{2,1,0:T(8,128)(2,1)S(1)} %pad_maximum_fusion.1), channel_id=1, replica_groups=mesh['row'=16,'col'=8] {'row'}, dimensions={0} | all-to-all | bytes 2228224 | tf_op jit(solution)/shard_map/all_to_all | solution.py:125
  157.9 0.2 convert_reduce_fusion
  158.1 12.4 %all_to_all.42 = f32[8,16,128]{2,1,0:T(8,128)S(1)} all-to-all(f32[8,16,128]{2,1,0:T(8,128)S(1)} %broadcast_in_dim.13), channel_id=1, replica_groups=mesh['row'=16,'col'=8] {'col'}, dimensions={0} | all-to-all | bytes 131072 | tf_op jit(solution)/shard_map/all_to_all | solution.py:81
  170.5 0.7 broadcast_in_dim.14
  171.2 5.1 %all-to-all-start.7 = ((f32[16,16,128]{2,1,0:T(8,128)}), f32[16,16,128]{2,1,0:T(8,128)S(1)}, u32[]{:S(2)}, u32[]{:S(2)}) async-start(f32[16,16,128]{2,1,0:T(8,128)} %broadcast_in_dim.14), calls=%async_computation.7 | async-start | bytes 262144 | tf_op jit(solution)/shard_map/all_to_all | solution.py:81
  176.3 0.7 pad_maximum_fusion.2
  177.0 0.6 slice.22
  177.6 4.8 %all-to-all-done.7 = f32[16,16,128]{2,1,0:T(8,128)S(1)} async-done(((f32[16,16,128]{2,1,0:T(8,128)}), f32[16,16,128]{2,1,0:T(8,128)S(1)}, u32[]{:S(2)}, u32[]{:S(2)}) %all-to-all-start.7) | async-done | bytes 131104 | tf_op jit(solution)/shard_map/all_to_all | solution.py:81
  182.5 0.7 div.21
  (20 shorter events, 0.6 us)
Async XLA Ops:
  0.6 25.1 %copy-start = (bf16[128,256]{1,0:T(8,128)(2,1)S(1)}, bf16[128,256]{1,0:T(8,128)(2,1)}, u32[]{:S(2)}) copy-start(bf16[128,256]{1,0:T(8,128)(2,1)} %param.8) | copy-start | bytes 196612
  2.7 23.1 %all-to-all-start = ((bf16[16,256,128]{2,1,0:T(8,128)(2,1)}), bf16[16,256,128]{2,1,0:T(8,128)(2,1)S(1)}, u32[]{:S(2)}, u32[]{:S(2)}) async-start(bf16[16,256,128]{2,1,0:T(8,128)(2,1)} %broadcast_in_dim.10), calls=%async_computation | async-start | bytes 2097152 | tf_op jit(solution)/shard_map/all_to_all | solution.py:81
  37.8 21.9 %all-to-all-start.2 = ((bf16[8,256,128]{2,1,0:T(8,128)(2,1)}), bf16[8,256,128]{2,1,0:T(8,128)(2,1)S(1)}, u32[]{:S(2)}, u32[]{:S(2)}) async-start(bf16[8,256,128]{2,1,0:T(8,128)(2,1)} %convert_element_type.64), calls=%async_computation.2 | async-start | bytes 1048576 | tf_op jit(solution)/shard_map/all_to_all | solution.py:112
  57.6 22.2 %copy-start.3 = (bf16[256,256]{1,0:T(8,128)(2,1)S(1)}, bf16[256,256]{1,0:T(8,128)(2,1)}, u32[]{:S(2)}) copy-start(bf16[256,256]{1,0:T(8,128)(2,1)} %param.13) | copy-start | bytes 393220
  59.8 20.0 %all-to-all-start.1 = ((bf16[8,256,128]{2,1,0:T(8,128)(2,1)}), bf16[8,256,128]{2,1,0:T(8,128)(2,1)S(1)}, u32[]{:S(2)}, u32[]{:S(2)}) async-start(bf16[8,256,128]{2,1,0:T(8,128)(2,1)} %convert_element_type.61), calls=%async_computation.1 | async-start | bytes 1048576 | tf_op jit(solution)/shard_map/all_to_all | solution.py:112
  92.7 13.2 %all-to-all-start.3 = ((bf16[8,256,128]{2,1,0:T(8,128)(2,1)}), bf16[8,256,128]{2,1,0:T(8,128)(2,1)}, u32[]{:S(2)}, u32[]{:S(2)}) async-start(bf16[8,256,128]{2,1,0:T(8,128)(2,1)} %broadcast_in_dim.11), calls=%async_computation.3 | async-start | bytes 1048576 | tf_op jit(solution)/shard_map/all_to_all | solution.py:81
  105.2 9.1 %copy-start.1 = (f32[16,256,128]{2,1,0:T(8,128)S(1)}, f32[16,256,128]{2,1,0:T(8,128)}, u32[]{:S(2)}) copy-start(f32[16,256,128]{2,1,0:T(8,128)} %shard_map.97) | copy-start | bytes 6291460
  114.2 4.0 %copy-start.2 = (f32[16,256,128]{2,1,0:T(8,128)S(1)}, f32[16,256,128]{2,1,0:T(8,128)}, u32[]{:S(2)}) copy-start(f32[16,256,128]{2,1,0:T(8,128)} %shard_map.96) | copy-start | bytes 6291460
  171.2 11.3 %all-to-all-start.7 = ((f32[16,16,128]{2,1,0:T(8,128)}), f32[16,16,128]{2,1,0:T(8,128)S(1)}, u32[]{:S(2)}, u32[]{:S(2)}) async-start(f32[16,16,128]{2,1,0:T(8,128)} %broadcast_in_dim.14), calls=%async_computation.7 | async-start | bytes 262144 | tf_op jit(solution)/shard_map/all_to_all | solution.py:81

commit v6 on v3

--- a/solution.py
+++ b/solution.py
@@ -8,7 +8,7 @@
 from jax.experimental.pallas import tpu as pltpu
 from jax.sharding import PartitionSpec as P
 
-GROUP = 8
+GROUP = 16
 
 
 def silu_slope(value):
@@ -16,7 +16,7 @@
     return sig * (1.0 + value * (1.0 - sig))
 
 
-def _block_kernel(transposed, n_in, n_out, rows_ref, cols_ref, live_ref, a_ref, src_ref, out_ref):
+def _block_kernel(transposed, n_in, n_out, rows_ref, cols_ref, live_ref, a_ref, src_ref, result_ref, out_ref):
     g = pl.program_id(0)
     live = live_ref[0]
 
@@ -42,8 +42,12 @@
             keep = jnp.where(s < live, 1.0, 0.0).astype(jnp.float32)
             out_ref[placed] += product * keep
 
+    @pl.when(g == pl.num_programs(0) - 1)
+    def _():
+        result_ref[...] = out_ref[...].astype(result_ref.dtype)
 
-def block_product(adj_values, slot_rows, slot_cols, slot_live, source, count_out, transposed):
+
+def block_product(adj_values, slot_rows, slot_cols, slot_live, source, count_out, transposed, dtype):
     slots, size, _ = adj_values.shape
     n_in, _, width = source.shape
     steps = slots // GROUP
@@ -63,8 +67,9 @@
                 pl.BlockSpec((n_in, size, width), lambda g, r, c, l: (0, 0, 0)),
             ],
             out_specs=pl.BlockSpec((count_out, size, width), lambda g, r, c, l: (0, 0, 0)),
+            scratch_shapes=[pltpu.VMEM((count_out, size, width), jnp.float32)],
         ),
-        out_shape=jax.ShapeDtypeStruct((count_out, size, width), jnp.float32),
+        out_shape=jax.ShapeDtypeStruct((count_out, size, width), dtype),
         compiler_params=pltpu.CompilerParams(dimension_semantics=("arbitrary",)),
         cost_estimate=pl.CostEstimate(
             flops=2 * slots * size * size * width,
@@ -103,16 +108,16 @@
     projected = jnp.dot(feature_cols, weight, preferred_element_type=jnp.float32).astype(jnp.bfloat16)
     column_blocks = projected.reshape(tile_cols, size, width)
     partial_value = block_product(
-        adj_values, slot_rows, slot_cols, slot_live, column_blocks, tile_rows, False
+        adj_values, slot_rows, slot_cols, slot_live, column_blocks, tile_rows, False, jnp.bfloat16
     )
-    received = lax.all_to_all(partial_value.astype(jnp.bfloat16), "col", 0, 0, tiled=True)
+    received = lax.all_to_all(partial_value, "col", 0, 0, tiled=True)
     summed = received.astype(jnp.float32).sum(axis=0)
     output = jax.nn.silu(summed).astype(jnp.bfloat16)
     grad_summed = (cotangent.astype(jnp.float32) * silu_slope(summed)).astype(jnp.bfloat16)
     grad_range = gather_axis(grad_summed, "col", n_col)
     grad_blocks = grad_range.reshape(tile_rows, size, width)
     back = block_product(
-        adj_values, slot_rows, slot_cols, slot_live, grad_blocks, tile_cols, True
+        adj_values, slot_rows, slot_cols, slot_live, grad_blocks, tile_cols, True, jnp.float32
     ).reshape(tile_cols * size, width)
     feature_part = split_dot(back, weight, (((1,), (1,)), ((), ())))
     weight_part = split_dot(back, feature_cols, (((0,), (0,)), ((), ()))).T

time: 151 us -> 145 us (0.960)
  blocking collectives: 84 us -> 78.8 us
  other arithmetic: 7 us -> 5.29 us
    all_to_all x1, blocking collectives: 30.8 us -> 24.2 us  [body(): lax.all_to_all(payload.astype(jnp.bfloat16), 'row', 0, 0, tiled=True)]
    all_to_all x2, blocking collectives: 26.6 us -> 28.9 us  [gather_axis(): return lax.all_to_all(spread, axis, 0, 0, tiled=True)]
    convert_element_type x1 -> x0, other arithmetic: 1.7 us -> none  [body(): partial_value.astype(jnp.bfloat16)]
where the time goes in v6:
time: 145 us
  blocking collectives  78.8 us (54%)
  waiting for transfers between devices  20.6 us (14%)
  Pallas kernels  15.8 us (11%)
  starting transfers between devices  12.5 us (9%)
  other arithmetic  5.29 us (4%)
  local copies, waits for them, and re-layouts  5.17 us (4%)
  matrix products  4.98 us (3%)
    all_to_all x2, blocking collectives, gather_axis(): return lax.all_to_all(spread, axis, 0, 0, tiled=True)  28.9 us
    all_to_all x1, blocking collectives, body(): received = lax.all_to_all(partial_value, 'col', 0, 0, tiled=True)  25.7 us
    all_to_all x1, blocking collectives, body(): lax.all_to_all(payload.astype(jnp.bfloat16), 'row', 0, 0, tiled=True)  24.2 us
    all_to_all x2, waiting for transfers between devices, gather_axis(): return lax.all_to_all(spread, axis, 0, 0, tiled=True)  20.6 us
    pallas_call x2, Pallas kernels, block_product(): pl.pallas_call(kernel, grid_spec=pltpu.PrefetchScalarGridSpec(num_scalar_...  15.8 us
    all_to_all x2, starting transfers between devices, gather_axis(): return lax.all_to_all(spread, axis, 0, 0, tiled=True)  12.5 us
    convert_element_type x1, other arithmetic, split_dot(): low = (left - high.astype(jnp.float32)).astype(jnp.bfloat16)  4.13 us
  transfers between devices with their start and end apart: 2, of which 2 were waited for; matrix products, arithmetic and copies ran while one was open for 0% of the time, Pallas kernels for 0%

profile of v6, /device:TPU:1, one launch (start us, length us, event | category | flops | bytes accessed | tf_op | source)
XLA Modules:
  0.0 144.5 jit_solution(7083128965793540116)
XLA Ops:
  0.6 0.0 copy-start
  0.6 2.1 %broadcast_in_dim.8 = bf16[16,256,128]{2,1,0:T(8,128)(2,1)} broadcast(bf16[256,128]{1,0:T(8,128)(2,1)} %param.7), dimensions={1,2} | broadcast | bytes 1114112 | tf_op jit(solution)/shard_map/broadcast_in_dim | solution.py:83
  2.7 7.3 %all-to-all-start = ((bf16[16,256,128]{2,1,0:T(8,128)(2,1)}), bf16[16,256,128]{2,1,0:T(8,128)(2,1)S(1)}, u32[]{:S(2)}, u32[]{:S(2)}) async-start(bf16[16,256,128]{2,1,0:T(8,128)(2,1)} %broadcast_in_dim.8), calls=%async_computation | async-start | bytes 2097152 | tf_op jit(solution)/shard_map/all_to_all | solution.py:84
  10.7 15.1 %all-to-all-done = bf16[16,256,128]{2,1,0:T(8,128)(2,1)S(1)} async-done(((bf16[16,256,128]{2,1,0:T(8,128)(2,1)}), bf16[16,256,128]{2,1,0:T(8,128)(2,1)S(1)}, u32[]{:S(2)}, u32[]{:S(2)}) %all-to-all-start) | async-done | bytes 1048608 | tf_op jit(solution)/shard_map/all_to_all | solution.py:84
  25.8 0.0 copy-done
  25.8 2.0 %convolution_convert_fusion = bf16[4096,256]{1,0:T(8,128)(2,1)} fusion(bf16[4096,128]{1,0:T(8,128)(2,1)S(1)} %bitcast.29, bf16[128,256]{1,0:T(8,128)(2,1)S(1)} %copy-done), kind=kOutput, calls=%fused_computation | convolution fusion | flops 269484032 | bytes 3211264 | tf_op jit(solution)/shard_map/dot_general | solution.py:108
  27.8 7.5 %shard_map.94 = bf16[8,256,256]{2,1,0:T(8,128)(2,1)} custom-call(s32[96]{0:T(128)} %rows_ref.3, s32[96]{0:T(128)} %cols_ref.3, s32[1]{0:T(128)S(6)} %copy.20.live_ref, bf16[96,256,256]{2,1,0:T(8,128)(2,1)} %a_ref.3, bf16[16,256,256]{2,1,0:T(8,128)(2,1)} %bitcast.30), custom_call_target="tpu_custom_call" | custom-call | flops 3221225472 | bytes 16777216 | tf_op jit(solution)/shard_map/pallas_call | solution.py:60
  35.3 25.7 %all_to_all.30 = bf16[8,256,256]{2,1,0:T(8,128)(2,1)S(1)} all-to-all(bf16[8,256,256]{2,1,0:T(8,128)(2,1)} %shard_map.94), channel_id=1, replica_groups=mesh['row'=16,'col'=8] {'col'}, dimensions={0} | all-to-all | bytes 2097152 | tf_op jit(solution)/shard_map/all_to_all | solution.py:113
  61.0 0.1 convert_reduce_fusion.1
  61.1 0.0 copy-done.3
  61.1 0.8 multiply_convert_fusion
  61.9 0.1 broadcast_in_dim.9
  61.9 17.3 %all_to_all.31.src_ref = bf16[8,256,256]{2,1,0:T(8,128)(2,1)} all-to-all(bf16[8,256,256]{2,1,0:T(8,128)(2,1)S(1)} %broadcast_in_dim.9), channel_id=1, replica_groups=mesh['row'=16,'col'=8] {'col'}, dimensions={0} | all-to-all | bytes 2097152 | tf_op jit(solution)/shard_map/all_to_all | solution.py:84
  79.2 8.4 %shard_map.95 = f32[16,256,256]{2,1,0:T(8,128)} custom-call(s32[96]{0:T(128)} %rows_ref.3, s32[96]{0:T(128)} %cols_ref.3, s32[1]{0:T(128)S(6)} %copy.20.live_ref, bf16[96,256,256]{2,1,0:T(8,128)(2,1)} %a_ref.3, bf16[8,256,256]{2,1,0:T(8,128)(2,1)} %all_to_all.31.src_ref), custom_call_target="tpu_custom_call" | custom-call | flops 3221225472 | bytes 17825792 | tf_op jit(solution)/shard_map/pallas_call | solution.py:60
  87.6 4.1 %fusion.1 = (bf16[4096,256]{1,0:T(8,128)(2,1)}, bf16[4096,256]{1,0:T(8,128)(2,1)S(1)}) fusion(f32[16,256,256]{2,1,0:T(8,128)} %shard_map.95), kind=kLoop, calls=%fused_computation.5 | loop fusion | flops 4194304 | bytes 8388608 | tf_op jit(solution)/shard_map/convert_element_type | solution.py:89
  91.8 0.0 copy-done.1
  91.8 0.8 fusion.3
  92.5 0.8 fusion.6
  93.3 0.1 copy.17
  93.5 0.0 copy-start.2
  93.5 0.7 fusion.9
  94.2 0.9 copy-done.2
  95.1 0.7 fusion
  95.8 0.1 pad_maximum_fusion
  95.9 24.2 %all_to_all.32 = bf16[16,272,128]{2,1,0:T(8,128)(2,1)S(1)} all-to-all(bf16[16,272,128]{2,1,0:T(8,128)(2,1)S(1)} %pad_maximum_fusion), channel_id=1, replica_groups=mesh['row'=16,'col'=8] {'row'}, dimensions={0} | all-to-all | bytes 2228224 | tf_op jit(solution)/shard_map/all_to_all | solution.py:126
  120.1 0.2 convert_reduce_fusion
  120.2 11.6 %all_to_all.33 = f32[8,16,128]{2,1,0:T(8,128)S(1)} all-to-all(f32[8,16,128]{2,1,0:T(8,128)S(1)} %broadcast_in_dim.10), channel_id=1, replica_groups=mesh['row'=16,'col'=8] {'col'}, dimensions={0} | all-to-all | bytes 131072 | tf_op jit(solution)/shard_map/all_to_all | solution.py:84
  131.9 0.7 broadcast_in_dim.11
  132.6 5.1 %all-to-all-start.5 = ((f32[16,16,128]{2,1,0:T(8,128)}), f32[16,16,128]{2,1,0:T(8,128)S(1)}, u32[]{:S(2)}, u32[]{:S(2)}) async-start(f32[16,16,128]{2,1,0:T(8,128)} %broadcast_in_dim.11), calls=%async_computation.5 | async-start | bytes 262144 | tf_op jit(solution)/shard_map/all_to_all | solution.py:84
  137.7 0.6 slice.12
  138.3 5.5 %all-to-all-done.5 = f32[16,16,128]{2,1,0:T(8,128)S(1)} async-done(((f32[16,16,128]{2,1,0:T(8,128)}), f32[16,16,128]{2,1,0:T(8,128)S(1)}, u32[]{:S(2)}, u32[]{:S(2)}) %all-to-all-start.5) | async-done | bytes 131104 | tf_op jit(solution)/shard_map/all_to_all | solution.py:84
  143.8 0.7 div.16
  (7 shorter events, 0.1 us)
Async XLA Ops:
  0.6 25.2 %copy-start = (bf16[128,256]{1,0:T(8,128)(2,1)S(1)}, bf16[128,256]{1,0:T(8,128)(2,1)}, u32[]{:S(2)}) copy-start(bf16[128,256]{1,0:T(8,128)(2,1)} %param.8) | copy-start | bytes 196612
  2.7 23.1 %all-to-all-start = ((bf16[16,256,128]{2,1,0:T(8,128)(2,1)}), bf16[16,256,128]{2,1,0:T(8,128)(2,1)S(1)}, u32[]{:S(2)}, u32[]{:S(2)}) async-start(bf16[16,256,128]{2,1,0:T(8,128)(2,1)} %broadcast_in_dim.8), calls=%async_computation | async-start | bytes 2097152 | tf_op jit(solution)/shard_map/all_to_all | solution.py:84
  35.3 25.8 %copy-start.3 = (bf16[256,256]{1,0:T(8,128)(2,1)S(1)}, bf16[256,256]{1,0:T(8,128)(2,1)}, u32[]{:S(2)}) copy-start(bf16[256,256]{1,0:T(8,128)(2,1)} %param.13) | copy-start | bytes 393220
  87.6 4.1 %copy-start.1 = (f32[16,256,256]{2,1,0:T(8,128)S(1)}, f32[16,256,256]{2,1,0:T(8,128)}, u32[]{:S(2)}) copy-start(f32[16,256,256]{2,1,0:T(8,128)} %shard_map.95) | copy-start | bytes 12582916
  93.5 1.6 %copy-start.2 = (bf16[4096,256]{1,0:T(8,128)(2,1)S(1)}, bf16[4096,256]{1,0:T(8,128)(2,1)}, u32[]{:S(2)}) copy-start(bf16[4096,256]{1,0:T(8,128)(2,1)} %get-tuple-element.3) | copy-start | bytes 6291460
  132.6 11.3 %all-to-all-start.5 = ((f32[16,16,128]{2,1,0:T(8,128)}), f32[16,16,128]{2,1,0:T(8,128)S(1)}, u32[]{:S(2)}, u32[]{:S(2)}) async-start(f32[16,16,128]{2,1,0:T(8,128)} %broadcast_in_dim.11), calls=%async_computation.5 | async-start | bytes 262144 | tf_op jit(solution)/shard_map/all_to_all | solution.py:84

commit v7 on v6

--- a/solution.py
+++ b/solution.py
@@ -8,7 +8,7 @@
 from jax.experimental.pallas import tpu as pltpu
 from jax.sharding import PartitionSpec as P
 
-GROUP = 16
+GROUP = 32
 
 
 def silu_slope(value):
@@ -16,7 +16,8 @@
     return sig * (1.0 + value * (1.0 - sig))
 
 
-def _block_kernel(transposed, n_in, n_out, rows_ref, cols_ref, live_ref, a_ref, src_ref, result_ref, out_ref):
+def _block_kernel(transposed, n_in, n_out, rows_ref, cols_ref, live_ref, a_ref, src_ref, *refs):
+    results, out_ref = refs[:-1], refs[-1]
     g = pl.program_id(0)
     live = live_ref[0]
 
@@ -44,10 +45,16 @@
 
     @pl.when(g == pl.num_programs(0) - 1)
     def _():
-        result_ref[...] = out_ref[...].astype(result_ref.dtype)
+        total = out_ref[...]
+        if len(results) == 1:
+            results[0][...] = total.astype(results[0].dtype)
+        else:
+            high = total.astype(jnp.bfloat16)
+            results[0][...] = high
+            results[1][...] = (total - high.astype(jnp.float32)).astype(jnp.bfloat16)
 
 
-def block_product(adj_values, slot_rows, slot_cols, slot_live, source, count_out, transposed, dtype):
+def block_product(adj_values, slot_rows, slot_cols, slot_live, source, count_out, transposed, dtype, outs=1):
     slots, size, _ = adj_values.shape
     n_in, _, width = source.shape
     steps = slots // GROUP
@@ -66,10 +73,10 @@
                 pl.BlockSpec((GROUP, size, size), a_map),
                 pl.BlockSpec((n_in, size, width), lambda g, r, c, l: (0, 0, 0)),
             ],
-            out_specs=pl.BlockSpec((count_out, size, width), lambda g, r, c, l: (0, 0, 0)),
+            out_specs=[pl.BlockSpec((count_out, size, width), lambda g, r, c, l: (0, 0, 0))] * outs,
             scratch_shapes=[pltpu.VMEM((count_out, size, width), jnp.float32)],
         ),
-        out_shape=jax.ShapeDtypeStruct((count_out, size, width), dtype),
+        out_shape=[jax.ShapeDtypeStruct((count_out, size, width), dtype)] * outs,
         compiler_params=pltpu.CompilerParams(dimension_semantics=("arbitrary",)),
         cost_estimate=pl.CostEstimate(
             flops=2 * slots * size * size * width,
@@ -84,9 +91,7 @@
     return lax.all_to_all(spread, axis, 0, 0, tiled=True)
 
 
-def split_dot(left, right, dims):
-    high = left.astype(jnp.bfloat16)
-    low = (left - high.astype(jnp.float32)).astype(jnp.bfloat16)
+def pair_dot(high, low, right, dims):
     first = lax.dot_general(high, right, dims, preferred_element_type=jnp.float32)
     second = lax.dot_general(low, right, dims, preferred_element_type=jnp.float32)
     return first + second
@@ -107,7 +112,7 @@
     feature_cols = gather_axis(features, "row", n_row).reshape(own_rows * n_row, fin)
     projected = jnp.dot(feature_cols, weight, preferred_element_type=jnp.float32).astype(jnp.bfloat16)
     column_blocks = projected.reshape(tile_cols, size, width)
-    partial_value = block_product(
+    (partial_value,) = block_product(
         adj_values, slot_rows, slot_cols, slot_live, column_blocks, tile_rows, False, jnp.bfloat16
     )
     received = lax.all_to_all(partial_value, "col", 0, 0, tiled=True)
@@ -116,11 +121,13 @@
     grad_summed = (cotangent.astype(jnp.float32) * silu_slope(summed)).astype(jnp.bfloat16)
     grad_range = gather_axis(grad_summed, "col", n_col)
     grad_blocks = grad_range.reshape(tile_rows, size, width)
-    back = block_product(
-        adj_values, slot_rows, slot_cols, slot_live, grad_blocks, tile_cols, True, jnp.float32
-    ).reshape(tile_cols * size, width)
-    feature_part = split_dot(back, weight, (((1,), (1,)), ((), ())))
-    weight_part = split_dot(back, feature_cols, (((0,), (0,)), ((), ()))).T
+    back_high, back_low = block_product(
+        adj_values, slot_rows, slot_cols, slot_live, grad_blocks, tile_cols, True, jnp.bfloat16, 2
+    )
+    back_high = back_high.reshape(tile_cols * size, width)
+    back_low = back_low.reshape(tile_cols * size, width)
+    feature_part = pair_dot(back_high, back_low, weight, (((1,), (1,)), ((), ())))
+    weight_part = pair_dot(back_high, back_low, feature_cols, (((0,), (0,)), ((), ()))).T
     pieces = weight_part.reshape(tile_cols, fin * width // (tile_cols * fin), fin)
     payload = jnp.concatenate([feature_part.reshape(tile_cols, size, fin), pieces], axis=1)
     exchanged = lax.all_to_all(payload.astype(jnp.bfloat16), "row", 0, 0, tiled=True)

time: 145 us -> 142 us (0.979)
  other arithmetic: 5.29 us -> 1.16 us
  matrix products: 4.98 us -> 6.66 us
  blocking collectives: 78.8 us -> 77.3 us
    convert_element_type x1 -> x0, other arithmetic: 4.13 us -> none  [split_dot(): low = (left - high.astype(jnp.float32)).astype(jnp.bfloat16)]
    dot_general x4, matrix products: 2.95 us -> 4.63 us  [the longest x2 3.19 us: pair_dot(): lax.dot_general(low, right, dims, preferred_element_type=jnp.float32)]
    all_to_all x1, blocking collectives: 24.2 us -> 22.7 us  [body(): lax.all_to_all(payload.astype(jnp.bfloat16), 'row', 0, 0, tiled=True)]
where the time goes in v7:
time: 142 us; the launch traced here: 141 us
  blocking collectives  77.3 us (54%)
  waiting for transfers between devices  20.6 us (15%)
  Pallas kernels  16.7 us (12%)
  starting transfers between devices  12.5 us (9%)
  matrix products  6.66 us (5%)
  local copies, waits for them, and re-layouts  5.16 us (4%)
    all_to_all x2, blocking collectives, gather_axis(): return lax.all_to_all(spread, axis, 0, 0, tiled=True)  28.9 us
    all_to_all x1, blocking collectives, body(): received = lax.all_to_all(partial_value, 'col', 0, 0, tiled=True)  25.8 us
    all_to_all x1, blocking collectives, body(): lax.all_to_all(payload.astype(jnp.bfloat16), 'row', 0, 0, tiled=True)  22.7 us
    all_to_all x2, waiting for transfers between devices, gather_axis(): return lax.all_to_all(spread, axis, 0, 0, tiled=True)  20.6 us
    pallas_call x2, Pallas kernels, block_product(): pl.pallas_call(kernel, grid_spec=pltpu.PrefetchScalarGridSpec(num_scalar_...  16.7 us
    all_to_all x2, starting transfers between devices, gather_axis(): return lax.all_to_all(spread, axis, 0, 0, tiled=True)  12.5 us
    dot_general x2, matrix products, pair_dot(): lax.dot_general(low, right, dims, preferred_element_type=jnp.float32)  3.19 us
  transfers between devices with their start and end apart: 2, of which 2 were waited for; matrix products, arithmetic and copies ran while one was open for 0% of the time, Pallas kernels for 0%

profile of v7, /device:TPU:1, one launch (start us, length us, event | category | flops | bytes accessed | tf_op | source)
XLA Modules:
  0.0 141.4 jit_solution(10150041255775919939)
XLA Ops:
  0.6 0.0 copy-start
  0.6 2.1 %broadcast_in_dim.8 = bf16[16,256,128]{2,1,0:T(8,128)(2,1)} broadcast(bf16[256,128]{1,0:T(8,128)(2,1)} %param.7), dimensions={1,2} | broadcast | bytes 1114112 | tf_op jit(solution)/shard_map/broadcast_in_dim | solution.py:90
  2.7 7.3 %all-to-all-start = ((bf16[16,256,128]{2,1,0:T(8,128)(2,1)}), bf16[16,256,128]{2,1,0:T(8,128)(2,1)S(1)}, u32[]{:S(2)}, u32[]{:S(2)}) async-start(bf16[16,256,128]{2,1,0:T(8,128)(2,1)} %broadcast_in_dim.8), calls=%async_computation | async-start | bytes 2097152 | tf_op jit(solution)/shard_map/all_to_all | solution.py:91
  10.7 15.1 %all-to-all-done = bf16[16,256,128]{2,1,0:T(8,128)(2,1)S(1)} async-done(((bf16[16,256,128]{2,1,0:T(8,128)(2,1)}), bf16[16,256,128]{2,1,0:T(8,128)(2,1)S(1)}, u32[]{:S(2)}, u32[]{:S(2)}) %all-to-all-start) | async-done | bytes 1048608 | tf_op jit(solution)/shard_map/all_to_all | solution.py:91
  25.8 0.0 copy-done
  25.8 2.0 %convolution_convert_fusion = bf16[4096,256]{1,0:T(8,128)(2,1)} fusion(bf16[4096,128]{1,0:T(8,128)(2,1)S(1)} %bitcast.28, bf16[128,256]{1,0:T(8,128)(2,1)S(1)} %copy-done), kind=kOutput, calls=%fused_computation | convolution fusion | flops 269484032 | bytes 3211264 | tf_op jit(solution)/shard_map/dot_general | solution.py:113
  27.8 7.7 %shard_map.94 = bf16[8,256,256]{2,1,0:T(8,128)(2,1)} custom-call(s32[96]{0:T(128)} %rows_ref.3, s32[96]{0:T(128)} %cols_ref.3, s32[1]{0:T(128)S(6)} %copy.20.live_ref, bf16[96,256,256]{2,1,0:T(8,128)(2,1)} %a_ref.3, bf16[16,256,256]{2,1,0:T(8,128)(2,1)} %bitcast.29), custom_call_target="tpu_custom_call" | custom-call | flops 3221225472 | bytes 16777216 | tf_op jit(solution)/shard_map/pallas_call | solution.py:67
  35.5 0.0 copy-start.3
  35.5 25.8 %all_to_all.30 = bf16[8,256,256]{2,1,0:T(8,128)(2,1)S(1)} all-to-all(bf16[8,256,256]{2,1,0:T(8,128)(2,1)} %shard_map.94), channel_id=1, replica_groups=mesh['row'=16,'col'=8] {'col'}, dimensions={0} | all-to-all | bytes 2097152 | tf_op jit(solution)/shard_map/all_to_all | solution.py:118
  61.3 0.1 convert_reduce_fusion.1
  61.4 0.0 copy-done.3
  61.4 0.8 multiply_convert_fusion
  62.2 0.1 broadcast_in_dim.9
  62.3 19.6 %all_to_all.31.src_ref = bf16[8,256,256]{2,1,0:T(8,128)(2,1)} all-to-all(bf16[8,256,256]{2,1,0:T(8,128)(2,1)S(1)} %broadcast_in_dim.9), channel_id=1, replica_groups=mesh['row'=16,'col'=8] {'col'}, dimensions={0} | all-to-all | bytes 2097152 | tf_op jit(solution)/shard_map/all_to_all | solution.py:91
  81.8 9.0 %shard_map.95 = (bf16[16,256,256]{2,1,0:T(8,128)(2,1)}, bf16[16,256,256]{2,1,0:T(8,128)(2,1)}) custom-call(s32[96]{0:T(128)} %rows_ref.3, s32[96]{0:T(128)} %cols_ref.3, s32[1]{0:T(128)S(6)} %copy.20.live_ref, bf16[96,256,256]{2,1,0:T(8,128)(2,1)} %a_ref.3, bf16[8,256,256]{2,1,0:T(8,128)(2,1)} %all_to_all.31.src_ref), custom_call_target="tpu_custom_call" | custom-call | flops 3221225472 | bytes 17825792 | tf_op jit(solution)/shard_map/pallas_call | solution.py:67
  90.8 2.5 %convolution_bitcast_fusion = f32[256,128]{1,0:T(8,128)S(1)} fusion(bf16[16,256,256]{2,1,0:T(8,128)(2,1)} %get-tuple-element.6, bf16[16,256,128]{2,1,0:T(8,128)(2,1)S(1)} %all-to-all-done), kind=kOutput, calls=%fused_computation.5 | convolution fusion | flops 268435456 | bytes 3276800 | tf_op jit(solution)/shard_map/dot_general | solution.py:96
  93.3 0.0 copy-done.1
  93.3 0.8 fusion.3
  94.1 0.1 copy.17
  94.2 0.0 copy-start.2
  94.2 0.7 fusion.4
  94.9 0.9 copy-done.2
  95.8 0.7 fusion
  96.5 0.1 pad_maximum_fusion
  96.6 22.7 %all_to_all.32 = bf16[16,272,128]{2,1,0:T(8,128)(2,1)S(1)} all-to-all(bf16[16,272,128]{2,1,0:T(8,128)(2,1)S(1)} %pad_maximum_fusion), channel_id=1, replica_groups=mesh['row'=16,'col'=8] {'row'}, dimensions={0} | all-to-all | bytes 2228224 | tf_op jit(solution)/shard_map/all_to_all | solution.py:133
  119.3 0.2 convert_reduce_fusion
  119.5 9.3 %all_to_all.33 = f32[8,16,128]{2,1,0:T(8,128)S(1)} all-to-all(f32[8,16,128]{2,1,0:T(8,128)S(1)} %broadcast_in_dim.10), channel_id=1, replica_groups=mesh['row'=16,'col'=8] {'col'}, dimensions={0} | all-to-all | bytes 131072 | tf_op jit(solution)/shard_map/all_to_all | solution.py:91
  128.8 0.7 broadcast_in_dim.11
  129.5 5.1 %all-to-all-start.5 = ((f32[16,16,128]{2,1,0:T(8,128)}), f32[16,16,128]{2,1,0:T(8,128)S(1)}, u32[]{:S(2)}, u32[]{:S(2)}) async-start(f32[16,16,128]{2,1,0:T(8,128)} %broadcast_in_dim.11), calls=%async_computation.5 | async-start | bytes 262144 | tf_op jit(solution)/shard_map/all_to_all | solution.py:91
  134.6 0.6 slice.12
  135.2 5.5 %all-to-all-done.5 = f32[16,16,128]{2,1,0:T(8,128)S(1)} async-done(((f32[16,16,128]{2,1,0:T(8,128)}), f32[16,16,128]{2,1,0:T(8,128)S(1)}, u32[]{:S(2)}, u32[]{:S(2)}) %all-to-all-start.5) | async-done | bytes 131104 | tf_op jit(solution)/shard_map/all_to_all | solution.py:91
  140.7 0.7 div.16
  (6 shorter events, 0.1 us)
Async XLA Ops:
  0.6 25.2 %copy-start = (bf16[128,256]{1,0:T(8,128)(2,1)S(1)}, bf16[128,256]{1,0:T(8,128)(2,1)}, u32[]{:S(2)}) copy-start(bf16[128,256]{1,0:T(8,128)(2,1)} %param.8) | copy-start | bytes 196612
  2.7 23.1 %all-to-all-start = ((bf16[16,256,128]{2,1,0:T(8,128)(2,1)}), bf16[16,256,128]{2,1,0:T(8,128)(2,1)S(1)}, u32[]{:S(2)}, u32[]{:S(2)}) async-start(bf16[16,256,128]{2,1,0:T(8,128)(2,1)} %broadcast_in_dim.8), calls=%async_computation | async-start | bytes 2097152 | tf_op jit(solution)/shard_map/all_to_all | solution.py:91
  35.5 25.9 %copy-start.3 = (bf16[256,256]{1,0:T(8,128)(2,1)S(1)}, bf16[256,256]{1,0:T(8,128)(2,1)}, u32[]{:S(2)}) copy-start(bf16[256,256]{1,0:T(8,128)(2,1)} %param.13) | copy-start | bytes 393220
  90.8 2.5 %copy-start.1 = (bf16[16,256,256]{2,1,0:T(8,128)(2,1)S(1)}, bf16[16,256,256]{2,1,0:T(8,128)(2,1)}, u32[]{:S(2)}) copy-start(bf16[16,256,256]{2,1,0:T(8,128)(2,1)} %get-tuple-element.5) | copy-start | bytes 6291460
  94.2 1.6 %copy-start.2 = (bf16[16,256,256]{2,1,0:T(8,128)(2,1)S(1)}, bf16[16,256,256]{2,1,0:T(8,128)(2,1)}, u32[]{:S(2)}) copy-start(bf16[16,256,256]{2,1,0:T(8,128)(2,1)} %get-tuple-element.6) | copy-start | bytes 6291460
  129.5 11.3 %all-to-all-start.5 = ((f32[16,16,128]{2,1,0:T(8,128)}), f32[16,16,128]{2,1,0:T(8,128)S(1)}, u32[]{:S(2)}, u32[]{:S(2)}) async-start(f32[16,16,128]{2,1,0:T(8,128)} %broadcast_in_dim.11), calls=%async_computation.5 | async-start | bytes 262144 | tf_op jit(solution)/shard_map/all_to_all | solution.py:91

commit v8 on v7

--- a/solution.py
+++ b/solution.py
@@ -25,8 +25,7 @@
     def _():
         out_ref[...] = jnp.zeros_like(out_ref)
 
-    @pl.when(g * GROUP < live)
-    def _():
+    def accumulate(masked):
         for k in range(GROUP):
             s = g * GROUP + k
             if transposed:
@@ -40,8 +39,17 @@
                 taken = jnp.clip(cols_ref[s], 0, n_in - 1)
                 placed = jnp.clip(rows_ref[s], 0, n_out - 1)
                 product = jnp.dot(a_ref[k], src_ref[taken], preferred_element_type=jnp.float32)
-            keep = jnp.where(s < live, 1.0, 0.0).astype(jnp.float32)
-            out_ref[placed] += product * keep
+            if masked:
+                product = product * jnp.where(s < live, 1.0, 0.0).astype(jnp.float32)
+            out_ref[placed] += product
+
+    @pl.when((g + 1) * GROUP <= live)
+    def _():
+        accumulate(False)
+
+    @pl.when((g * GROUP < live) & ((g + 1) * GROUP > live))
+    def _():
+        accumulate(True)
 
     @pl.when(g == pl.num_programs(0) - 1)
     def _():

time: 142 us -> 142 us (level)
  Pallas kernels: 16.7 us -> 13.9 us
  blocking collectives: 77.3 us -> 79.8 us
    all_to_all x1, blocking collectives: 22.7 us -> 29.3 us  [body(): lax.all_to_all(payload.astype(jnp.bfloat16), 'row', 0, 0, tiled=True)]
    pallas_call x2, Pallas kernels: 16.7 us -> 13.9 us  [block_product(): pl.pallas_call(kernel, grid_spec=pltpu.PrefetchScalarGridSpec(num_scalar_...]
    all_to_all x1, blocking collectives: 25.8 us -> 23.6 us  [body(): received = lax.all_to_all(partial_value, 'col', 0, 0, tiled=True)]
    all_to_all x2, blocking collectives: 28.9 us -> 26.9 us  [gather_axis(): return lax.all_to_all(spread, axis, 0, 0, tiled=True)]
where the time goes in v8:
time: 142 us; the launch traced here: 141 us
  blocking collectives  79.8 us (56%)
  waiting for transfers between devices  20.6 us (15%)
  Pallas kernels  13.9 us (10%)
  starting transfers between devices  12.5 us (9%)
  matrix products  6.67 us (5%)
  local copies, waits for them, and re-layouts  5.16 us (4%)
    all_to_all x1, blocking collectives, body(): lax.all_to_all(payload.astype(jnp.bfloat16), 'row', 0, 0, tiled=True)  29.3 us
    all_to_all x2, blocking collectives, gather_axis(): return lax.all_to_all(spread, axis, 0, 0, tiled=True)  26.9 us
    all_to_all x1, blocking collectives, body(): received = lax.all_to_all(partial_value, 'col', 0, 0, tiled=True)  23.6 us
    all_to_all x2, waiting for transfers between devices, gather_axis(): return lax.all_to_all(spread, axis, 0, 0, tiled=True)  20.6 us
    pallas_call x2, Pallas kernels, block_product(): pl.pallas_call(kernel, grid_spec=pltpu.PrefetchScalarGridSpec(num_scalar_...  13.9 us
    all_to_all x2, starting transfers between devices, gather_axis(): return lax.all_to_all(spread, axis, 0, 0, tiled=True)  12.5 us
    dot_general x2, matrix products, pair_dot(): lax.dot_general(low, right, dims, preferred_element_type=jnp.float32)  3.2 us
  transfers between devices with their start and end apart: 2, of which 2 were waited for; matrix products, arithmetic and copies ran while one was open for 0% of the time, Pallas kernels for 0%

profile of v8, /device:TPU:1, one launch (start us, length us, event | category | flops | bytes accessed | tf_op | source)
XLA Modules:
  0.0 141.1 jit_solution(5746709073359711332)
XLA Ops:
  0.6 0.0 copy-start
  0.6 2.1 %broadcast_in_dim.8 = bf16[16,256,128]{2,1,0:T(8,128)(2,1)} broadcast(bf16[256,128]{1,0:T(8,128)(2,1)} %param.7), dimensions={1,2} | broadcast | bytes 1114112 | tf_op jit(solution)/shard_map/broadcast_in_dim | solution.py:98
  2.7 7.3 %all-to-all-start = ((bf16[16,256,128]{2,1,0:T(8,128)(2,1)}), bf16[16,256,128]{2,1,0:T(8,128)(2,1)S(1)}, u32[]{:S(2)}, u32[]{:S(2)}) async-start(bf16[16,256,128]{2,1,0:T(8,128)(2,1)} %broadcast_in_dim.8), calls=%async_computation | async-start | bytes 2097152 | tf_op jit(solution)/shard_map/all_to_all | solution.py:99
  10.7 15.1 %all-to-all-done = bf16[16,256,128]{2,1,0:T(8,128)(2,1)S(1)} async-done(((bf16[16,256,128]{2,1,0:T(8,128)(2,1)}), bf16[16,256,128]{2,1,0:T(8,128)(2,1)S(1)}, u32[]{:S(2)}, u32[]{:S(2)}) %all-to-all-start) | async-done | bytes 1048608 | tf_op jit(solution)/shard_map/all_to_all | solution.py:99
  25.8 0.0 copy-done
  25.8 2.0 %convolution_convert_fusion = bf16[4096,256]{1,0:T(8,128)(2,1)} fusion(bf16[4096,128]{1,0:T(8,128)(2,1)S(1)} %bitcast.28, bf16[128,256]{1,0:T(8,128)(2,1)S(1)} %copy-done), kind=kOutput, calls=%fused_computation | convolution fusion | flops 269484032 | bytes 3211264 | tf_op jit(solution)/shard_map/dot_general | solution.py:121
  27.8 6.3 %shard_map.94 = bf16[8,256,256]{2,1,0:T(8,128)(2,1)} custom-call(s32[96]{0:T(128)} %rows_ref.3, s32[96]{0:T(128)} %cols_ref.3, s32[1]{0:T(128)S(6)} %copy.20.live_ref, bf16[96,256,256]{2,1,0:T(8,128)(2,1)} %a_ref.3, bf16[16,256,256]{2,1,0:T(8,128)(2,1)} %bitcast.29), custom_call_target="tpu_custom_call" | custom-call | flops 3221225472 | bytes 16777216 | tf_op jit(solution)/shard_map/pallas_call | solution.py:75
  34.1 0.0 copy-start.3
  34.1 23.6 %all_to_all.30 = bf16[8,256,256]{2,1,0:T(8,128)(2,1)S(1)} all-to-all(bf16[8,256,256]{2,1,0:T(8,128)(2,1)} %shard_map.94), channel_id=1, replica_groups=mesh['row'=16,'col'=8] {'col'}, dimensions={0} | all-to-all | bytes 2097152 | tf_op jit(solution)/shard_map/all_to_all | solution.py:126
  57.7 0.1 convert_reduce_fusion.1
  57.9 0.0 copy-done.3
  57.9 0.8 multiply_convert_fusion
  58.6 0.1 broadcast_in_dim.9
  58.7 17.1 %all_to_all.31.src_ref = bf16[8,256,256]{2,1,0:T(8,128)(2,1)} all-to-all(bf16[8,256,256]{2,1,0:T(8,128)(2,1)S(1)} %broadcast_in_dim.9), channel_id=1, replica_groups=mesh['row'=16,'col'=8] {'col'}, dimensions={0} | all-to-all | bytes 2097152 | tf_op jit(solution)/shard_map/all_to_all | solution.py:99
  75.8 7.6 %shard_map.95 = (bf16[16,256,256]{2,1,0:T(8,128)(2,1)}, bf16[16,256,256]{2,1,0:T(8,128)(2,1)}) custom-call(s32[96]{0:T(128)} %rows_ref.3, s32[96]{0:T(128)} %cols_ref.3, s32[1]{0:T(128)S(6)} %copy.20.live_ref, bf16[96,256,256]{2,1,0:T(8,128)(2,1)} %a_ref.3, bf16[8,256,256]{2,1,0:T(8,128)(2,1)} %all_to_all.31.src_ref), custom_call_target="tpu_custom_call" | custom-call | flops 3221225472 | bytes 17825792 | tf_op jit(solution)/shard_map/pallas_call | solution.py:75
  83.4 2.5 %convolution_bitcast_fusion = f32[256,128]{1,0:T(8,128)S(1)} fusion(bf16[16,256,256]{2,1,0:T(8,128)(2,1)} %get-tuple-element.6, bf16[16,256,128]{2,1,0:T(8,128)(2,1)S(1)} %all-to-all-done), kind=kOutput, calls=%fused_computation.5 | convolution fusion | flops 268435456 | bytes 3276800 | tf_op jit(solution)/shard_map/dot_general | solution.py:104
  85.9 0.0 copy-done.1
  85.9 0.8 fusion.3
  86.6 0.1 copy.17
  86.8 0.0 copy-start.2
  86.8 0.7 fusion.4
  87.5 0.9 copy-done.2
  88.4 0.7 fusion
  89.1 0.1 pad_maximum_fusion
  89.2 29.3 %all_to_all.32 = bf16[16,272,128]{2,1,0:T(8,128)(2,1)S(1)} all-to-all(bf16[16,272,128]{2,1,0:T(8,128)(2,1)S(1)} %pad_maximum_fusion), channel_id=1, replica_groups=mesh['row'=16,'col'=8] {'row'}, dimensions={0} | all-to-all | bytes 2228224 | tf_op jit(solution)/shard_map/all_to_all | solution.py:141
  118.5 0.2 convert_reduce_fusion
  118.7 9.8 %all_to_all.33 = f32[8,16,128]{2,1,0:T(8,128)S(1)} all-to-all(f32[8,16,128]{2,1,0:T(8,128)S(1)} %broadcast_in_dim.10), channel_id=1, replica_groups=mesh['row'=16,'col'=8] {'col'}, dimensions={0} | all-to-all | bytes 131072 | tf_op jit(solution)/shard_map/all_to_all | solution.py:99
  128.5 0.7 broadcast_in_dim.11
  129.1 5.1 %all-to-all-start.5 = ((f32[16,16,128]{2,1,0:T(8,128)}), f32[16,16,128]{2,1,0:T(8,128)S(1)}, u32[]{:S(2)}, u32[]{:S(2)}) async-start(f32[16,16,128]{2,1,0:T(8,128)} %broadcast_in_dim.11), calls=%async_computation.5 | async-start | bytes 262144 | tf_op jit(solution)/shard_map/all_to_all | solution.py:99
  134.3 0.6 slice.12
  134.9 5.5 %all-to-all-done.5 = f32[16,16,128]{2,1,0:T(8,128)S(1)} async-done(((f32[16,16,128]{2,1,0:T(8,128)}), f32[16,16,128]{2,1,0:T(8,128)S(1)}, u32[]{:S(2)}, u32[]{:S(2)}) %all-to-all-start.5) | async-done | bytes 131104 | tf_op jit(solution)/shard_map/all_to_all | solution.py:99
  140.4 0.7 div.16
  (6 shorter events, 0.1 us)
Async XLA Ops:
  0.6 25.2 %copy-start = (bf16[128,256]{1,0:T(8,128)(2,1)S(1)}, bf16[128,256]{1,0:T(8,128)(2,1)}, u32[]{:S(2)}) copy-start(bf16[128,256]{1,0:T(8,128)(2,1)} %param.8) | copy-start | bytes 196612
  2.7 23.1 %all-to-all-start = ((bf16[16,256,128]{2,1,0:T(8,128)(2,1)}), bf16[16,256,128]{2,1,0:T(8,128)(2,1)S(1)}, u32[]{:S(2)}, u32[]{:S(2)}) async-start(bf16[16,256,128]{2,1,0:T(8,128)(2,1)} %broadcast_in_dim.8), calls=%async_computation | async-start | bytes 2097152 | tf_op jit(solution)/shard_map/all_to_all | solution.py:99
  34.1 23.8 %copy-start.3 = (bf16[256,256]{1,0:T(8,128)(2,1)S(1)}, bf16[256,256]{1,0:T(8,128)(2,1)}, u32[]{:S(2)}) copy-start(bf16[256,256]{1,0:T(8,128)(2,1)} %param.13) | copy-start | bytes 393220
  83.4 2.5 %copy-start.1 = (bf16[16,256,256]{2,1,0:T(8,128)(2,1)S(1)}, bf16[16,256,256]{2,1,0:T(8,128)(2,1)}, u32[]{:S(2)}) copy-start(bf16[16,256,256]{2,1,0:T(8,128)(2,1)} %get-tuple-element.5) | copy-start | bytes 6291460
  86.8 1.6 %copy-start.2 = (bf16[16,256,256]{2,1,0:T(8,128)(2,1)S(1)}, bf16[16,256,256]{2,1,0:T(8,128)(2,1)}, u32[]{:S(2)}) copy-start(bf16[16,256,256]{2,1,0:T(8,128)(2,1)} %get-tuple-element.6) | copy-start | bytes 6291460
  129.1 11.3 %all-to-all-start.5 = ((f32[16,16,128]{2,1,0:T(8,128)}), f32[16,16,128]{2,1,0:T(8,128)S(1)}, u32[]{:S(2)}, u32[]{:S(2)}) async-start(f32[16,16,128]{2,1,0:T(8,128)} %broadcast_in_dim.11), calls=%async_computation.5 | async-start | bytes 262144 | tf_op jit(solution)/shard_map/all_to_all | solution.py:99

commit v9 on v8

--- a/solution.py
+++ b/solution.py
@@ -16,14 +16,24 @@
     return sig * (1.0 + value * (1.0 - sig))
 
 
-def _block_kernel(transposed, n_in, n_out, rows_ref, cols_ref, live_ref, a_ref, src_ref, *refs):
-    results, out_ref = refs[:-1], refs[-1]
+def _block_kernel(transposed, n_in, n_out, project, rows_ref, cols_ref, live_ref, a_ref, *refs):
+    if project:
+        feat_ref, w_ref = refs[0], refs[1]
+        results, out_ref, src_ref = refs[2:-2], refs[-2], refs[-1]
+    else:
+        src_ref = refs[0]
+        results, out_ref = refs[1:-1], refs[-1]
     g = pl.program_id(0)
     live = live_ref[0]
 
     @pl.when(g == 0)
     def _():
         out_ref[...] = jnp.zeros_like(out_ref)
+        if project:
+            for c in range(n_in):
+                src_ref[c] = jnp.dot(
+                    feat_ref[c], w_ref[...], preferred_element_type=jnp.float32
+                ).astype(src_ref.dtype)
 
     def accumulate(masked):
         for k in range(GROUP):
@@ -62,27 +72,38 @@
             results[1][...] = (total - high.astype(jnp.float32)).astype(jnp.bfloat16)
 
 
-def block_product(adj_values, slot_rows, slot_cols, slot_live, source, count_out, transposed, dtype, outs=1):
+def block_product(adj_values, slot_rows, slot_cols, slot_live, source, count_out, transposed, dtype, outs=1, weight=None):
     slots, size, _ = adj_values.shape
-    n_in, _, width = source.shape
+    project = weight is not None
+    n_in = source.shape[0]
+    width = weight.shape[1] if project else source.shape[2]
     steps = slots // GROUP
+    if project:
+        fin = weight.shape[0]
+        operands = (source, weight)
+        specs = [
+            pl.BlockSpec((n_in, size, fin), lambda g, r, c, l: (0, 0, 0)),
+            pl.BlockSpec((fin, width), lambda g, r, c, l: (0, 0)),
+        ]
+        scratch = [pltpu.VMEM((count_out, size, width), jnp.float32), pltpu.VMEM((n_in, size, width), jnp.bfloat16)]
+    else:
+        operands = (source,)
+        specs = [pl.BlockSpec((n_in, size, width), lambda g, r, c, l: (0, 0, 0))]
+        scratch = [pltpu.VMEM((count_out, size, width), jnp.float32)]
 
     def a_map(g, rows, cols, live):
         last = jnp.maximum((live[0] - 1) // GROUP, 0)
         return (jnp.minimum(g, last), 0, 0)
 
-    kernel = functools.partial(_block_kernel, transposed, n_in, count_out)
+    kernel = functools.partial(_block_kernel, transposed, n_in, count_out, project)
     return pl.pallas_call(
         kernel,
         grid_spec=pltpu.PrefetchScalarGridSpec(
             num_scalar_prefetch=3,
             grid=(steps,),
-            in_specs=[
-                pl.BlockSpec((GROUP, size, size), a_map),
-                pl.BlockSpec((n_in, size, width), lambda g, r, c, l: (0, 0, 0)),
-            ],
+            in_specs=[pl.BlockSpec((GROUP, size, size), a_map)] + specs,
             out_specs=[pl.BlockSpec((count_out, size, width), lambda g, r, c, l: (0, 0, 0))] * outs,
-            scratch_shapes=[pltpu.VMEM((count_out, size, width), jnp.float32)],
+            scratch_shapes=scratch,
         ),
         out_shape=[jax.ShapeDtypeStruct((count_out, size, width), dtype)] * outs,
         compiler_params=pltpu.CompilerParams(dimension_semantics=("arbitrary",)),
@@ -91,7 +112,7 @@
             bytes_accessed=slots * size * size * 2 + n_in * size * width * 2 + count_out * size * width * 4,
             transcendentals=0,
         ),
-    )(slot_rows, slot_cols, slot_live, adj_values, source)
+    )(slot_rows, slot_cols, slot_live, adj_values, *operands)
 
 
 def gather_axis(block, axis, count):
@@ -118,10 +139,9 @@
     nodes = own_rows * n_row * n_col
 
     feature_cols = gather_axis(features, "row", n_row).reshape(own_rows * n_row, fin)
-    projected = jnp.dot(feature_cols, weight, preferred_element_type=jnp.float32).astype(jnp.bfloat16)
-    column_blocks = projected.reshape(tile_cols, size, width)
     (partial_value,) = block_product(
-        adj_values, slot_rows, slot_cols, slot_live, column_blocks, tile_rows, False, jnp.bfloat16
+        adj_values, slot_rows, slot_cols, slot_live, feature_cols.reshape(tile_cols, size, fin),
+        tile_rows, False, jnp.bfloat16, weight=weight,
     )
     received = lax.all_to_all(partial_value, "col", 0, 0, tiled=True)
     summed = received.astype(jnp.float32).sum(axis=0)

time: 142 us -> 141 us (level)
  blocking collectives: 79.8 us -> 76.7 us
  Pallas kernels: 13.9 us -> 16.9 us
  matrix products: 6.67 us -> 4.65 us
    all_to_all x1, blocking collectives: 29.3 us -> 25.9 us  [body(): lax.all_to_all(payload.astype(jnp.bfloat16), 'row', 0, 0, tiled=True)]
    pallas_call x2, Pallas kernels: 13.9 us -> 16.9 us  [block_product(): pl.pallas_call(kernel, grid_spec=pltpu.PrefetchScalarGridSpec(num_scalar_...]
    dot_general x1 -> x0, matrix products: 2.03 us -> none  [body(): jnp.dot(feature_cols, weight, preferred_element_type=jnp.float32)]
where the time goes in v9:
time: 141 us; the launch traced here: 140 us
  blocking collectives  76.7 us (54%)
  waiting for transfers between devices  20.6 us (15%)
  Pallas kernels  16.9 us (12%)
  starting transfers between devices  12.5 us (9%)
  local copies, waits for them, and re-layouts  6.09 us (4%)
  matrix products  4.65 us (3%)
    all_to_all x2, blocking collectives, gather_axis(): return lax.all_to_all(spread, axis, 0, 0, tiled=True)  26.4 us
    all_to_all x1, blocking collectives, body(): lax.all_to_all(payload.astype(jnp.bfloat16), 'row', 0, 0, tiled=True)  25.9 us
    all_to_all x1, blocking collectives, body(): received = lax.all_to_all(partial_value, 'col', 0, 0, tiled=True)  24.4 us
    all_to_all x2, waiting for transfers between devices, gather_axis(): return lax.all_to_all(spread, axis, 0, 0, tiled=True)  20.6 us
    pallas_call x2, Pallas kernels, block_product(): pl.pallas_call(kernel, grid_spec=pltpu.PrefetchScalarGridSpec(num_scalar_...  16.9 us
    all_to_all x2, starting transfers between devices, gather_axis(): return lax.all_to_all(spread, axis, 0, 0, tiled=True)  12.5 us
    dot_general x2, matrix products, pair_dot(): lax.dot_general(low, right, dims, preferred_element_type=jnp.float32)  3.2 us
  transfers between devices with their start and end apart: 2, of which 2 were waited for; matrix products, arithmetic and copies ran while one was open for 0% of the time, Pallas kernels for 0%

profile of v9, /device:TPU:1, one launch (start us, length us, event | category | flops | bytes accessed | tf_op | source)
XLA Modules:
  0.0 140.0 jit_solution(51336276325806382)
XLA Ops:
  0.6 2.0 %broadcast_in_dim.8 = bf16[16,256,128]{2,1,0:T(8,128)(2,1)} broadcast(bf16[256,128]{1,0:T(8,128)(2,1)} %param.7), dimensions={1,2} | broadcast | bytes 1114112 | tf_op jit(solution)/shard_map/broadcast_in_dim | solution.py:119
  2.6 7.3 %all-to-all-start = ((bf16[16,256,128]{2,1,0:T(8,128)(2,1)}), bf16[16,256,128]{2,1,0:T(8,128)(2,1)S(1)}, u32[]{:S(2)}, u32[]{:S(2)}) async-start(bf16[16,256,128]{2,1,0:T(8,128)(2,1)} %broadcast_in_dim.8), calls=%async_computation | async-start | bytes 2097152 | tf_op jit(solution)/shard_map/all_to_all | solution.py:120
  10.6 15.1 %all-to-all-done.refs_0_ = bf16[16,256,128]{2,1,0:T(8,128)(2,1)S(1)} async-done(((bf16[16,256,128]{2,1,0:T(8,128)(2,1)}), bf16[16,256,128]{2,1,0:T(8,128)(2,1)S(1)}, u32[]{:S(2)}, u32[]{:S(2)}) %all-to-all-start) | async-done | bytes 1048608 | tf_op jit(solution)/shard_map/all_to_all | solution.py:120
  25.7 1.0 copy-done.1
  26.7 7.8 %shard_map.94 = bf16[8,256,256]{2,1,0:T(8,128)(2,1)} custom-call(s32[96]{0:T(128)} %rows_ref.3, s32[96]{0:T(128)} %cols_ref.3, s32[1]{0:T(128)S(6)} %copy.20.live_ref, bf16[96,256,256]{2,1,0:T(8,128)(2,1)} %a_ref.3, bf16[16,256,128]{2,1,0:T(8,128)(2,1)} %copy-done.1, bf16[128,256]{1,0:T(8,128)(2,1)} %refs_1_.1), custom_call_target="tpu_custom_call" | custom-call | flops 3221225472 | bytes 16777216 | tf_op jit(solution)/shard_map/pallas_call | solution.py:99
  34.5 24.4 %all_to_all.30 = bf16[8,256,256]{2,1,0:T(8,128)(2,1)S(1)} all-to-all(bf16[8,256,256]{2,1,0:T(8,128)(2,1)} %shard_map.94), channel_id=1, replica_groups=mesh['row'=16,'col'=8] {'col'}, dimensions={0} | all-to-all | bytes 2097152 | tf_op jit(solution)/shard_map/all_to_all | solution.py:146
  58.9 0.1 convert_reduce_fusion.1
  59.0 0.0 copy-done.5
  59.1 0.8 multiply_convert_fusion
  59.8 0.1 broadcast_in_dim.9
  59.9 17.1 %all_to_all.31.refs_0_ = bf16[8,256,256]{2,1,0:T(8,128)(2,1)} all-to-all(bf16[8,256,256]{2,1,0:T(8,128)(2,1)S(1)} %broadcast_in_dim.9), channel_id=1, replica_groups=mesh['row'=16,'col'=8] {'col'}, dimensions={0} | all-to-all | bytes 2097152 | tf_op jit(solution)/shard_map/all_to_all | solution.py:120
  77.0 9.1 %shard_map.95 = (bf16[16,256,256]{2,1,0:T(8,128)(2,1)}, bf16[16,256,256]{2,1,0:T(8,128)(2,1)}) custom-call(s32[96]{0:T(128)} %rows_ref.3, s32[96]{0:T(128)} %cols_ref.3, s32[1]{0:T(128)S(6)} %copy.20.live_ref, bf16[96,256,256]{2,1,0:T(8,128)(2,1)} %a_ref.3, bf16[8,256,256]{2,1,0:T(8,128)(2,1)} %all_to_all.31.refs_0_), custom_call_target="tpu_custom_call" | custom-call | flops 3221225472 | bytes 17825792 | tf_op jit(solution)/shard_map/pallas_call | solution.py:99
  86.1 0.0 copy-done.2
  86.1 2.5 %convolution_bitcast_fusion = f32[256,128]{1,0:T(8,128)S(1)} fusion(bf16[16,256,256]{2,1,0:T(8,128)(2,1)} %get-tuple-element.6, bf16[16,256,128]{2,1,0:T(8,128)(2,1)S(1)} %copy-done.2), kind=kOutput, calls=%fused_computation.4 | convolution fusion | flops 268435456 | bytes 3276800 | tf_op jit(solution)/shard_map/dot_general | solution.py:125
  88.6 0.0 copy-start.4
  88.6 0.0 copy-done
  88.6 0.8 fusion.3
  89.4 0.1 copy.17
  89.5 0.0 copy-done.4
  89.5 0.0 copy-start.3
  89.5 0.7 fusion.4
  90.2 0.9 copy-done.3
  91.1 0.7 fusion
  91.8 0.1 pad_maximum_fusion
  91.9 25.9 %all_to_all.32 = bf16[16,272,128]{2,1,0:T(8,128)(2,1)S(1)} all-to-all(bf16[16,272,128]{2,1,0:T(8,128)(2,1)S(1)} %pad_maximum_fusion), channel_id=1, replica_groups=mesh['row'=16,'col'=8] {'row'}, dimensions={0} | all-to-all | bytes 2228224 | tf_op jit(solution)/shard_map/all_to_all | solution.py:161
  117.8 0.2 convert_reduce_fusion
  118.0 9.3 %all_to_all.33 = f32[8,16,128]{2,1,0:T(8,128)S(1)} all-to-all(f32[8,16,128]{2,1,0:T(8,128)S(1)} %broadcast_in_dim.10), channel_id=1, replica_groups=mesh['row'=16,'col'=8] {'col'}, dimensions={0} | all-to-all | bytes 131072 | tf_op jit(solution)/shard_map/all_to_all | solution.py:120
  127.3 0.7 broadcast_in_dim.11
  128.0 5.1 %all-to-all-start.5 = ((f32[16,16,128]{2,1,0:T(8,128)}), f32[16,16,128]{2,1,0:T(8,128)S(1)}, u32[]{:S(2)}, u32[]{:S(2)}) async-start(f32[16,16,128]{2,1,0:T(8,128)} %broadcast_in_dim.11), calls=%async_computation.5 | async-start | bytes 262144 | tf_op jit(solution)/shard_map/all_to_all | solution.py:120
  133.1 0.6 slice.12
  133.8 5.5 %all-to-all-done.5 = f32[16,16,128]{2,1,0:T(8,128)S(1)} async-done(((f32[16,16,128]{2,1,0:T(8,128)}), f32[16,16,128]{2,1,0:T(8,128)S(1)}, u32[]{:S(2)}, u32[]{:S(2)}) %all-to-all-start.5) | async-done | bytes 131104 | tf_op jit(solution)/shard_map/all_to_all | solution.py:120
  139.3 0.7 div.16
  (9 shorter events, 0.1 us)
Async XLA Ops:
  2.6 23.1 %all-to-all-start = ((bf16[16,256,128]{2,1,0:T(8,128)(2,1)}), bf16[16,256,128]{2,1,0:T(8,128)(2,1)S(1)}, u32[]{:S(2)}, u32[]{:S(2)}) async-start(bf16[16,256,128]{2,1,0:T(8,128)(2,1)} %broadcast_in_dim.8), calls=%async_computation | async-start | bytes 2097152 | tf_op jit(solution)/shard_map/all_to_all | solution.py:120
  25.7 1.0 copy-start.1
  34.5 24.5 %copy-start.5 = (bf16[256,256]{1,0:T(8,128)(2,1)S(1)}, bf16[256,256]{1,0:T(8,128)(2,1)}, u32[]{:S(2)}) copy-start(bf16[256,256]{1,0:T(8,128)(2,1)} %param.13) | copy-start | bytes 393220
  77.0 9.1 %copy-start.2 = (bf16[16,256,128]{2,1,0:T(8,128)(2,1)S(1)}, bf16[16,256,128]{2,1,0:T(8,128)(2,1)}, u32[]{:S(2)}) copy-start(bf16[16,256,128]{2,1,0:T(8,128)(2,1)} %copy-done.1) | copy-start | bytes 3145732
  86.1 2.5 %copy-start = (bf16[16,256,256]{2,1,0:T(8,128)(2,1)S(1)}, bf16[16,256,256]{2,1,0:T(8,128)(2,1)}, u32[]{:S(2)}) copy-start(bf16[16,256,256]{2,1,0:T(8,128)(2,1)} %get-tuple-element.5) | copy-start | bytes 6291460
  88.6 0.9 copy-start.4
  89.5 1.6 %copy-start.3 = (bf16[16,256,256]{2,1,0:T(8,128)(2,1)S(1)}, bf16[16,256,256]{2,1,0:T(8,128)(2,1)}, u32[]{:S(2)}) copy-start(bf16[16,256,256]{2,1,0:T(8,128)(2,1)} %get-tuple-element.6) | copy-start | bytes 6291460
  128.0 11.3 %all-to-all-start.5 = ((f32[16,16,128]{2,1,0:T(8,128)}), f32[16,16,128]{2,1,0:T(8,128)S(1)}, u32[]{:S(2)}, u32[]{:S(2)}) async-start(f32[16,16,128]{2,1,0:T(8,128)} %broadcast_in_dim.11), calls=%async_computation.5 | async-start | bytes 262144 | tf_op jit(solution)/shard_map/all_to_all | solution.py:120

commit v10 on v9

--- a/solution.py
+++ b/solution.py
@@ -17,7 +17,11 @@
 
 
 def _block_kernel(transposed, n_in, n_out, project, rows_ref, cols_ref, live_ref, a_ref, *refs):
-    if project:
+    grads = transposed and len(refs) == 6
+    if grads:
+        src_ref, feat_ref, w_ref = refs[0], refs[1], refs[2]
+        results, out_ref = refs[3:-1], refs[-1]
+    elif project:
         feat_ref, w_ref = refs[0], refs[1]
         results, out_ref, src_ref = refs[2:-2], refs[-2], refs[-1]
     else:
@@ -63,6 +67,22 @@
 
     @pl.when(g == pl.num_programs(0) - 1)
     def _():
+        if grads:
+            dims_f = (((1,), (1,)), ((), ()))
+            dims_w = (((0,), (0,)), ((), ()))
+            weight_total = jnp.zeros(results[1].shape, jnp.float32)
+            for c in range(n_out):
+                block = out_ref[c]
+                high = block.astype(jnp.bfloat16)
+                low = (block - high.astype(jnp.float32)).astype(jnp.bfloat16)
+                results[0][c] = lax.dot_general(
+                    high, w_ref[...], dims_f, preferred_element_type=jnp.float32
+                ) + lax.dot_general(low, w_ref[...], dims_f, preferred_element_type=jnp.float32)
+                weight_total = weight_total + lax.dot_general(
+                    feat_ref[c], high, dims_w, preferred_element_type=jnp.float32
+                ) + lax.dot_general(feat_ref[c], low, dims_w, preferred_element_type=jnp.float32)
+            results[1][...] = weight_total
+            return
         total = out_ref[...]
         if len(results) == 1:
             results[0][...] = total.astype(results[0].dtype)
@@ -72,13 +92,32 @@
             results[1][...] = (total - high.astype(jnp.float32)).astype(jnp.bfloat16)
 
 
-def block_product(adj_values, slot_rows, slot_cols, slot_live, source, count_out, transposed, dtype, outs=1, weight=None):
+def block_product(adj_values, slot_rows, slot_cols, slot_live, source, count_out, transposed, dtype, outs=1, weight=None, feats=None):
     slots, size, _ = adj_values.shape
-    project = weight is not None
+    project = weight is not None and not transposed
     n_in = source.shape[0]
-    width = weight.shape[1] if project else source.shape[2]
+    width = source.shape[2] if transposed or not project else weight.shape[1]
+    out_specs = [pl.BlockSpec((count_out, size, width), lambda g, r, c, l: (0, 0, 0))] * outs
+    out_shapes = [jax.ShapeDtypeStruct((count_out, size, width), dtype)] * outs
     steps = slots // GROUP
-    if project:
+    if transposed and weight is not None:
+        fin = weight.shape[0]
+        operands = (source, feats, weight)
+        specs = [
+            pl.BlockSpec((n_in, size, width), lambda g, r, c, l: (0, 0, 0)),
+            pl.BlockSpec((count_out, size, fin), lambda g, r, c, l: (0, 0, 0)),
+            pl.BlockSpec((fin, width), lambda g, r, c, l: (0, 0)),
+        ]
+        scratch = [pltpu.VMEM((count_out, size, width), jnp.float32)]
+        out_specs = [
+            pl.BlockSpec((count_out, size, fin), lambda g, r, c, l: (0, 0, 0)),
+            pl.BlockSpec((fin, width), lambda g, r, c, l: (0, 0)),
+        ]
+        out_shapes = [
+            jax.ShapeDtypeStruct((count_out, size, fin), jnp.float32),
+            jax.ShapeDtypeStruct((fin, width), jnp.float32),
+        ]
+    elif project:
         fin = weight.shape[0]
         operands = (source, weight)
         specs = [
@@ -102,10 +141,10 @@
             num_scalar_prefetch=3,
             grid=(steps,),
             in_specs=[pl.BlockSpec((GROUP, size, size), a_map)] + specs,
-            out_specs=[pl.BlockSpec((count_out, size, width), lambda g, r, c, l: (0, 0, 0))] * outs,
+            out_specs=out_specs,
             scratch_shapes=scratch,
         ),
-        out_shape=[jax.ShapeDtypeStruct((count_out, size, width), dtype)] * outs,
+        out_shape=out_shapes,
         compiler_params=pltpu.CompilerParams(dimension_semantics=("arbitrary",)),
         cost_estimate=pl.CostEstimate(
             flops=2 * slots * size * size * width,
@@ -149,13 +188,10 @@
     grad_summed = (cotangent.astype(jnp.float32) * silu_slope(summed)).astype(jnp.bfloat16)
     grad_range = gather_axis(grad_summed, "col", n_col)
     grad_blocks = grad_range.reshape(tile_rows, size, width)
-    back_high, back_low = block_product(
-        adj_values, slot_rows, slot_cols, slot_live, grad_blocks, tile_cols, True, jnp.bfloat16, 2
-    )
-    back_high = back_high.reshape(tile_cols * size, width)
-    back_low = back_low.reshape(tile_cols * size, width)
-    feature_part = pair_dot(back_high, back_low, weight, (((1,), (1,)), ((), ())))
-    weight_part = pair_dot(back_high, back_low, feature_cols, (((0,), (0,)), ((), ()))).T
+    feature_part, weight_part = block_product(
+        adj_values, slot_rows, slot_cols, slot_live, grad_blocks, tile_cols, True, jnp.float32,
+        weight=weight, feats=feature_cols.reshape(tile_cols, size, fin),
+    )
     pieces = weight_part.reshape(tile_cols, fin * width // (tile_cols * fin), fin)
     payload = jnp.concatenate([feature_part.reshape(tile_cols, size, fin), pieces], axis=1)
     exchanged = lax.all_to_all(payload.astype(jnp.bfloat16), "row", 0, 0, tiled=True)

time: 141 us -> 138 us (0.979)
  Pallas kernels: 16.9 us -> 21.9 us
  matrix products: 4.65 us -> 0 us
  blocking collectives: 76.7 us -> 72.5 us
  other arithmetic: 1.16 us -> 2.98 us
    all_to_all x1, blocking collectives: 25.9 us -> 19.1 us  [body(): lax.all_to_all(payload.astype(jnp.bfloat16), 'row', 0, 0, tiled=True)]
    pallas_call x2, Pallas kernels: 16.9 us -> 21.9 us  [block_product(): pl.pallas_call(kernel, grid_spec=pltpu.PrefetchScalarGridSpec(num_scalar_...]
    dot_general x4 -> x0, matrix products: 4.65 us -> none  [the longest x2 3.2 us: pair_dot(): lax.dot_general(low, right, dims, preferred_element_type=jnp.float32)]
    all_to_all x2, blocking collectives: 26.4 us -> 30.8 us  [gather_axis(): return lax.all_to_all(spread, axis, 0, 0, tiled=True)]
    all_to_all x1, blocking collectives: 24.4 us -> 22.5 us  [body(): received = lax.all_to_all(partial_value, 'col', 0, 0, tiled=True)]
    another operation x0 -> x2, other arithmetic: none -> 1.82 us
where the time goes in v10:
time: 138 us; the launch traced here: 137 us
  blocking collectives  72.5 us (53%)
  Pallas kernels  21.9 us (16%)
  waiting for transfers between devices  20.6 us (15%)
  starting transfers between devices  12.5 us (9%)
  local copies, waits for them, and re-layouts  5.14 us (4%)
  other arithmetic  2.98 us (2%)
    all_to_all x2, blocking collectives, gather_axis(): return lax.all_to_all(spread, axis, 0, 0, tiled=True)  30.8 us
    all_to_all x1, blocking collectives, body(): received = lax.all_to_all(partial_value, 'col', 0, 0, tiled=True)  22.5 us
    pallas_call x2, Pallas kernels, block_product(): pl.pallas_call(kernel, grid_spec=pltpu.PrefetchScalarGridSpec(num_scalar_...  21.9 us
    all_to_all x2, waiting for transfers between devices, gather_axis(): return lax.all_to_all(spread, axis, 0, 0, tiled=True)  20.6 us
    all_to_all x1, blocking collectives, body(): lax.all_to_all(payload.astype(jnp.bfloat16), 'row', 0, 0, tiled=True)  19.1 us
    all_to_all x2, starting transfers between devices, gather_axis(): return lax.all_to_all(spread, axis, 0, 0, tiled=True)  12.5 us
    broadcast_in_dim x4, local copies, waits for them, and re-layouts, gather_axis(): spread = jnp.broadcast_to(block[None], (count,) + block.shape)  2.77 us
  transfers between devices with their start and end apart: 2, of which 2 were waited for; matrix products, arithmetic and copies ran while one was open for 0% of the time, Pallas kernels for 0%

profile of v10, /device:TPU:1, one launch (start us, length us, event | category | flops | bytes accessed | tf_op | source)
XLA Modules:
  0.0 137.0 jit_solution(3179296605266387912)
XLA Ops:
  0.6 2.0 %broadcast_in_dim.8 = bf16[16,256,128]{2,1,0:T(8,128)(2,1)} broadcast(bf16[256,128]{1,0:T(8,128)(2,1)} %param.7), dimensions={1,2} | broadcast | bytes 1114112 | tf_op jit(solution)/shard_map/broadcast_in_dim | solution.py:158
  2.7 7.3 %all-to-all-start = ((bf16[16,256,128]{2,1,0:T(8,128)(2,1)}), bf16[16,256,128]{2,1,0:T(8,128)(2,1)S(1)}, u32[]{:S(2)}, u32[]{:S(2)}) async-start(bf16[16,256,128]{2,1,0:T(8,128)(2,1)} %broadcast_in_dim.8), calls=%async_computation | async-start | bytes 2097152 | tf_op jit(solution)/shard_map/all_to_all | solution.py:159
  10.6 15.1 %all-to-all-done.refs_0_.refs_1_ = bf16[16,256,128]{2,1,0:T(8,128)(2,1)S(1)} async-done(((bf16[16,256,128]{2,1,0:T(8,128)(2,1)}), bf16[16,256,128]{2,1,0:T(8,128)(2,1)S(1)}, u32[]{:S(2)}, u32[]{:S(2)}) %all-to-all-start) | async-done | bytes 1048608 | tf_op jit(solution)/shard_map/all_to_all | solution.py:159
  25.7 0.0 copy-start
  25.7 1.0 copy-done
  26.7 10.0 %shard_map.94 = bf16[8,256,256]{2,1,0:T(8,128)(2,1)} custom-call(s32[96]{0:T(128)} %rows_ref.3, s32[96]{0:T(128)} %cols_ref.3, s32[1]{0:T(128)S(6)} %copy.10.live_ref, bf16[96,256,256]{2,1,0:T(8,128)(2,1)} %a_ref.3, bf16[16,256,128]{2,1,0:T(8,128)(2,1)} %copy-done, bf16[128,256]{1,0:T(8,128)(2,1)} %refs_2_.1), custom_call_target="tpu_custom_call" | custom-call | flops 3221225472 | bytes 16777216 | tf_op jit(solution)/shard_map/pallas_call | solution.py:138
  36.7 0.0 copy-start.1
  36.7 22.5 %all_to_all.30 = bf16[8,256,256]{2,1,0:T(8,128)(2,1)S(1)} all-to-all(bf16[8,256,256]{2,1,0:T(8,128)(2,1)} %shard_map.94), channel_id=1, replica_groups=mesh['row'=16,'col'=8] {'col'}, dimensions={0} | all-to-all | bytes 2097152 | tf_op jit(solution)/shard_map/all_to_all | solution.py:185
  59.2 0.1 convert_reduce_fusion.1
  59.4 0.0 copy-done.1
  59.4 0.8 multiply_convert_fusion
  60.2 0.1 broadcast_in_dim.9
  60.2 19.5 %all_to_all.31.refs_0_ = bf16[8,256,256]{2,1,0:T(8,128)(2,1)} all-to-all(bf16[8,256,256]{2,1,0:T(8,128)(2,1)S(1)} %broadcast_in_dim.9), channel_id=1, replica_groups=mesh['row'=16,'col'=8] {'col'}, dimensions={0} | all-to-all | bytes 2097152 | tf_op jit(solution)/shard_map/all_to_all | solution.py:159
  79.7 12.0 %shard_map.95 = (f32[16,256,128]{2,1,0:T(8,128)}, f32[128,256]{1,0:T(8,128)}) custom-call(s32[96]{0:T(128)} %rows_ref.3, s32[96]{0:T(128)} %cols_ref.3, s32[1]{0:T(128)S(6)} %copy.10.live_ref, bf16[96,256,256]{2,1,0:T(8,128)(2,1)} %a_ref.3, bf16[8,256,256]{2,1,0:T(8,128)(2,1)} %all_to_all.31.refs_0_, bf16[16,256,128]{2,1,0:T(8,128)(2,1)} %copy-done, ...), custom_call_target="tpu_custom_call" | custom-call | flops 3221225472 | bytes 17825792 | tf_op jit(solution)/shard_map/pallas_call | solution.py:138
  91.7 0.0 copy-start.2
  91.7 1.8 %convert.10 = bf16[16,256,128]{2,1,0:T(8,128)(2,1)S(1)} convert(f32[16,256,128]{2,1,0:T(8,128)} %get-tuple-element.5) | non-fusion elementwise | flops 524288 | bytes 3145728 | tf_op jit(solution)/shard_map/convert.1
  93.6 0.0 copy-done.2
  93.6 0.1 pad_maximum_fusion
  93.7 19.1 %all_to_all.32 = bf16[16,272,128]{2,1,0:T(8,128)(2,1)S(1)} all-to-all(bf16[16,272,128]{2,1,0:T(8,128)(2,1)S(1)} %pad_maximum_fusion), channel_id=1, replica_groups=mesh['row'=16,'col'=8] {'row'}, dimensions={0} | all-to-all | bytes 2228224 | tf_op jit(solution)/shard_map/all_to_all | solution.py:197
  112.8 0.2 convert_reduce_fusion
  113.0 11.3 %all_to_all.33 = f32[8,16,128]{2,1,0:T(8,128)S(1)} all-to-all(f32[8,16,128]{2,1,0:T(8,128)S(1)} %broadcast_in_dim.10), channel_id=1, replica_groups=mesh['row'=16,'col'=8] {'col'}, dimensions={0} | all-to-all | bytes 131072 | tf_op jit(solution)/shard_map/all_to_all | solution.py:159
  124.3 0.7 broadcast_in_dim.11
  125.0 5.1 %all-to-all-start.5 = ((f32[16,16,128]{2,1,0:T(8,128)}), f32[16,16,128]{2,1,0:T(8,128)S(1)}, u32[]{:S(2)}, u32[]{:S(2)}) async-start(f32[16,16,128]{2,1,0:T(8,128)} %broadcast_in_dim.11), calls=%async_computation.5 | async-start | bytes 262144 | tf_op jit(solution)/shard_map/all_to_all | solution.py:159
  130.1 0.6 slice.12
  130.8 5.5 %all-to-all-done.5 = f32[16,16,128]{2,1,0:T(8,128)S(1)} async-done(((f32[16,16,128]{2,1,0:T(8,128)}), f32[16,16,128]{2,1,0:T(8,128)S(1)}, u32[]{:S(2)}, u32[]{:S(2)}) %all-to-all-start.5) | async-done | bytes 131104 | tf_op jit(solution)/shard_map/all_to_all | solution.py:159
  136.3 0.7 div.16
  (6 shorter events, 0.1 us)
Async XLA Ops:
  2.7 23.1 %all-to-all-start = ((bf16[16,256,128]{2,1,0:T(8,128)(2,1)}), bf16[16,256,128]{2,1,0:T(8,128)(2,1)S(1)}, u32[]{:S(2)}, u32[]{:S(2)}) async-start(bf16[16,256,128]{2,1,0:T(8,128)(2,1)} %broadcast_in_dim.8), calls=%async_computation | async-start | bytes 2097152 | tf_op jit(solution)/shard_map/all_to_all | solution.py:159
  25.7 1.0 copy-start
  36.7 22.7 %copy-start.1 = (bf16[256,256]{1,0:T(8,128)(2,1)S(1)}, bf16[256,256]{1,0:T(8,128)(2,1)}, u32[]{:S(2)}) copy-start(bf16[256,256]{1,0:T(8,128)(2,1)} %param.13) | copy-start | bytes 393220
  91.7 1.8 %copy-start.2 = (f32[128,256]{1,0:T(8,128)S(1)}, f32[128,256]{1,0:T(8,128)}, u32[]{:S(2)}) copy-start(f32[128,256]{1,0:T(8,128)} %get-tuple-element.6) | copy-start | bytes 393220
  125.0 11.3 %all-to-all-start.5 = ((f32[16,16,128]{2,1,0:T(8,128)}), f32[16,16,128]{2,1,0:T(8,128)S(1)}, u32[]{:S(2)}, u32[]{:S(2)}) async-start(f32[16,16,128]{2,1,0:T(8,128)} %broadcast_in_dim.11), calls=%async_computation.5 | async-start | bytes 262144 | tf_op jit(solution)/shard_map/all_to_all | solution.py:159

commit v11 on v10

--- a/solution.py
+++ b/solution.py
@@ -17,7 +17,7 @@
 
 
 def _block_kernel(transposed, n_in, n_out, project, rows_ref, cols_ref, live_ref, a_ref, *refs):
-    grads = transposed and len(refs) == 6
+    grads = transposed and len(refs) == 5
     if grads:
         src_ref, feat_ref, w_ref = refs[0], refs[1], refs[2]
         results, out_ref = refs[3:-1], refs[-1]
@@ -70,18 +70,26 @@
         if grads:
             dims_f = (((1,), (1,)), ((), ()))
             dims_w = (((0,), (0,)), ((), ()))
-            weight_total = jnp.zeros(results[1].shape, jnp.float32)
+            fin = feat_ref.shape[2]
+            size = out_ref.shape[1]
+            weight_total = jnp.zeros((fin, out_ref.shape[2]), jnp.float32)
             for c in range(n_out):
                 block = out_ref[c]
                 high = block.astype(jnp.bfloat16)
                 low = (block - high.astype(jnp.float32)).astype(jnp.bfloat16)
-                results[0][c] = lax.dot_general(
+                part = lax.dot_general(
                     high, w_ref[...], dims_f, preferred_element_type=jnp.float32
                 ) + lax.dot_general(low, w_ref[...], dims_f, preferred_element_type=jnp.float32)
+                results[0][c, :size, :] = part.astype(results[0].dtype)
                 weight_total = weight_total + lax.dot_general(
                     feat_ref[c], high, dims_w, preferred_element_type=jnp.float32
                 ) + lax.dot_general(feat_ref[c], low, dims_w, preferred_element_type=jnp.float32)
-            results[1][...] = weight_total
+            rows_per = fin // n_out
+            half = weight_total.shape[1] // 2
+            for c in range(n_out):
+                chunk = weight_total[c * rows_per:(c + 1) * rows_per]
+                results[0][c, size:size + rows_per, :] = chunk[:, :half].astype(results[0].dtype)
+                results[0][c, size + rows_per:size + 2 * rows_per, :] = chunk[:, half:].astype(results[0].dtype)
             return
         total = out_ref[...]
         if len(results) == 1:
@@ -109,14 +117,9 @@
             pl.BlockSpec((fin, width), lambda g, r, c, l: (0, 0)),
         ]
         scratch = [pltpu.VMEM((count_out, size, width), jnp.float32)]
-        out_specs = [
-            pl.BlockSpec((count_out, size, fin), lambda g, r, c, l: (0, 0, 0)),
-            pl.BlockSpec((fin, width), lambda g, r, c, l: (0, 0)),
-        ]
-        out_shapes = [
-            jax.ShapeDtypeStruct((count_out, size, fin), jnp.float32),
-            jax.ShapeDtypeStruct((fin, width), jnp.float32),
-        ]
+        extra = 2 * (fin // count_out)
+        out_specs = [pl.BlockSpec((count_out, size + extra, fin), lambda g, r, c, l: (0, 0, 0))]
+        out_shapes = [jax.ShapeDtypeStruct((count_out, size + extra, fin), jnp.bfloat16)]
     elif project:
         fin = weight.shape[0]
         operands = (source, weight)
@@ -188,17 +191,17 @@
     grad_summed = (cotangent.astype(jnp.float32) * silu_slope(summed)).astype(jnp.bfloat16)
     grad_range = gather_axis(grad_summed, "col", n_col)
     grad_blocks = grad_range.reshape(tile_rows, size, width)
-    feature_part, weight_part = block_product(
+    (payload,) = block_product(
         adj_values, slot_rows, slot_cols, slot_live, grad_blocks, tile_cols, True, jnp.float32,
         weight=weight, feats=feature_cols.reshape(tile_cols, size, fin),
     )
-    pieces = weight_part.reshape(tile_cols, fin * width // (tile_cols * fin), fin)
-    payload = jnp.concatenate([feature_part.reshape(tile_cols, size, fin), pieces], axis=1)
-    exchanged = lax.all_to_all(payload.astype(jnp.bfloat16), "row", 0, 0, tiled=True)
+    exchanged = lax.all_to_all(payload, "row", 0, 0, tiled=True)
     gathered = exchanged.astype(jnp.float32).sum(axis=0)
     grad_features = gathered[:size].astype(jnp.bfloat16)
     weight_piece = gather_axis(gathered[size:], "col", n_col).sum(axis=0)
-    grad_weight = gather_axis(weight_piece, "row", n_row).reshape(fin, width)
+    pieces = gather_axis(weight_piece, "row", n_row)
+    rows_per = fin // tile_cols
+    grad_weight = pieces.reshape(tile_cols, 2, rows_per, fin).transpose(0, 2, 1, 3).reshape(fin, width)
     grad_weight = grad_weight / math.sqrt(nodes)
     return (output, grad_features, grad_weight)
 

time: 138 us -> 136 us (0.986)
  Pallas kernels: 21.9 us -> 17.4 us
  blocking collectives: 72.5 us -> 77 us
    all_to_all x1, blocking collectives: 19.1 us -> 26.3 us  [body(): exchanged = lax.all_to_all(payload, 'row', 0, 0, tiled=True)]
    pallas_call x2, Pallas kernels: 21.9 us -> 17.4 us  [block_product(): pl.pallas_call(kernel, grid_spec=pltpu.PrefetchScalarGridSpec(num_scalar_...]
    all_to_all x2, blocking collectives: 30.8 us -> 26.3 us  [gather_axis(): return lax.all_to_all(spread, axis, 0, 0, tiled=True)]
    all_to_all x1, blocking collectives: 22.5 us -> 24.4 us  [body(): received = lax.all_to_all(partial_value, 'col', 0, 0, tiled=True)]
    another operation x2 -> x0, other arithmetic: 1.82 us -> none
where the time goes in v11:
time: 136 us; the launch traced here: 135 us
  blocking collectives  77 us (57%)
  waiting for transfers between devices  20.6 us (15%)
  Pallas kernels  17.4 us (13%)
  starting transfers between devices  12.5 us (9%)
  local copies, waits for them, and re-layouts  4.43 us (3%)
  other arithmetic  1.74 us (1%)
    all_to_all x1, blocking collectives, body(): exchanged = lax.all_to_all(payload, 'row', 0, 0, tiled=True)  26.3 us
    all_to_all x2, blocking collectives, gather_axis(): return lax.all_to_all(spread, axis, 0, 0, tiled=True)  26.3 us
    all_to_all x1, blocking collectives, body(): received = lax.all_to_all(partial_value, 'col', 0, 0, tiled=True)  24.4 us
    all_to_all x2, waiting for transfers between devices, gather_axis(): return lax.all_to_all(spread, axis, 0, 0, tiled=True)  20.6 us
    pallas_call x2, Pallas kernels, block_product(): pl.pallas_call(kernel, grid_spec=pltpu.PrefetchScalarGridSpec(num_scalar_...  17.4 us
    all_to_all x2, starting transfers between devices, gather_axis(): return lax.all_to_all(spread, axis, 0, 0, tiled=True)  12.5 us
    broadcast_in_dim x4, local copies, waits for them, and re-layouts, gather_axis(): spread = jnp.broadcast_to(block[None], (count,) + block.shape)  2.77 us
  transfers between devices with their start and end apart: 2, of which 2 were waited for; matrix products, arithmetic and copies ran while one was open for 0% of the time, Pallas kernels for 0%

profile of v11, /device:TPU:1, one launch (start us, length us, event | category | flops | bytes accessed | tf_op | source)
XLA Modules:
  0.0 134.9 jit_solution(9456139503125057512)
XLA Ops:
  0.6 2.0 %broadcast_in_dim.8 = bf16[16,256,128]{2,1,0:T(8,128)(2,1)} broadcast(bf16[256,128]{1,0:T(8,128)(2,1)} %param.7), dimensions={1,2} | broadcast | bytes 1114112 | tf_op jit(solution)/shard_map/broadcast_in_dim | solution.py:161
  2.7 7.3 %all-to-all-start = ((bf16[16,256,128]{2,1,0:T(8,128)(2,1)}), bf16[16,256,128]{2,1,0:T(8,128)(2,1)S(1)}, u32[]{:S(2)}, u32[]{:S(2)}) async-start(bf16[16,256,128]{2,1,0:T(8,128)(2,1)} %broadcast_in_dim.8), calls=%async_computation | async-start | bytes 2097152 | tf_op jit(solution)/shard_map/all_to_all | solution.py:162
  10.6 15.1 %all-to-all-done.refs_0_.refs_1_ = bf16[16,256,128]{2,1,0:T(8,128)(2,1)S(1)} async-done(((bf16[16,256,128]{2,1,0:T(8,128)(2,1)}), bf16[16,256,128]{2,1,0:T(8,128)(2,1)S(1)}, u32[]{:S(2)}, u32[]{:S(2)}) %all-to-all-start) | async-done | bytes 1048608 | tf_op jit(solution)/shard_map/all_to_all | solution.py:162
  25.7 0.0 copy-start
  25.8 1.0 copy-done
  26.8 7.8 %shard_map.94 = bf16[8,256,256]{2,1,0:T(8,128)(2,1)} custom-call(s32[96]{0:T(128)} %rows_ref.3, s32[96]{0:T(128)} %cols_ref.3, s32[1]{0:T(128)S(6)} %copy.10.live_ref, bf16[96,256,256]{2,1,0:T(8,128)(2,1)} %a_ref.3, bf16[16,256,128]{2,1,0:T(8,128)(2,1)} %copy-done, bf16[128,256]{1,0:T(8,128)(2,1)} %refs_2_.1), custom_call_target="tpu_custom_call" | custom-call | flops 3221225472 | bytes 16777216 | tf_op jit(solution)/shard_map/pallas_call | solution.py:141
  34.6 0.0 copy-start.1
  34.6 24.4 %all_to_all.30 = bf16[8,256,256]{2,1,0:T(8,128)(2,1)S(1)} all-to-all(bf16[8,256,256]{2,1,0:T(8,128)(2,1)} %shard_map.94), channel_id=1, replica_groups=mesh['row'=16,'col'=8] {'col'}, dimensions={0} | all-to-all | bytes 2097152 | tf_op jit(solution)/shard_map/all_to_all | solution.py:188
  59.0 0.1 convert_reduce_fusion.1
  59.1 0.0 copy-done.1
  59.1 0.8 multiply_convert_fusion
  59.9 0.1 broadcast_in_dim.9
  60.0 17.1 %all_to_all.31.refs_0_ = bf16[8,256,256]{2,1,0:T(8,128)(2,1)} all-to-all(bf16[8,256,256]{2,1,0:T(8,128)(2,1)S(1)} %broadcast_in_dim.9), channel_id=1, replica_groups=mesh['row'=16,'col'=8] {'col'}, dimensions={0} | all-to-all | bytes 2097152 | tf_op jit(solution)/shard_map/all_to_all | solution.py:162
  77.1 9.5 %shard_map.95 = bf16[16,272,128]{2,1,0:T(8,128)(2,1)} custom-call(s32[96]{0:T(128)} %rows_ref.3, s32[96]{0:T(128)} %cols_ref.3, s32[1]{0:T(128)S(6)} %copy.10.live_ref, bf16[96,256,256]{2,1,0:T(8,128)(2,1)} %a_ref.3, bf16[8,256,256]{2,1,0:T(8,128)(2,1)} %all_to_all.31.refs_0_, bf16[16,256,128]{2,1,0:T(8,128)(2,1)} %copy-done, bf16[128,256]{1,0:T(8,128)(2,1)} %refs_2_.1), custom_call_target="tpu_custom_call" | custom-call | flops 3221225472 | bytes 17825792 | tf_op jit(solution)/shard_map/pallas_call | solution.py:141
  86.6 26.3 %all_to_all.32 = bf16[16,272,128]{2,1,0:T(8,128)(2,1)S(1)} all-to-all(bf16[16,272,128]{2,1,0:T(8,128)(2,1)} %shard_map.95), channel_id=1, replica_groups=mesh['row'=16,'col'=8] {'row'}, dimensions={0} | all-to-all | bytes 2228224 | tf_op jit(solution)/shard_map/all_to_all | solution.py:198
  112.9 0.2 convert_reduce_fusion
  113.1 9.3 %all_to_all.33 = f32[8,16,128]{2,1,0:T(8,128)S(1)} all-to-all(f32[8,16,128]{2,1,0:T(8,128)S(1)} %broadcast_in_dim.10), channel_id=1, replica_groups=mesh['row'=16,'col'=8] {'col'}, dimensions={0} | all-to-all | bytes 131072 | tf_op jit(solution)/shard_map/all_to_all | solution.py:162
  122.4 0.7 broadcast_in_dim.11
  123.0 5.1 %all-to-all-start.5 = ((f32[16,16,128]{2,1,0:T(8,128)}), f32[16,16,128]{2,1,0:T(8,128)S(1)}, u32[]{:S(2)}, u32[]{:S(2)}) async-start(f32[16,16,128]{2,1,0:T(8,128)} %broadcast_in_dim.11), calls=%async_computation.5 | async-start | bytes 262144 | tf_op jit(solution)/shard_map/all_to_all | solution.py:162
  128.1 0.6 slice.12
  128.8 5.5 %all-to-all-done.5 = f32[16,16,128]{2,1,0:T(8,128)S(1)} async-done(((f32[16,16,128]{2,1,0:T(8,128)}), f32[16,16,128]{2,1,0:T(8,128)S(1)}, u32[]{:S(2)}, u32[]{:S(2)}) %all-to-all-start.5) | async-done | bytes 131104 | tf_op jit(solution)/shard_map/all_to_all | solution.py:162
  134.3 0.7 multiply_bitcast_fusion
  (3 shorter events, 0.0 us)
Async XLA Ops:
  2.7 23.1 %all-to-all-start = ((bf16[16,256,128]{2,1,0:T(8,128)(2,1)}), bf16[16,256,128]{2,1,0:T(8,128)(2,1)S(1)}, u32[]{:S(2)}, u32[]{:S(2)}) async-start(bf16[16,256,128]{2,1,0:T(8,128)(2,1)} %broadcast_in_dim.8), calls=%async_computation | async-start | bytes 2097152 | tf_op jit(solution)/shard_map/all_to_all | solution.py:162
  25.7 1.0 copy-start
  34.6 24.5 %copy-start.1 = (bf16[256,256]{1,0:T(8,128)(2,1)S(1)}, bf16[256,256]{1,0:T(8,128)(2,1)}, u32[]{:S(2)}) copy-start(bf16[256,256]{1,0:T(8,128)(2,1)} %param.13) | copy-start | bytes 393220
  123.0 11.3 %all-to-all-start.5 = ((f32[16,16,128]{2,1,0:T(8,128)}), f32[16,16,128]{2,1,0:T(8,128)S(1)}, u32[]{:S(2)}, u32[]{:S(2)}) async-start(f32[16,16,128]{2,1,0:T(8,128)} %broadcast_in_dim.11), calls=%async_computation.5 | async-start | bytes 262144 | tf_op jit(solution)/shard_map/all_to_all | solution.py:162

commit v12 on v11

--- a/solution.py
+++ b/solution.py
@@ -8,7 +8,7 @@
 from jax.experimental.pallas import tpu as pltpu
 from jax.sharding import PartitionSpec as P
 
-GROUP = 32
+GROUP = 16
 
 
 def silu_slope(value):

time: 136 us -> 136 us (level)
  no operation moved by 1% of the time
where the time goes in v12:
time: 136 us
  blocking collectives  78 us (57%)
  waiting for transfers between devices  20.6 us (15%)
  Pallas kernels  17 us (12%)
  starting transfers between devices  12.5 us (9%)
  local copies, waits for them, and re-layouts  4.43 us (3%)
  other arithmetic  1.74 us (1%)
    all_to_all x2, blocking collectives, gather_axis(): return lax.all_to_all(spread, axis, 0, 0, tiled=True)  27.1 us
    all_to_all x1, blocking collectives, body(): exchanged = lax.all_to_all(payload, 'row', 0, 0, tiled=True)  26.3 us
    all_to_all x1, blocking collectives, body(): received = lax.all_to_all(partial_value, 'col', 0, 0, tiled=True)  24.6 us
    all_to_all x2, waiting for transfers between devices, gather_axis(): return lax.all_to_all(spread, axis, 0, 0, tiled=True)  20.6 us
    pallas_call x2, Pallas kernels, block_product(): pl.pallas_call(kernel, grid_spec=pltpu.PrefetchScalarGridSpec(num_scalar_...  17 us
    all_to_all x2, starting transfers between devices, gather_axis(): return lax.all_to_all(spread, axis, 0, 0, tiled=True)  12.5 us
    broadcast_in_dim x4, local copies, waits for them, and re-layouts, gather_axis(): spread = jnp.broadcast_to(block[None], (count,) + block.shape)  2.77 us
  transfers between devices with their start and end apart: 2, of which 2 were waited for; matrix products, arithmetic and copies ran while one was open for 0% of the time, Pallas kernels for 0%

profile of v12, /device:TPU:1, one launch (start us, length us, event | category | flops | bytes accessed | tf_op | source)
XLA Modules:
  0.0 135.6 jit_solution(4681793496736065226)
XLA Ops:
  0.6 2.0 %broadcast_in_dim.8 = bf16[16,256,128]{2,1,0:T(8,128)(2,1)} broadcast(bf16[256,128]{1,0:T(8,128)(2,1)} %param.7), dimensions={1,2} | broadcast | bytes 1114112 | tf_op jit(solution)/shard_map/broadcast_in_dim | solution.py:161
  2.7 7.3 %all-to-all-start = ((bf16[16,256,128]{2,1,0:T(8,128)(2,1)}), bf16[16,256,128]{2,1,0:T(8,128)(2,1)S(1)}, u32[]{:S(2)}, u32[]{:S(2)}) async-start(bf16[16,256,128]{2,1,0:T(8,128)(2,1)} %broadcast_in_dim.8), calls=%async_computation | async-start | bytes 2097152 | tf_op jit(solution)/shard_map/all_to_all | solution.py:162
  10.6 15.1 %all-to-all-done.refs_0_.refs_1_ = bf16[16,256,128]{2,1,0:T(8,128)(2,1)S(1)} async-done(((bf16[16,256,128]{2,1,0:T(8,128)(2,1)}), bf16[16,256,128]{2,1,0:T(8,128)(2,1)S(1)}, u32[]{:S(2)}, u32[]{:S(2)}) %all-to-all-start) | async-done | bytes 1048608 | tf_op jit(solution)/shard_map/all_to_all | solution.py:162
  25.7 0.0 copy-start
  25.8 1.0 copy-done
  26.8 7.7 %shard_map.94 = bf16[8,256,256]{2,1,0:T(8,128)(2,1)} custom-call(s32[96]{0:T(128)} %rows_ref.3, s32[96]{0:T(128)} %cols_ref.3, s32[1]{0:T(128)S(6)} %copy.10.live_ref, bf16[96,256,256]{2,1,0:T(8,128)(2,1)} %a_ref.3, bf16[16,256,128]{2,1,0:T(8,128)(2,1)} %copy-done, bf16[128,256]{1,0:T(8,128)(2,1)} %refs_2_.1), custom_call_target="tpu_custom_call" | custom-call | flops 3221225472 | bytes 16777216 | tf_op jit(solution)/shard_map/pallas_call | solution.py:141
  34.5 0.0 copy-start.1
  34.5 24.6 %all_to_all.30 = bf16[8,256,256]{2,1,0:T(8,128)(2,1)S(1)} all-to-all(bf16[8,256,256]{2,1,0:T(8,128)(2,1)} %shard_map.94), channel_id=1, replica_groups=mesh['row'=16,'col'=8] {'col'}, dimensions={0} | all-to-all | bytes 2097152 | tf_op jit(solution)/shard_map/all_to_all | solution.py:188
  59.0 0.1 convert_reduce_fusion.1
  59.2 0.0 copy-done.1
  59.2 0.8 multiply_convert_fusion
  60.0 0.1 broadcast_in_dim.9
  60.0 17.1 %all_to_all.31.refs_0_ = bf16[8,256,256]{2,1,0:T(8,128)(2,1)} all-to-all(bf16[8,256,256]{2,1,0:T(8,128)(2,1)S(1)} %broadcast_in_dim.9), channel_id=1, replica_groups=mesh['row'=16,'col'=8] {'col'}, dimensions={0} | all-to-all | bytes 2097152 | tf_op jit(solution)/shard_map/all_to_all | solution.py:162
  77.1 9.3 %shard_map.95 = bf16[16,272,128]{2,1,0:T(8,128)(2,1)} custom-call(s32[96]{0:T(128)} %rows_ref.3, s32[96]{0:T(128)} %cols_ref.3, s32[1]{0:T(128)S(6)} %copy.10.live_ref, bf16[96,256,256]{2,1,0:T(8,128)(2,1)} %a_ref.3, bf16[8,256,256]{2,1,0:T(8,128)(2,1)} %all_to_all.31.refs_0_, bf16[16,256,128]{2,1,0:T(8,128)(2,1)} %copy-done, bf16[128,256]{1,0:T(8,128)(2,1)} %refs_2_.1), custom_call_target="tpu_custom_call" | custom-call | flops 3221225472 | bytes 17825792 | tf_op jit(solution)/shard_map/pallas_call | solution.py:141
  86.5 26.3 %all_to_all.32 = bf16[16,272,128]{2,1,0:T(8,128)(2,1)S(1)} all-to-all(bf16[16,272,128]{2,1,0:T(8,128)(2,1)} %shard_map.95), channel_id=1, replica_groups=mesh['row'=16,'col'=8] {'row'}, dimensions={0} | all-to-all | bytes 2228224 | tf_op jit(solution)/shard_map/all_to_all | solution.py:198
  112.7 0.2 convert_reduce_fusion
  112.9 10.1 %all_to_all.33 = f32[8,16,128]{2,1,0:T(8,128)S(1)} all-to-all(f32[8,16,128]{2,1,0:T(8,128)S(1)} %broadcast_in_dim.10), channel_id=1, replica_groups=mesh['row'=16,'col'=8] {'col'}, dimensions={0} | all-to-all | bytes 131072 | tf_op jit(solution)/shard_map/all_to_all | solution.py:162
  123.0 0.7 broadcast_in_dim.11
  123.6 5.1 %all-to-all-start.5 = ((f32[16,16,128]{2,1,0:T(8,128)}), f32[16,16,128]{2,1,0:T(8,128)S(1)}, u32[]{:S(2)}, u32[]{:S(2)}) async-start(f32[16,16,128]{2,1,0:T(8,128)} %broadcast_in_dim.11), calls=%async_computation.5 | async-start | bytes 262144 | tf_op jit(solution)/shard_map/all_to_all | solution.py:162
  128.8 0.6 slice.12
  129.4 5.5 %all-to-all-done.5 = f32[16,16,128]{2,1,0:T(8,128)S(1)} async-done(((f32[16,16,128]{2,1,0:T(8,128)}), f32[16,16,128]{2,1,0:T(8,128)S(1)}, u32[]{:S(2)}, u32[]{:S(2)}) %all-to-all-start.5) | async-done | bytes 131104 | tf_op jit(solution)/shard_map/all_to_all | solution.py:162
  134.9 0.7 multiply_bitcast_fusion
  (3 shorter events, 0.0 us)
Async XLA Ops:
  2.7 23.1 %all-to-all-start = ((bf16[16,256,128]{2,1,0:T(8,128)(2,1)}), bf16[16,256,128]{2,1,0:T(8,128)(2,1)S(1)}, u32[]{:S(2)}, u32[]{:S(2)}) async-start(bf16[16,256,128]{2,1,0:T(8,128)(2,1)} %broadcast_in_dim.8), calls=%async_computation | async-start | bytes 2097152 | tf_op jit(solution)/shard_map/all_to_all | solution.py:162
  25.7 1.0 copy-start
  34.5 24.7 %copy-start.1 = (bf16[256,256]{1,0:T(8,128)(2,1)S(1)}, bf16[256,256]{1,0:T(8,128)(2,1)}, u32[]{:S(2)}) copy-start(bf16[256,256]{1,0:T(8,128)(2,1)} %param.13) | copy-start | bytes 393220
  123.6 11.3 %all-to-all-start.5 = ((f32[16,16,128]{2,1,0:T(8,128)}), f32[16,16,128]{2,1,0:T(8,128)S(1)}, u32[]{:S(2)}, u32[]{:S(2)}) async-start(f32[16,16,128]{2,1,0:T(8,128)} %broadcast_in_dim.11), calls=%async_computation.5 | async-start | bytes 262144 | tf_op jit(solution)/shard_map/all_to_all | solution.py:162

commit v13 on v11

--- a/solution.py
+++ b/solution.py
@@ -196,9 +196,9 @@
         weight=weight, feats=feature_cols.reshape(tile_cols, size, fin),
     )
     exchanged = lax.all_to_all(payload, "row", 0, 0, tiled=True)
-    gathered = exchanged.astype(jnp.float32).sum(axis=0)
-    grad_features = gathered[:size].astype(jnp.bfloat16)
-    weight_piece = gather_axis(gathered[size:], "col", n_col).sum(axis=0)
+    weight_in = exchanged[:, size:].astype(jnp.float32).sum(axis=0)
+    grad_features = exchanged[:, :size].astype(jnp.float32).sum(axis=0).astype(jnp.bfloat16)
+    weight_piece = gather_axis(weight_in, "col", n_col).sum(axis=0)
     pieces = gather_axis(weight_piece, "row", n_row)
     rows_per = fin // tile_cols
     grad_weight = pieces.reshape(tile_cols, 2, rows_per, fin).transpose(0, 2, 1, 3).reshape(fin, width)

time: 136 us -> 137 us (level)
    all_to_all x2, blocking collectives: 26.3 us -> 28.5 us  [gather_axis(): return lax.all_to_all(spread, axis, 0, 0, tiled=True)]
    all_to_all x1, blocking collectives: 26.3 us -> 24.9 us  [body(): exchanged = lax.all_to_all(payload, 'row', 0, 0, tiled=True)]
  transfers between devices with their start and end apart: 2 -> 2, of which waited for: 2 -> 2; matrix products, arithmetic and copies ran while one was open for 0% -> 1% of each run, Pallas kernels for 0% -> 0%
where the time goes in v13:
time: 137 us; the launch traced here: 136 us
  blocking collectives  77.6 us (57%)
  waiting for transfers between devices  20.5 us (15%)
  Pallas kernels  17.4 us (13%)
  starting transfers between devices  12.5 us (9%)
  local copies, waits for them, and re-layouts  4.55 us (3%)
  other arithmetic  2.38 us (2%)
    all_to_all x2, blocking collectives, gather_axis(): return lax.all_to_all(spread, axis, 0, 0, tiled=True)  28.5 us
    all_to_all x1, blocking collectives, body(): exchanged = lax.all_to_all(payload, 'row', 0, 0, tiled=True)  24.9 us
    all_to_all x1, blocking collectives, body(): received = lax.all_to_all(partial_value, 'col', 0, 0, tiled=True)  24.2 us
    all_to_all x2, waiting for transfers between devices, gather_axis(): return lax.all_to_all(spread, axis, 0, 0, tiled=True)  20.5 us
    pallas_call x2, Pallas kernels, block_product(): pl.pallas_call(kernel, grid_spec=pltpu.PrefetchScalarGridSpec(num_scalar_...  17.4 us
    all_to_all x2, starting transfers between devices, gather_axis(): return lax.all_to_all(spread, axis, 0, 0, tiled=True)  12.5 us
    broadcast_in_dim x4, local copies, waits for them, and re-layouts, gather_axis(): spread = jnp.broadcast_to(block[None], (count,) + block.shape)  2.77 us
  transfers between devices with their start and end apart: 2, of which 2 were waited for; matrix products, arithmetic and copies ran while one was open for 1% of the time, Pallas kernels for 0%

profile of v13, /device:TPU:1, one launch (start us, length us, event | category | flops | bytes accessed | tf_op | source)
XLA Modules:
  0.0 136.1 jit_solution(12054057555619635791)
XLA Ops:
  0.6 2.0 %broadcast_in_dim.8 = bf16[16,256,128]{2,1,0:T(8,128)(2,1)} broadcast(bf16[256,128]{1,0:T(8,128)(2,1)} %param.7), dimensions={1,2} | broadcast | bytes 1114112 | tf_op jit(solution)/shard_map/broadcast_in_dim | solution.py:161
  2.7 7.3 %all-to-all-start = ((bf16[16,256,128]{2,1,0:T(8,128)(2,1)}), bf16[16,256,128]{2,1,0:T(8,128)(2,1)S(1)}, u32[]{:S(2)}, u32[]{:S(2)}) async-start(bf16[16,256,128]{2,1,0:T(8,128)(2,1)} %broadcast_in_dim.8), calls=%async_computation | async-start | bytes 2097152 | tf_op jit(solution)/shard_map/all_to_all | solution.py:162
  10.6 15.1 %all-to-all-done.refs_0_.refs_1_ = bf16[16,256,128]{2,1,0:T(8,128)(2,1)S(1)} async-done(((bf16[16,256,128]{2,1,0:T(8,128)(2,1)}), bf16[16,256,128]{2,1,0:T(8,128)(2,1)S(1)}, u32[]{:S(2)}, u32[]{:S(2)}) %all-to-all-start) | async-done | bytes 1048608 | tf_op jit(solution)/shard_map/all_to_all | solution.py:162
  25.7 0.0 copy-start
  25.8 1.0 copy-done
  26.8 7.8 %shard_map.94 = bf16[8,256,256]{2,1,0:T(8,128)(2,1)} custom-call(s32[96]{0:T(128)} %rows_ref.3, s32[96]{0:T(128)} %cols_ref.3, s32[1]{0:T(128)S(6)} %copy.10.live_ref, bf16[96,256,256]{2,1,0:T(8,128)(2,1)} %a_ref.3, bf16[16,256,128]{2,1,0:T(8,128)(2,1)} %copy-done, bf16[128,256]{1,0:T(8,128)(2,1)} %refs_2_.1), custom_call_target="tpu_custom_call" | custom-call | flops 3221225472 | bytes 16777216 | tf_op jit(solution)/shard_map/pallas_call | solution.py:141
  34.6 24.2 %all_to_all.30 = bf16[8,256,256]{2,1,0:T(8,128)(2,1)S(1)} all-to-all(bf16[8,256,256]{2,1,0:T(8,128)(2,1)} %shard_map.94), channel_id=1, replica_groups=mesh['row'=16,'col'=8] {'col'}, dimensions={0} | all-to-all | bytes 2097152 | tf_op jit(solution)/shard_map/all_to_all | solution.py:188
  58.8 0.0 copy-start.1
  58.8 0.1 convert_reduce_fusion
  59.0 0.8 copy-done.1
  59.7 0.8 multiply_convert_fusion
  60.5 0.1 broadcast_in_dim.9
  60.6 18.5 %all_to_all.31.refs_0_ = bf16[8,256,256]{2,1,0:T(8,128)(2,1)} all-to-all(bf16[8,256,256]{2,1,0:T(8,128)(2,1)S(1)} %broadcast_in_dim.9), channel_id=1, replica_groups=mesh['row'=16,'col'=8] {'col'}, dimensions={0} | all-to-all | bytes 2097152 | tf_op jit(solution)/shard_map/all_to_all | solution.py:162
  79.0 9.5 %shard_map.95 = bf16[16,272,128]{2,1,0:T(8,128)(2,1)} custom-call(s32[96]{0:T(128)} %rows_ref.3, s32[96]{0:T(128)} %cols_ref.3, s32[1]{0:T(128)S(6)} %copy.10.live_ref, bf16[96,256,256]{2,1,0:T(8,128)(2,1)} %a_ref.3, bf16[8,256,256]{2,1,0:T(8,128)(2,1)} %all_to_all.31.refs_0_, bf16[16,256,128]{2,1,0:T(8,128)(2,1)} %copy-done, bf16[128,256]{1,0:T(8,128)(2,1)} %refs_2_.1), custom_call_target="tpu_custom_call" | custom-call | flops 3221225472 | bytes 17825792 | tf_op jit(solution)/shard_map/pallas_call | solution.py:141
  88.6 24.9 %all_to_all.32 = bf16[16,272,128]{2,1,0:T(8,128)(2,1)S(1)} all-to-all(bf16[16,272,128]{2,1,0:T(8,128)(2,1)} %shard_map.95), channel_id=1, replica_groups=mesh['row'=16,'col'=8] {'row'}, dimensions={0} | all-to-all | bytes 2228224 | tf_op jit(solution)/shard_map/all_to_all | solution.py:198
  113.5 10.0 %all_to_all.33 = f32[8,16,128]{2,1,0:T(8,128)S(1)} all-to-all(f32[8,16,128]{2,1,0:T(8,128)S(1)} %broadcast_in_dim.10), channel_id=1, replica_groups=mesh['row'=16,'col'=8] {'col'}, dimensions={0} | all-to-all | bytes 131072 | tf_op jit(solution)/shard_map/all_to_all | solution.py:162
  123.5 0.7 broadcast_in_dim.11
  124.2 5.1 %all-to-all-start.5 = ((f32[16,16,128]{2,1,0:T(8,128)}), f32[16,16,128]{2,1,0:T(8,128)S(1)}, u32[]{:S(2)}, u32[]{:S(2)}) async-start(f32[16,16,128]{2,1,0:T(8,128)} %broadcast_in_dim.11), calls=%async_computation.5 | async-start | bytes 262144 | tf_op jit(solution)/shard_map/all_to_all | solution.py:162
  129.3 0.8 slice_reduce_fusion
  130.1 5.4 %all-to-all-done.5 = f32[16,16,128]{2,1,0:T(8,128)S(1)} async-done(((f32[16,16,128]{2,1,0:T(8,128)}), f32[16,16,128]{2,1,0:T(8,128)S(1)}, u32[]{:S(2)}, u32[]{:S(2)}) %all-to-all-start.5) | async-done | bytes 131104 | tf_op jit(solution)/shard_map/all_to_all | solution.py:162
  135.4 0.7 multiply_bitcast_fusion
  (3 shorter events, 0.0 us)
Async XLA Ops:
  2.7 23.1 %all-to-all-start = ((bf16[16,256,128]{2,1,0:T(8,128)(2,1)}), bf16[16,256,128]{2,1,0:T(8,128)(2,1)S(1)}, u32[]{:S(2)}, u32[]{:S(2)}) async-start(bf16[16,256,128]{2,1,0:T(8,128)(2,1)} %broadcast_in_dim.8), calls=%async_computation | async-start | bytes 2097152 | tf_op jit(solution)/shard_map/all_to_all | solution.py:162
  25.7 1.0 copy-start
  58.8 0.9 copy-start.1
  124.2 11.3 %all-to-all-start.5 = ((f32[16,16,128]{2,1,0:T(8,128)}), f32[16,16,128]{2,1,0:T(8,128)S(1)}, u32[]{:S(2)}, u32[]{:S(2)}) async-start(f32[16,16,128]{2,1,0:T(8,128)} %broadcast_in_dim.11), calls=%async_computation.5 | async-start | bytes 262144 | tf_op jit(solution)/shard_map/all_to_all | solution.py:162
